TPU v7x, 128 devices: a whole 4x4x4 slice. The times are simulated.
128 devices in a mesh: lat: 8 (over z_hi, y), lon: 16 (over z_lo, x, core).
Axes of the slice: x: 4, y: 4, z: 4 (z_hi: 2, z_lo: 2; z = z_hi * 2 + z_lo), core: 2. Of those that a mesh axis runs over, the one named last changes fastest.
Arguments:
- stored_tiles: float32 [3456, 8, 8100], P(('lat', 'lon')), may hold values from -6 to 6
- stored_ids: int32 [3456], P(('lat', 'lon')), may hold values from -1 to 143, as said below
- wet_tiles: int32 [24, 48], P('lat', 'lon'), may hold values from 0 to 1, as said below
- control_map: int32 [24, 48], P('lat', 'lon'), may hold values from 0 to 127, as said below
- zonal_diffusivity: float32 [2160, 4320], P('lat', 'lon'), may hold values from 0.05 to 0.18
- meridional_diffusivity: float32 [2160, 4320], P('lat', 'lon'), may hold values from 0.05 to 0.18
- zonal_flow: float32 [2160, 4320], P('lat', 'lon'), may hold values from -0.1 to 0.1
- meridional_flow: float32 [2160, 4320], P('lat', 'lon'), may hold values from -0.1 to 0.1
- vertical_mixing: float32 [2160, 4320], P('lat', 'lon'), may hold values from 0.02 to 0.1
- forcing: float32 [2, 2160, 4320], P(None, 'lat', 'lon'), may hold values from -4 to 4
- final_adjoint: float32 [2, 4, 2160, 4320], P(None, None, 'lat', 'lon'), may hold values from -6 to 6
Outputs:
- final_state: float32 [2, 4, 2160, 4320], P(None, None, 'lat', 'lon')
- initial_adjoint: float32 [2, 4, 2160, 4320], P(None, None, 'lat', 'lon')
- control_adjoint: float32 [128, 2, 900], P(('lat', 'lon'))
Inputs may be any that keep to these rules, and one draw needn't show every extreme that they name: `stored_ids`: entry -1 marks an empty slot; any other entry r * 48 + c names the wet tile in row r of the storing device's band of 3 tile rows and tile column c. Each wet tile of a band stands in exactly one slot of one device of that band. One device's slots name at most 2 tiles whose columns lie in one compute owner's 3 columns, and some device has exactly 2; in every band one device uses all 27 slots. `wet_tiles`: the wet tiles are exactly those named in stored_ids. `control_map`: the 3 x 3 tiles of one device name different control tiles.
All inputs are finite; a program needn't handle non-finite values.
Results may differ from a plain program's by a relative error of at most 0.000096.
Values sent between devices are 32-bit elements; how exact they have to be, the bound alone decides.
No kernel may reach another device: no remote copies, remote signals or barrier semaphores. Data moves between devices by JAX's collectives and lax.ppermute only.
A program may use at most 192 MiB of HBM per device.

v0:
```python
import jax
import jax.numpy as jnp
from jax import lax
from jax.sharding import PartitionSpec as P

STEPS = 3
COARSE = 3
PAIR_MOST = 2


def extended(block, sides, width, periodic):
    for axis, dim in sides:
        count = lax.axis_size(axis)
        forward = [(i, i + 1) for i in range(count - 1)]
        if periodic:
            forward.append((count - 1, 0))
        backward = [(target, source) for source, target in forward]
        low = lax.ppermute(
            lax.slice_in_dim(block, block.shape[dim] - width, None, axis=dim), axis, forward
        )
        high = lax.ppermute(lax.slice_in_dim(block, 0, width, axis=dim), axis, backward)
        block = jnp.concatenate([low, block, high], axis=dim)
    return block


def shift_rims(field):
    widened = extended(field, (("lon", 3),), 1, True)
    return extended(widened, (("lat", 2),), 1, False)


def face_terms(padded):
    wet_rim = padded[0]
    east_open = wet_rim[1:-1, :-1] * wet_rim[1:-1, 1:]
    north_open = wet_rim[:-1, 1:-1] * wet_rim[1:, 1:-1]
    east_diff = padded[1][1:-1, :-1] * east_open
    east_adv = 0.5 * padded[2][1:-1, :-1] * east_open
    north_diff = padded[3][:-1, 1:-1] * north_open
    north_adv = 0.5 * padded[4][:-1, 1:-1] * north_open
    return (east_diff, east_adv, north_diff, north_adv)


def vertical(center, mixing):
    flux = mixing * (center[:, :-1] - center[:, 1:])
    edge = jnp.zeros_like(center[:, :1])
    return jnp.concatenate([edge, flux], axis=1) - jnp.concatenate([flux, edge], axis=1)


def forward_change(padded, faces, mixing):
    east_diff, east_adv, north_diff, north_adv = faces
    mid_rows = padded[:, :, 1:-1, :]
    mid_cols = padded[:, :, :, 1:-1]
    east_flux = east_diff * (mid_rows[..., :-1] - mid_rows[..., 1:]) + east_adv * (
        mid_rows[..., :-1] + mid_rows[..., 1:]
    )
    north_flux = north_diff * (mid_cols[..., :-1, :] - mid_cols[..., 1:, :]) + north_adv * (
        mid_cols[..., :-1, :] + mid_cols[..., 1:, :]
    )
    center = padded[:, :, 1:-1, 1:-1]
    return (
        east_flux[..., :-1]
        - east_flux[..., 1:]
        + (north_flux[..., :-1, :] - north_flux[..., 1:, :])
        + vertical(center, mixing)
    )


def backward_change(padded, faces, mixing):
    east_diff, east_adv, north_diff, north_adv = faces
    mid_rows = padded[:, :, 1:-1, :]
    mid_cols = padded[:, :, :, 1:-1]
    east_step = mid_rows[..., 1:] - mid_rows[..., :-1]
    north_step = mid_cols[..., 1:, :] - mid_cols[..., :-1, :]
    zonal_part = ((east_diff + east_adv) * east_step)[..., 1:] + (
        (east_adv - east_diff) * east_step
    )[..., :-1]
    merid_part = ((north_diff + north_adv) * north_step)[..., 1:, :] + (
        (north_adv - north_diff) * north_step
    )[..., :-1, :]
    center = padded[:, :, 1:-1, 1:-1]
    return zonal_part + merid_part + vertical(center, mixing)


def coarsen(fine_cells, tile_side):
    tile_count = fine_cells.shape[0]
    coarse_side = tile_side // COARSE
    shaped = fine_cells.reshape(tile_count, 2, coarse_side, COARSE, coarse_side, COARSE)
    return shaped.mean(axis=(3, 5)).reshape(tile_count, 2, coarse_side * coarse_side)


def per_device(
    stored_tiles,
    stored_ids,
    wet_tiles,
    control_map,
    zonal_diffusivity,
    meridional_diffusivity,
    zonal_flow,
    meridional_flow,
    vertical_mixing,
    forcing,
    final_adjoint,
):
    tile_rows, tile_cols = wet_tiles.shape
    tile_side = zonal_diffusivity.shape[0] // tile_rows
    lon_count = lax.axis_size("lon")
    columns = tile_cols * lon_count
    slot_count = stored_ids.shape[0]
    levels = final_adjoint.shape[1]
    tile_total = tile_rows * tile_cols
    slot_valid = stored_ids >= 0
    tile_col = stored_ids % columns
    owner_lon = jnp.where(slot_valid, tile_col // tile_cols, lon_count)
    tile_place = stored_ids // columns * tile_cols + tile_col % tile_cols
    slot_order = jnp.arange(slot_count, dtype=jnp.int32)
    earlier = slot_order[None, :] < slot_order[:, None]
    same_owner = owner_lon[:, None] == owner_lon[None, :]
    slot_rank = jnp.sum((earlier & same_owner).astype(jnp.int32), axis=1)
    route_match = (
        owner_lon[None, None, :] == jnp.arange(lon_count, dtype=jnp.int32)[:, None, None]
    ) & (slot_rank[None, None, :] == jnp.arange(PAIR_MOST, dtype=jnp.int32)[None, :, None])
    route_used = jnp.any(route_match, axis=2)
    route_slot = jnp.sum(jnp.where(route_match, slot_order[None, None, :], 0), axis=2)
    outgoing = (
        jnp.take(stored_tiles, route_slot, axis=0)
        * route_used.astype(jnp.float32)[:, :, None, None]
    )
    out_place = jnp.where(
        route_used, jnp.sum(jnp.where(route_match, tile_place[None, None, :], 0), axis=2), -1
    )
    incoming, in_place = (
        lax.all_to_all(outgoing, "lon", split_axis=0, concat_axis=0, tiled=True),
        lax.all_to_all(out_place, "lon", split_axis=0, concat_axis=0, tiled=True),
    )
    received = incoming.reshape(lon_count * PAIR_MOST, 2 * levels, tile_side * tile_side)
    arrive_place = in_place.reshape(-1)
    target = jnp.where(arrive_place >= 0, arrive_place, tile_total).astype(jnp.int32)
    tile_data = (
        jnp.zeros((tile_total, 2 * levels, tile_side * tile_side), jnp.float32)
        .at[target]
        .set(received, mode="drop")
    )
    wet_cells = jnp.repeat(
        jnp.repeat(wet_tiles.astype(jnp.float32), tile_side, axis=0), tile_side, axis=1
    )
    ocean_state = (
        tile_data.reshape(tile_rows, tile_cols, 2, levels, tile_side, tile_side)
        .transpose(2, 3, 0, 4, 1, 5)
        .reshape(2, levels, tile_rows * tile_side, tile_cols * tile_side)
        * wet_cells
    )
    stacked = jnp.stack(
        [wet_cells, zonal_diffusivity, zonal_flow, meridional_diffusivity, meridional_flow]
    )[None]
    faces = face_terms(shift_rims(stacked)[0])
    mixing = vertical_mixing * wet_cells
    forcing_wet = forcing * wet_cells
    adjoint_field = final_adjoint
    surface = jnp.zeros((2,) + wet_cells.shape, jnp.float32)
    for _ in range(STEPS):
        ocean_state = ocean_state + forward_change(shift_rims(ocean_state), faces, mixing)
        ocean_state = ocean_state.at[:, 0].add(forcing_wet)
    for _ in range(STEPS):
        surface = surface + wet_cells * adjoint_field[:, 0]
        adjoint_field = adjoint_field + backward_change(shift_rims(adjoint_field), faces, mixing)
    per_tile = (
        surface.reshape(2, tile_rows, tile_side, tile_cols, tile_side)
        .transpose(1, 3, 0, 2, 4)
        .reshape(tile_total, 2, tile_side * tile_side)
    )
    labels = control_map.reshape(-1)
    blocks = coarsen(per_tile, tile_side)
    hit_table = (
        labels[:, None] == jnp.arange(1 * lax.axis_size(("lat", "lon")), dtype=jnp.int32)[None, :]
    ).astype(jnp.float32)
    control = lax.psum_scatter(
        jnp.einsum("tc,tfk->cfk", hit_table, blocks, precision=lax.Precision.HIGHEST),
        ("lat", "lon"),
        scatter_dimension=0,
        tiled=True,
    )
    return (ocean_state, wet_cells * adjoint_field, control)


def solution(mesh):
    return jax.shard_map(
        per_device,
        mesh=mesh,
        in_specs=(
            P(("lat", "lon"), None, None),
            P(("lat", "lon")),
            P("lat", "lon"),
            P("lat", "lon"),
            P("lat", "lon"),
            P("lat", "lon"),
            P("lat", "lon"),
            P("lat", "lon"),
            P("lat", "lon"),
            P(None, "lat", "lon"),
            P(None, None, "lat", "lon"),
        ),
        out_specs=(
            P(None, None, "lat", "lon"),
            P(None, None, "lat", "lon"),
            P(("lat", "lon"), None, None),
        ),
        check_vma=False,
    )
```

profile of v0, /device:TPU:96, one launch (start us, length us, event | category | flops | bytes accessed | tf_op | source)
XLA Modules:
  0.0 614.5 jit_solution(14896235526079132128)
XLA Ops:
  9.0 5.8 all-to-all-start
  26.5 7.5 %gather_fusion = f32[32,8,8100]{2,1,0:T(8,128)} fusion(f32[27,8,8100]{2,1,0:T(8,128)} %param.17, s32[1024]{0:T(1024)S(1)} %pad_clamp_fusion), kind=kCustom, calls=%fused_computation | custom fusion | bytes 16588928 | tf_op jit(solution)/shard_map/jit(_take)/gather | solution.py:124
  34.0 8.3 %select_multiply_fusion = f32[16,2,8,8100]{3,2,1,0:T(8,128)} fusion(f32[16,2,8,8100]{3,2,1,0:T(8,128)} %bitcast.57, f32[16,2]{1,0:T(8,128)S(1)} %copy.142, pred[16,2]{1,0:T(8,128)(4,1)S(1)} %copy.140), kind=kLoop, calls=%fused_computation.2 | loop fusion | flops 4147200 | bytes 16588960 | tf_op jit(solution)/shard_map/mul | solution.py:124
  42.3 4.9 all-to-all-start.1
  77.0 4.9 collective-permute-start.3
  83.9 56.9 %collective-permute-done.17 = f32[2,4,270,1]{2,1,3,0:T(4,128)S(1)} collective-permute-done((f32[2,4,270,1]{2,1,3,0:T(4,128)S(1)}, f32[2,4,270,1]{2,1,3,0:T(4,128)S(1)}, u32[]{:S(2)}, u32[]{:S(2)}) %collective-permute-start.17) | collective-permute-done | bytes 8672 | tf_op jit(solution)/shard_map/ppermute | solution.py:18
  143.7 4.6 maximum_subtract_fusion
  148.5 4.9 collective-permute-start.18
  187.2 4.6 fusion.17
  200.8 18.0 %collective-permute-start.21 = (f32[2,4,270,1]{2,1,3,0:T(4,128)S(1)}, f32[2,4,270,1]{2,1,3,0:T(4,128)S(1)}, u32[]{:S(2)}, u32[]{:S(2)}) collective-permute-start(f32[2,4,270,1]{2,1,3,0:T(4,128)S(1)} %copy.201), channel_id=1, source_target_pairs={{0,1},{1,2},{2,3},{3,4},{4,5},{5,6},{6,7},{7,8},{8,9},{9,10},{10,1... | collective-permute-start | bytes 25928 | tf_op jit(solution)/shard_map/ppermute | solution.py:18
  225.4 7.3 %collective-permute-start.22 = (f32[2,4,1,272]{3,2,1,0:T(1,128)S(1)}, f32[2,4,1,272]{3,2,1,0:T(1,128)S(1)}, u32[]{:S(2)}, u32[]{:S(2)}) collective-permute-start(f32[2,4,1,272]{3,2,1,0:T(1,128)S(1)} %get-tuple-element.61), channel_id=1, source_target_pairs={{16,0},{32,16},{48,32},{64,48},{80,64},{96,80},{112,96},{17,1},{33... | collective-permute-start | bytes 26120 | tf_op jit(solution)/shard_map/ppermute | solution.py:21
  236.3 5.5 collective-permute-done.23
  262.7 28.7 %reshape_reshape.3 = f32[9,2,30,3,30,3]{5,4,1,3,2,0:T(8,128)} reshape(f32[3,3,2,90,90]{4,2,3,1,0:T(2,128)} %copy.212) | data formatting | bytes 1166400 | tf_op jit(solution)/shard_map/reshape;reshape | solution.py:86
  291.3 10.9 %reduce_sum.42 = f32[9,2,30,30]{3,1,2,0:T(2,128)} reduce(f32[9,2,30,3,30,3]{5,4,1,3,2,0:T(8,128)} %reshape_reshape.3, f32[]{:T(128)} %constant.121.clone.1), dimensions={3,5}, to_apply=%region_5.6 | reduce | flops 129600 | bytes 648004 | tf_op jit(solution)/shard_map/reduce_sum | solution.py:87
  330.0 125.4 %all-reduce.15.cloned.1.call-done = f32[128,2,900]{2,1,0:T(2,128)} async-done(((f32[128,2,900]{2,1,0:T(2,128)}), f32[128,2,900]{2,1,0:T(2,128)}) %all-reduce.15.cloned.1.call-update) | async-done | bytes 921616
  458.3 14.0 %scatter_fusion = f32[9,8,8100]{2,1,0:T(8,128)} fusion(f32[9,8,8100]{2,1,0:T(8,128)} %broadcast_in_dim.48, s32[32]{0:T(128)S(1)} %fusion.47, f32[32,8,8100]{2,1,0:T(8,128)} %bitcast.4), kind=kCustom, calls=%fused_computation.1 | custom fusion | bytes 24883328 | tf_op jit(solution)/shard_map/scatter | solution.py:140
  472.3 7.7 %reshape.272 = f32[3,3,2,4,90,90]{5,4,3,2,1,0:T(8,128)} reshape(f32[9,8,8100]{2,1,0:T(8,128)} %scatter_fusion) | data formatting | bytes 4665600 | tf_op jit(solution)/shard_map/reshape | solution.py:146
  480.0 6.5 %copy.143 = f32[2,4,3,90,3,90]{5,4,3,2,1,0:T(4,128)} copy(f32[2,4,3,90,3,90]{5,3,1,0,4,2:T(8,128)} %bitcast.58) | data formatting | bytes 4665600 | tf_op jit(solution)/shard_map/transpose | solution.py:147
  486.5 5.6 reshape.273
  492.1 10.8 %fusion.4 = (f32[2,4,270,270]{3,2,1,0:T(8,128)}, f32[2,4,270,270]{3,2,1,0:T(8,128)S(1)}) fusion(f32[2,4,270,270]{3,2,1,0:T(8,128)S(1)} %copy-done.3, f32[2,4,271,270]{3,2,1,0:T(8,128)} %fusion.5, f32[2,4,270,271]{3,2,1,0:T(8,128)} %maximum_subtract_fusion.2, f32[2,3,270,270]{3,2,1,0:T(8,128)} %fusion.28, f32[270,270]{1,0:T(8,128)} %copy.230, ...), kind=kLoop, calls=%fused_computation.8 | loop fusion | flops 6998400 | bytes 21870000 | tf_op jit(solution)/shard_map/mul | solution.py:181
  519.1 6.4 %collective-permute-start.7 = (f32[2,4,1,272]{3,2,1,0:T(1,128)S(1)}, f32[2,4,1,272]{3,2,1,0:T(1,128)S(1)}, u32[]{:S(2)}, u32[]{:S(2)}) collective-permute-start(f32[2,4,1,272]{3,2,1,0:T(1,128)S(1)} %get-tuple-element.69), channel_id=1, source_target_pairs={{16,0},{32,16},{48,32},{64,48},{80,64},{96,80},{112,96},{17,1},{33... | collective-permute-start | bytes 26120 | tf_op jit(solution)/shard_map/ppermute | solution.py:21
  528.9 5.9 collective-permute-done.6
  564.0 4.9 collective-permute-done.10
  578.0 4.5 fusion.31
  (303 shorter events, 234.3 us)
Async XLA Ops:
  9.0 33.2 %all-to-all-start = ((s32[16,1,2]{2,1,0:T(1,128)}), s32[16,1,2]{2,1,0:T(1,128)S(1)}, u32[]{:S(2)}, u32[]{:S(2)}) async-start(s32[16,1,2]{2,1,0:T(1,128)} %copy.139), calls=%async_computation | async-start | bytes 16384 | tf_op jit(solution)/shard_map/all_to_all | solution.py:132
  22.2 49.2 %collective-permute-start = (f32[1,5,270,1]{2,3,1,0:T(1,128)S(1)}, f32[1,5,270,1]{2,3,1,0:T(1,128)S(1)}, u32[]{:S(2)}, u32[]{:S(2)}) collective-permute-start(f32[1,5,270,1]{2,3,1,0:T(1,128)S(1)} %get-tuple-element.90), channel_id=1, source_target_pairs={{0,1},{1,2},{2,3},{3,4},{4,5},{5,6},{6,7},{7,8},{8,9},{9,10},{10,1... | collective-permute-start | bytes 16208 | tf_op jit(solution)/shard_map/ppermute | solution.py:18
  22.4 49.1 %collective-permute-start.1 = (f32[1,5,270,1]{2,3,1,0:T(1,128)S(1)}, f32[1,5,270,1]{2,3,1,0:T(1,128)S(1)}, u32[]{:S(2)}, u32[]{:S(2)}) collective-permute-start(f32[1,5,270,1]{2,3,1,0:T(1,128)S(1)} %get-tuple-element.91), channel_id=1, source_target_pairs={{1,0},{2,1},{3,2},{4,3},{5,4},{6,5},{7,6},{8,7},{9,8},{10,9},{11,1... | collective-permute-start | bytes 16208 | tf_op jit(solution)/shard_map/ppermute | solution.py:21
  42.3 414.4 %all-to-all-start.1 = ((f32[16,2,8,8100]{3,2,1,0:T(8,128)}), f32[16,2,8,8100]{3,2,1,0:T(8,128)}, u32[]{:S(2)}, u32[]{:S(2)}) async-start(f32[16,2,8,8100]{3,2,1,0:T(8,128)} %select_multiply_fusion), calls=%async_computation.1 | async-start | bytes 16777216 | tf_op jit(solution)/shard_map/all_to_all | solution.py:131
  47.2 408.2 %all-reduce.15.cloned.1.call-start = ((), (), s32[]{:S(2)}) async-start(), calls=%async_computation.2 | async-start | bytes 2097152
  51.1 91.1 %collective-permute-start.16 = (f32[2,4,270,1]{2,1,3,0:T(4,128)S(1)}, f32[2,4,270,1]{2,1,3,0:T(4,128)S(1)}, u32[]{:S(2)}, u32[]{:S(2)}) collective-permute-start(f32[2,4,270,1]{2,1,3,0:T(4,128)S(1)} %copy.220), channel_id=1, source_target_pairs={{1,0},{2,1},{3,2},{4,3},{5,4},{6,5},{7,6},{8,7},{9,8},{10,9},{11,1... | collective-permute-start | bytes 25928 | tf_op jit(solution)/shard_map/ppermute | solution.py:21
  55.2 85.6 %collective-permute-start.17 = (f32[2,4,270,1]{2,1,3,0:T(4,128)S(1)}, f32[2,4,270,1]{2,1,3,0:T(4,128)S(1)}, u32[]{:S(2)}, u32[]{:S(2)}) collective-permute-start(f32[2,4,270,1]{2,1,3,0:T(4,128)S(1)} %copy.221), channel_id=1, source_target_pairs={{0,1},{1,2},{2,3},{3,4},{4,5},{5,6},{6,7},{7,8},{8,9},{9,10},{10,1... | collective-permute-start | bytes 25928 | tf_op jit(solution)/shard_map/ppermute | solution.py:18
  77.0 79.7 %collective-permute-start.3 = (f32[1,5,1,272]{3,2,1,0:T(1,128)S(1)}, f32[1,5,1,272]{3,2,1,0:T(1,128)S(1)}, u32[]{:S(2)}, u32[]{:S(2)}) collective-permute-start(f32[1,5,1,272]{3,2,1,0:T(1,128)S(1)} %copy.151), channel_id=1, source_target_pairs={{16,0},{32,16},{48,32},{64,48},{80,64},{96,80},{112,96},{17,1},{33... | collective-permute-start | bytes 16328 | tf_op jit(solution)/shard_map/ppermute | solution.py:21
  81.9 73.6 %collective-permute-start.2 = (f32[1,5,1,272]{3,2,1,0:T(1,128)S(1)}, f32[1,5,1,272]{3,2,1,0:T(1,128)S(1)}, u32[]{:S(2)}, u32[]{:S(2)}) collective-permute-start(f32[1,5,1,272]{3,2,1,0:T(1,128)S(1)} %copy.150), channel_id=1, source_target_pairs={{0,16},{16,32},{32,48},{48,64},{64,80},{80,96},{96,112},{1,17},{17... | collective-permute-start | bytes 16328 | tf_op jit(solution)/shard_map/ppermute | solution.py:18
  148.5 38.7 %collective-permute-start.18 = (f32[2,4,1,272]{3,2,1,0:T(1,128)S(1)}, f32[2,4,1,272]{3,2,1,0:T(1,128)S(1)}, u32[]{:S(2)}, u32[]{:S(2)}) collective-permute-start(f32[2,4,1,272]{3,2,1,0:T(1,128)S(1)} %get-tuple-element.63), channel_id=1, source_target_pairs={{16,0},{32,16},{48,32},{64,48},{80,64},{96,80},{112,96},{17,1},{33... | collective-permute-start | bytes 26120 | tf_op jit(solution)/shard_map/ppermute | solution.py:21
  153.4 33.8 %collective-permute-start.19 = (f32[2,4,1,272]{3,2,1,0:T(1,128)S(1)}, f32[2,4,1,272]{3,2,1,0:T(1,128)S(1)}, u32[]{:S(2)}, u32[]{:S(2)}) collective-permute-start(f32[2,4,1,272]{3,2,1,0:T(1,128)S(1)} %get-tuple-element.64), channel_id=1, source_target_pairs={{0,16},{16,32},{32,48},{48,64},{64,80},{80,96},{96,112},{1,17},{17... | collective-permute-start | bytes 26120 | tf_op jit(solution)/shard_map/ppermute | solution.py:18
  200.8 22.1 %collective-permute-start.20 = (f32[2,4,270,1]{2,1,3,0:T(4,128)S(1)}, f32[2,4,270,1]{2,1,3,0:T(4,128)S(1)}, u32[]{:S(2)}, u32[]{:S(2)}) collective-permute-start(f32[2,4,270,1]{2,1,3,0:T(4,128)S(1)} %copy.199), channel_id=1, source_target_pairs={{1,0},{2,1},{3,2},{4,3},{5,4},{6,5},{7,6},{8,7},{9,8},{10,9},{11,1... | collective-permute-start | bytes 25928 | tf_op jit(solution)/shard_map/ppermute | solution.py:21
  200.8 20.6 %collective-permute-start.21 = (f32[2,4,270,1]{2,1,3,0:T(4,128)S(1)}, f32[2,4,270,1]{2,1,3,0:T(4,128)S(1)}, u32[]{:S(2)}, u32[]{:S(2)}) collective-permute-start(f32[2,4,270,1]{2,1,3,0:T(4,128)S(1)} %copy.201), channel_id=1, source_target_pairs={{0,1},{1,2},{2,3},{3,4},{4,5},{5,6},{6,7},{7,8},{8,9},{9,10},{10,1... | collective-permute-start | bytes 25928 | tf_op jit(solution)/shard_map/ppermute | solution.py:18
  225.4 10.9 %collective-permute-start.22 = (f32[2,4,1,272]{3,2,1,0:T(1,128)S(1)}, f32[2,4,1,272]{3,2,1,0:T(1,128)S(1)}, u32[]{:S(2)}, u32[]{:S(2)}) collective-permute-start(f32[2,4,1,272]{3,2,1,0:T(1,128)S(1)} %get-tuple-element.61), channel_id=1, source_target_pairs={{16,0},{32,16},{48,32},{64,48},{80,64},{96,80},{112,96},{17,1},{33... | collective-permute-start | bytes 26120 | tf_op jit(solution)/shard_map/ppermute | solution.py:21
  232.6 9.2 %collective-permute-start.23 = (f32[2,4,1,272]{3,2,1,0:T(1,128)S(1)}, f32[2,4,1,272]{3,2,1,0:T(1,128)S(1)}, u32[]{:S(2)}, u32[]{:S(2)}) collective-permute-start(f32[2,4,1,272]{3,2,1,0:T(1,128)S(1)} %get-tuple-element.62), channel_id=1, source_target_pairs={{0,16},{16,32},{32,48},{48,64},{64,80},{80,96},{96,112},{1,17},{17... | collective-permute-start | bytes 26120 | tf_op jit(solution)/shard_map/ppermute | solution.py:18
  260.9 50.9 %collective-permute-start.24 = (f32[2,4,270,1]{2,1,3,0:T(4,128)S(1)}, f32[2,4,270,1]{2,1,3,0:T(4,128)S(1)}, u32[]{:S(2)}, u32[]{:S(2)}) collective-permute-start(f32[2,4,270,1]{2,1,3,0:T(4,128)S(1)} %copy.205), channel_id=1, source_target_pairs={{1,0},{2,1},{3,2},{4,3},{5,4},{6,5},{7,6},{8,7},{9,8},{10,9},{11,1... | collective-permute-start | bytes 25928 | tf_op jit(solution)/shard_map/ppermute | solution.py:21
  261.0 49.4 %collective-permute-start.25 = (f32[2,4,270,1]{2,1,3,0:T(4,128)S(1)}, f32[2,4,270,1]{2,1,3,0:T(4,128)S(1)}, u32[]{:S(2)}, u32[]{:S(2)}) collective-permute-start(f32[2,4,270,1]{2,1,3,0:T(4,128)S(1)} %copy.207), channel_id=1, source_target_pairs={{0,1},{1,2},{2,3},{3,4},{4,5},{5,6},{6,7},{7,8},{8,9},{9,10},{10,1... | collective-permute-start | bytes 25928 | tf_op jit(solution)/shard_map/ppermute | solution.py:18
  314.3 9.1 %collective-permute-start.26 = (f32[2,4,1,272]{3,2,1,0:T(1,128)S(1)}, f32[2,4,1,272]{3,2,1,0:T(1,128)S(1)}, u32[]{:S(2)}, u32[]{:S(2)}) collective-permute-start(f32[2,4,1,272]{3,2,1,0:T(1,128)S(1)} %get-tuple-element.59), channel_id=1, source_target_pairs={{16,0},{32,16},{48,32},{64,48},{80,64},{96,80},{112,96},{17,1},{33... | collective-permute-start | bytes 26120 | tf_op jit(solution)/shard_map/ppermute | solution.py:21
  317.2 9.2 %collective-permute-start.27 = (f32[2,4,1,272]{3,2,1,0:T(1,128)S(1)}, f32[2,4,1,272]{3,2,1,0:T(1,128)S(1)}, u32[]{:S(2)}, u32[]{:S(2)}) collective-permute-start(f32[2,4,1,272]{3,2,1,0:T(1,128)S(1)} %get-tuple-element.60), channel_id=1, source_target_pairs={{0,16},{16,32},{32,48},{48,64},{64,80},{80,96},{96,112},{1,17},{17... | collective-permute-start | bytes 26120 | tf_op jit(solution)/shard_map/ppermute | solution.py:18
  505.9 10.6 %collective-permute-start.5 = (f32[2,4,270,1]{2,1,3,0:T(4,128)S(1)}, f32[2,4,270,1]{2,1,3,0:T(4,128)S(1)}, u32[]{:S(2)}, u32[]{:S(2)}) collective-permute-start(f32[2,4,270,1]{2,1,3,0:T(4,128)S(1)} %copy.157), channel_id=1, source_target_pairs={{1,0},{2,1},{3,2},{4,3},{5,4},{6,5},{7,6},{8,7},{9,8},{10,9},{11,1... | collective-permute-start | bytes 25928 | tf_op jit(solution)/shard_map/ppermute | solution.py:21
  519.1 9.8 %collective-permute-start.7 = (f32[2,4,1,272]{3,2,1,0:T(1,128)S(1)}, f32[2,4,1,272]{3,2,1,0:T(1,128)S(1)}, u32[]{:S(2)}, u32[]{:S(2)}) collective-permute-start(f32[2,4,1,272]{3,2,1,0:T(1,128)S(1)} %get-tuple-element.69), channel_id=1, source_target_pairs={{16,0},{32,16},{48,32},{64,48},{80,64},{96,80},{112,96},{17,1},{33... | collective-permute-start | bytes 26120 | tf_op jit(solution)/shard_map/ppermute | solution.py:21
  525.5 9.3 %collective-permute-start.6 = (f32[2,4,1,272]{3,2,1,0:T(1,128)S(1)}, f32[2,4,1,272]{3,2,1,0:T(1,128)S(1)}, u32[]{:S(2)}, u32[]{:S(2)}) collective-permute-start(f32[2,4,1,272]{3,2,1,0:T(1,128)S(1)} %get-tuple-element.70), channel_id=1, source_target_pairs={{0,16},{16,32},{32,48},{48,64},{64,80},{80,96},{96,112},{1,17},{17... | collective-permute-start | bytes 26120 | tf_op jit(solution)/shard_map/ppermute | solution.py:18
  559.5 9.3 %collective-permute-start.10 = (f32[2,4,1,272]{3,2,1,0:T(1,128)S(1)}, f32[2,4,1,272]{3,2,1,0:T(1,128)S(1)}, u32[]{:S(2)}, u32[]{:S(2)}) collective-permute-start(f32[2,4,1,272]{3,2,1,0:T(1,128)S(1)} %get-tuple-element.68), channel_id=1, source_target_pairs={{0,16},{16,32},{32,48},{48,64},{64,80},{80,96},{96,112},{1,17},{17... | collective-permute-start | bytes 26120 | tf_op jit(solution)/shard_map/ppermute | solution.py:18
  589.3 9.3 %collective-permute-start.14 = (f32[2,4,1,272]{3,2,1,0:T(1,128)S(1)}, f32[2,4,1,272]{3,2,1,0:T(1,128)S(1)}, u32[]{:S(2)}, u32[]{:S(2)}) collective-permute-start(f32[2,4,1,272]{3,2,1,0:T(1,128)S(1)} %get-tuple-element.66), channel_id=1, source_target_pairs={{0,16},{16,32},{32,48},{48,64},{64,80},{80,96},{96,112},{1,17},{17... | collective-permute-start | bytes 26120 | tf_op jit(solution)/shard_map/ppermute | solution.py:18
  (65 other events, 544.8 us)
Sparse Core Ops, SparseCore 0:
  310.5 144.8 all-reduce.14
where the time goes:
time: 624 us; the launch traced here: 615 us
  waiting for transfers between devices  209 us (33%)
  local copies, waits for them, and re-layouts  176 us (28%)
  other arithmetic  122 us (20%)
  starting transfers between devices  91.5 us (15%)
  between operations  15.8 us (3%)
    unnamed x2, waiting for transfers between devices  125 us
    ppermute x14, waiting for transfers between devices, extended(): lax.ppermute(lax.slice_in_dim(block, block.shape[dim] - width, None, axis...  83.5 us
    ppermute x14, starting transfers between devices, extended(): lax.ppermute(lax.slice_in_dim(block, 0, width, axis=dim), axis, backward)  41.9 us
    ppermute x14, starting transfers between devices, extended(): lax.ppermute(lax.slice_in_dim(block, block.shape[dim] - width, None, axis...  38.9 us
    unnamed x135, local copies, waits for them, and re-layouts  34.7 us
    another operation x1, local copies, waits for them, and re-layouts, coarsen(): fine_cells.reshape(tile_count, 2, coarse_side, COARSE, coarse_side, COARSE)  28.7 us
    mul x6, other arithmetic, vertical(): flux = mixing * (center[:, :-1] - center[:, 1:])  19.3 us
    slice x13, local copies, waits for them, and re-layouts, extended(): lax.slice_in_dim(block, block.shape[dim] - width, None, axis=dim)  15.4 us
  transfers between devices with their start and end apart: 31, of which 9 were waited for; matrix products, arithmetic and copies ran while one was open for 34% of the time, Pallas kernels for 0%

commit v1 on v0

v1 whole, which is shorter than its diff:
```python
import jax
import jax.numpy as jnp
from jax import lax
from jax.experimental import pallas as pl
from jax.experimental.pallas import tpu as pltpu
from jax.sharding import PartitionSpec as P

F32 = jnp.float32
I32 = jnp.int32
TILE = 90
SIDE = 3
COLUMNS = 48
HALO = 3
STEPS = 3
SLOTS = 27
PAIR = 2
LEV = 4
CELLS = TILE * TILE
N = TILE * SIDE
FLAT = 8192
TAIL = 8064
TAG = CELLS - TAIL
TOP = 16
ROWS = 296
LANES = 384
CHUNKS = 34
COARSE = 30
VMEM = pl.BlockSpec(memory_space=pltpu.VMEM)
SMEM = pl.BlockSpec(memory_space=pltpu.SMEM)
ANY = pl.BlockSpec(memory_space=pl.ANY)


def aligned(x):
    return pl.multiple_of(x, 8)


def pack_kernel(ids, stored, after, out, held, tail, empty, count, route, in_sem, out_sem, tail_sem, empty_sem):
    owners = out.shape[0]

    def fetch(s):
        return pltpu.make_async_copy(stored.at[s], held.at[s], in_sem.at[s])

    def send(s, owner, rank):
        return pltpu.make_async_copy(
            held.at[s, :, pl.ds(0, TAIL)], out.at[owner, rank, :, pl.ds(0, TAIL)], out_sem.at[s]
        )

    def send_tail(s, owner, rank):
        return pltpu.make_async_copy(
            tail.at[s], out.at[owner, rank, :, pl.ds(TAIL, 128)], tail_sem.at[s]
        )

    def send_empty(owner, rank):
        return pltpu.make_async_copy(
            empty, out.at[owner, rank, :, pl.ds(TAIL, 128)], empty_sem.at[owner, rank]
        )

    @pl.loop(0, SLOTS)
    def _(s):
        @pl.when(ids[s] >= 0)
        def _():
            fetch(s).start()

    @pl.loop(0, owners)
    def _(o):
        count[o] = 0

    empty[...] = jnp.full((8, 128), -1.0, F32)
    lane = lax.broadcasted_iota(I32, (8, 128), 1)

    @pl.loop(0, SLOTS)
    def _(s):
        tile = ids[s]

        @pl.when(tile >= 0)
        def _():
            row = tile // COLUMNS
            column = tile - row * COLUMNS
            owner = column // SIDE
            rank = count[owner]
            count[owner] = rank + 1
            route[s] = owner * PAIR + rank
            place = row * SIDE + column - owner * SIDE
            fetch(s).wait()
            last = jnp.concatenate([held[s, :, TAIL:CELLS], jnp.zeros((8, 128 - TAG), F32)], axis=1)
            tail[s] = jnp.where(lane < TAG, last, place.astype(F32))
            send(s, owner, rank).start()
            send_tail(s, owner, rank).start()

    for rank in range(PAIR):

        @pl.loop(0, owners)
        def _(o):
            @pl.when(count[o] <= rank)
            def _():
                send_empty(o, rank).start()

    @pl.loop(0, SLOTS)
    def _(s):
        @pl.when(ids[s] >= 0)
        def _():
            owner = route[s] // PAIR
            rank = route[s] - owner * PAIR
            send(s, owner, rank).wait()
            send_tail(s, owner, rank).wait()

    for rank in range(PAIR):

        @pl.loop(0, owners)
        def _(o):
            @pl.when(count[o] <= rank)
            def _():
                send_empty(o, rank).wait()


def pack_tiles(ids, stored, after, owners):
    return pl.pallas_call(
        pack_kernel,
        out_shape=jax.ShapeDtypeStruct((owners, PAIR, 8, FLAT), F32),
        in_specs=[SMEM, ANY, ANY],
        out_specs=ANY,
        scratch_shapes=[
            pltpu.VMEM((SLOTS, 8, CELLS), F32),
            pltpu.VMEM((SLOTS, 8, 128), F32),
            pltpu.VMEM((8, 128), F32),
            pltpu.SMEM((owners,), I32),
            pltpu.SMEM((SLOTS,), I32),
            pltpu.SemaphoreType.DMA((SLOTS,)),
            pltpu.SemaphoreType.DMA((SLOTS,)),
            pltpu.SemaphoreType.DMA((SLOTS,)),
            pltpu.SemaphoreType.DMA((owners, PAIR)),
        ],
        name="pack_tiles",
    )(ids, stored, after)


def strip_columns(load, count, first):
    lane = lax.broadcasted_iota(I32, (N + 2, 128), 1)
    strip = jnp.zeros((N + 2, 128), F32)
    for f in range(count):
        moved = pltpu.roll(load(f), (HALO * f - first) % 128, 1)
        strip = jnp.where((lane >= HALO * f) & (lane < HALO * f + HALO), moved, strip)
    return strip.T[0 : HALO * count]


def wet_field(wet, rows, row0):
    row = lax.broadcasted_iota(I32, (rows, LANES), 0) + row0
    lane = lax.broadcasted_iota(I32, (rows, LANES), 1)
    bands = []
    for r in range(SIDE):
        w = [wet[r, c].astype(F32) for c in range(SIDE)]
        bands.append(jnp.where(lane < TILE, w[0], jnp.where(lane < 2 * TILE, w[1], w[2])))
    return jnp.where(row < TILE, bands[0], jnp.where(row < 2 * TILE, bands[1], bands[2]))


def edges_kernel(wet, zd, zf, md, mf, vm, forcing, adjoint, west, east, south, north, held):
    views = [zd, zf, md, mf, vm]

    def plane(f):
        if f < 6:
            return views[f - 1]
        if f < 8:
            return forcing.at[f - 6]
        return adjoint.at[(f - 8) // LEV, (f - 8) % LEV]

    full = wet_field(wet, N + 2, 0)
    held[0] = full[:, 0:128]
    held[1] = full[:, 256:384]
    south[0:HALO, 0:N] = full[0:HALO, 0:N]
    north[0:HALO, 0:N] = full[N - HALO : N, 0:N]
    for f in range(1, 16):
        ref = plane(f)
        south[HALO * f : HALO * f + HALO, 0:N] = ref[0:HALO, :]
        north[HALO * f : HALO * f + HALO, 0:N] = ref[N - HALO : N, :]

    def low(f):
        if f == 0:
            return held[0]
        return jnp.concatenate([plane(f)[:, 0:128], jnp.zeros((2, 128), F32)], axis=0)

    def high(f):
        if f == 0:
            return held[1]
        part = jnp.concatenate([plane(f)[:, 256:N], jnp.zeros((N, LANES - N), F32)], axis=1)
        return jnp.concatenate([part, jnp.zeros((2, 128), F32)], axis=0)

    west[...] = strip_columns(low, 16, 0)
    east[...] = strip_columns(high, 16, N - HALO - 256)


def edge_strips(wet, zd, zf, md, mf, vm, forcing, adjoint):
    columns = jax.ShapeDtypeStruct((48, N + 2), F32)
    rows = jax.ShapeDtypeStruct((48, N + 2), F32)
    return pl.pallas_call(
        edges_kernel,
        out_shape=(columns, columns, rows, rows),
        in_specs=[SMEM] + [VMEM] * 7,
        out_specs=(VMEM,) * 4,
        scratch_shapes=[pltpu.VMEM((2, N + 2, 128), F32)],
        name="edge_strips",
    )(wet, zd, zf, md, mf, vm, forcing, adjoint)


def corners_kernel(south, north, west, east, to_south, to_north):
    for rows, out, first in ((south, to_south, 0), (north, to_north, N - HALO)):
        out[:, 0:N] = rows[:, 0:N]
        out[:, N : N + HALO] = west[:, first : first + HALO]
        out[:, N + HALO : N + 2 * HALO] = east[:, first : first + HALO]


def with_corners(south, north, west, east):
    shape = jax.ShapeDtypeStruct((south.shape[0], LANES), F32)
    return pl.pallas_call(
        corners_kernel,
        out_shape=(shape, shape),
        in_specs=[VMEM] * 4,
        out_specs=(VMEM,) * 2,
        name="row_strips",
    )(south, north, west, east)


def insert_halos(ext, base, count, west, east, south, north):
    blank = jnp.zeros((128 - HALO * count, N + 2), F32)
    from_west = jnp.concatenate([west[...], blank], axis=0).T
    from_east = jnp.concatenate([east[...], blank], axis=0).T
    blank = jnp.zeros((128 - HALO * count, 128), F32)
    low = jnp.concatenate([south[:, 256:384], blank], axis=0).T
    high = jnp.concatenate([north[:, 256:384], blank], axis=0).T
    for f in range(count):
        s = slice(HALO * f, HALO * f + HALO)
        field = ext.at[base + f]
        field[TOP : TOP + N + 2, LANES - HALO : LANES] = from_west[:, s]
        field[TOP : TOP + N + 2, N : N + HALO] = from_east[:, s]
        for first, rows, block in ((TOP - HALO, south, low), (TOP + N, north, high)):
            at = N - 256
            field[first : first + HALO, 0:N] = rows[s, 0:N]
            field[first : first + HALO, LANES - HALO : LANES] = block[at : at + HALO, s]
            field[first : first + HALO, N : N + HALO] = block[at + HALO : at + 2 * HALO, s]


def row_mask(k):
    return lax.broadcasted_iota(I32, (8, LANES), 0) == k


def to_south(current, following):
    return pltpu.roll(jnp.where(row_mask(0), following, current), 7, 0)


def to_north(current, previous):
    return pltpu.roll(jnp.where(row_mask(7), previous, current), 1, 0)


def stencil(src, b, coef):
    center, east, west, north, south, mix = coef
    result = []
    for t in range(2):
        level = [src[t * LEV + k, pl.ds(b, 8), :] for k in range(LEV)]
        flux = [mix * (level[k] - level[k + 1]) for k in range(LEV - 1)]
        for k in range(LEV):
            c = level[k]
            f = t * LEV + k
            up = to_south(c, src[f, pl.ds(aligned(b + 8), 8), :])
            down = to_north(c, src[f, pl.ds(aligned(b - 8), 8), :])
            new = center * c + east * pltpu.roll(c, LANES - 1, 1) + west * pltpu.roll(c, 1, 1)
            new = new + (north * up + south * down)
            if k > 0:
                new = new + flux[k - 1]
            if k < LEV - 1:
                new = new - flux[k]
            result.append((c, new))
    return result


def adjoint_kernel(
    wet, labels, zd, zf, md, mf, vm, forcing, adjoint, west, east, south, north,
    initial, forward_coef, control,
    ext, other, coef, surface, coarse, piece,
):
    views = [zd, zf, md, mf, vm]
    ext[0, TOP : TOP + N + 2, :] = wet_field(wet, N + 2, 0)
    for f in range(1, 16):
        if f < 6:
            value = views[f - 1]
        elif f < 8:
            value = forcing.at[f - 6]
        else:
            value = adjoint.at[(f - 8) // LEV, (f - 8) % LEV]
        ext[f, TOP : TOP + N, 0:N] = value[...]
    insert_halos(ext, 0, 16, west, east, south, north)

    def coefficients(r, carry):
        north_a, north_b = carry
        b = aligned(r * 8)
        w, z_d, z_f, m_d, m_f, v = [ext[f, pl.ds(b, 8), :] for f in range(6)]
        east_open = w * pltpu.roll(w, LANES - 1, 1)
        north_open = w * to_south(w, ext[0, pl.ds(aligned(b + 8), 8), :])
        de = z_d * east_open
        ue = 0.5 * z_f * east_open
        dn = m_d * north_open
        vn = 0.5 * m_f * north_open
        ea, eb, na, nb = de + ue, ue - de, dn + vn, vn - dn
        eb_west = pltpu.roll(eb, 1, 1)
        nb_south = to_north(nb, north_b)
        rows = pl.ds(b, 8)
        forward_coef[0, rows, :] = 1.0 + ((eb_west - ea) + (nb_south - na))
        forward_coef[1, rows, :] = -eb
        forward_coef[2, rows, :] = pltpu.roll(ea, 1, 1)
        forward_coef[3, rows, :] = -nb
        forward_coef[4, rows, :] = to_north(na, north_a)
        forward_coef[5, rows, :] = v * w
        forward_coef[6, rows, :] = ext[6, rows, :] * w
        forward_coef[7, rows, :] = ext[7, rows, :] * w
        coef[0, rows, :] = ea
        coef[1, rows, :] = -eb_west
        coef[2, rows, :] = na
        coef[3, rows, :] = -nb_south
        return na, nb

    zero = jnp.zeros((8, LANES), F32)
    lax.fori_loop(1, CHUNKS + 2, coefficients, (zero, zero))

    def load_coef(b):
        rows = pl.ds(b, 8)
        return [forward_coef[0, rows, :]] + [coef[i, rows, :] for i in range(4)] + [forward_coef[5, rows, :]]

    lam = ext.at[pl.ds(8, 8)]

    def step(src, dst, first):
        @pl.loop(1, CHUNKS + 2)
        def _(r):
            b = aligned(r * 8)
            for f, (old, new) in enumerate(stencil(src, b, load_coef(b))):
                dst[f, pl.ds(b, 8), :] = new
                if f % LEV == 0:
                    t = f // LEV
                    surface[t, pl.ds(b, 8), :] = old if first else surface[t, pl.ds(b, 8), :] + old

    step(lam, other, True)
    step(other, lam, False)

    def finish(i, rows):
        b = aligned(TOP + 8 * i)
        w = ext[0, pl.ds(b, 8), :]
        for f, (old, new) in enumerate(stencil(lam, b, load_coef(b))):
            t, k = f // LEV, f % LEV
            if rows == 8:
                initial[t, k, pl.ds(aligned(8 * i), 8), :] = (w * new)[:, 0:N]
            else:
                initial[t, k, 8 * i : 8 * i + rows, :] = (w * new)[0:rows, 0:N]
            if k == 0:
                surface[t, pl.ds(b, 8), :] = w * (surface[t, pl.ds(b, 8), :] + old)

    @pl.loop(0, N // 8)
    def _(i):
        finish(i, 8)

    finish(N // 8, N % 8)

    BF = jnp.bfloat16

    def parts(x):
        hi = x.astype(BF)
        rest = x - hi.astype(F32)
        mid = rest.astype(BF)
        return hi, mid, (rest - mid.astype(F32)).astype(BF)

    def band(shape, out_axis):
        i = lax.broadcasted_iota(I32, shape, out_axis) * 3
        j = lax.broadcasted_iota(I32, shape, 1 - out_axis)
        return ((j >= i) & (j < i + 3) & (j < N)).astype(F32).astype(BF)

    by_row = band((96, N + 2), 0)
    by_lane = band((LANES, 128), 1)
    shape = (N + 2, LANES)
    inside = (lax.broadcasted_iota(I32, shape, 0) < N) & (lax.broadcasted_iota(I32, shape, 1) < N)
    for t in range(2):
        cells = jnp.where(inside, surface[t, TOP : TOP + N + 2, :], 0.0)
        half = sum(jnp.dot(by_row, p, preferred_element_type=F32) for p in parts(cells))
        full = sum(jnp.dot(p, by_lane, preferred_element_type=F32) for p in parts(half))
        coarse[t] = full / 9.0
    control[...] = jnp.zeros(control.shape, F32)
    piece[...] = jnp.zeros((16, 128), F32)
    part = COARSE // 2
    for r in range(SIDE):
        for c in range(SIDE):
            for t in range(2):
                for h in range(2):
                    at = COARSE * r + part * h
                    lane = 64 * h + COARSE * t
                    piece[0:part, lane : lane + COARSE] = coarse[
                        t, at : at + part, COARSE * c : COARSE * c + COARSE
                    ]
            control[labels[r, c]] = piece[...]


def adjoint_window(wet, labels, zd, zf, md, mf, vm, forcing, adjoint, west, east, south, north, owners):
    return pl.pallas_call(
        adjoint_kernel,
        out_shape=(
            jax.ShapeDtypeStruct((2, LEV, N, N), F32),
            jax.ShapeDtypeStruct((8, ROWS, LANES), F32),
            jax.ShapeDtypeStruct((owners, 16, 128), F32),
        ),
        in_specs=[SMEM, SMEM] + [VMEM] * 11,
        out_specs=(VMEM,) * 3,
        scratch_shapes=[
            pltpu.VMEM((16, ROWS, LANES), F32),
            pltpu.VMEM((8, ROWS, LANES), F32),
            pltpu.VMEM((4, ROWS, LANES), F32),
            pltpu.VMEM((2, ROWS, LANES), F32),
            pltpu.VMEM((2, 96, 128), F32),
            pltpu.VMEM((16, 128), F32),
        ],
        name="adjoint_window",
    )(wet, labels, zd, zf, md, mf, vm, forcing, adjoint, west, east, south, north)


def unpack_kernel(arrived, state, west, east, south, north, tags, slot_of, tiles, lined, tag_sem, tile_sem):
    sources = arrived.shape[0]
    copy = pltpu.make_async_copy(
        arrived.at[:, :, pl.ds(0, 1), pl.ds(TAIL, 128)], tags, tag_sem
    )
    copy.start()
    places = SIDE * SIDE

    @pl.loop(0, places)
    def _(p):
        slot_of[p] = -1

    copy.wait()

    @pl.loop(0, sources * PAIR)
    def _(i):
        source = i // PAIR
        place = tags[source, i - source * PAIR, 0, TAG].astype(I32)

        @pl.when(place >= 0)
        def _():
            slot_of[place] = i

    def fetch(p):
        slot = slot_of[p]
        source = slot // PAIR
        return pltpu.make_async_copy(arrived.at[source, slot - source * PAIR], tiles.at[p], tile_sem.at[p])

    @pl.loop(0, places)
    def _(p):
        @pl.when(slot_of[p] >= 0)
        def _():
            fetch(p).start()

        @pl.when(slot_of[p] < 0)
        def _():
            tiles[p] = jnp.zeros((8, FLAT), F32)

    @pl.loop(0, SIDE)
    def _(r):
        for c in range(SIDE):

            @pl.when(slot_of[r * SIDE + c] >= 0)
            def _():
                fetch(r * SIDE + c).wait()

        for y in range(TILE):
            for c in range(SIDE):
                lined[r * TILE + y, :, TILE * c : TILE * c + TILE] = tiles[
                    r * SIDE + c, :, TILE * y : TILE * y + TILE
                ]

    @pl.loop(0, CHUNKS)
    def _(g):
        state[:, pl.ds(aligned(TOP + 8 * g), 8), :] = jnp.swapaxes(lined[pl.ds(8 * g, 8)], 0, 1)

    west[...] = strip_columns(lambda f: state[f, TOP : TOP + N + 2, 0:128], 8, 0)
    east[...] = strip_columns(lambda f: state[f, TOP : TOP + N + 2, 256:384], 8, N - HALO - 256)
    for f in range(8):
        south[HALO * f : HALO * f + HALO, 0:N] = state[f, TOP : TOP + HALO, 0:N]
        north[HALO * f : HALO * f + HALO, 0:N] = state[f, TOP + N - HALO : TOP + N, 0:N]


def unpack_tiles(arrived):
    strip = jax.ShapeDtypeStruct((24, N + 2), F32)
    return pl.pallas_call(
        unpack_kernel,
        out_shape=(jax.ShapeDtypeStruct((8, ROWS, LANES), F32),) + (strip,) * 4,
        in_specs=[ANY],
        out_specs=(VMEM,) * 5,
        scratch_shapes=[
            pltpu.SMEM((arrived.shape[0], PAIR, 1, 128), F32),
            pltpu.SMEM((SIDE * SIDE,), I32),
            pltpu.VMEM((SIDE * SIDE, 8, FLAT), F32),
            pltpu.VMEM((8 * CHUNKS, 8, LANES), F32),
            pltpu.SemaphoreType.DMA,
            pltpu.SemaphoreType.DMA((SIDE * SIDE,)),
        ],
        name="unpack_tiles",
    )(arrived)


def forward_kernel(state, coef, west, east, south, north, final, first, second, sem):
    copy = pltpu.make_async_copy(state, first, sem)
    copy.start()
    copy.wait()
    insert_halos(first, 0, 8, west, east, south, north)

    def advanced(src, b):
        rows = pl.ds(b, 8)
        result = []
        for f, (_, new) in enumerate(stencil(src, b, [coef[i, rows, :] for i in range(6)])):
            if f % LEV == 0:
                new = new + coef[6 + f // LEV, rows, :]
            result.append(new)
        return result

    def step(src, dst):
        @pl.loop(1, CHUNKS + 2)
        def _(r):
            b = aligned(r * 8)
            for f, new in enumerate(advanced(src, b)):
                dst[f, pl.ds(b, 8), :] = new

    step(first, second)
    step(second, first)

    @pl.loop(0, N // 8)
    def _(i):
        for f, new in enumerate(advanced(first, aligned(TOP + 8 * i))):
            final[f // LEV, f % LEV, pl.ds(aligned(8 * i), 8), :] = new[:, 0:N]

    i = N // 8
    for f, new in enumerate(advanced(first, TOP + 8 * i)):
        final[f // LEV, f % LEV, 8 * i : N, :] = new[0 : N % 8, 0:N]


def forward_window(state, coef, west, east, south, north):
    return pl.pallas_call(
        forward_kernel,
        out_shape=jax.ShapeDtypeStruct((2, LEV, N, N), F32),
        in_specs=[ANY] + [VMEM] * 5,
        out_specs=VMEM,
        scratch_shapes=[
            pltpu.VMEM((8, ROWS, LANES), F32),
            pltpu.VMEM((8, ROWS, LANES), F32),
            pltpu.SemaphoreType.DMA,
        ],
        name="forward_window",
    )(state, coef, west, east, south, north)


def neighbours(low, high, axis, periodic):
    count = lax.axis_size(axis)
    up = [(i, i + 1) for i in range(count - 1)] + ([(count - 1, 0)] if periodic else [])
    down = [(b, a) for a, b in up]
    return lax.ppermute(high, axis, up), lax.ppermute(low, axis, down)


def per_device(
    stored_tiles, stored_ids, wet_tiles, control_map, zonal_diffusivity, meridional_diffusivity,
    zonal_flow, meridional_flow, vertical_mixing, forcing, final_adjoint,
):
    owners = lax.axis_size("lon")
    devices = lax.axis_size(("lat", "lon"))
    fields = (
        zonal_diffusivity, zonal_flow, meridional_diffusivity, meridional_flow, vertical_mixing,
        forcing, final_adjoint,
    )
    low, high, bottom, top = edge_strips(wet_tiles, *fields)
    west, east = neighbours(low, high, "lon", True)
    outgoing = pack_tiles(stored_ids, stored_tiles, low, owners)
    outgoing, west, east = lax.optimization_barrier((outgoing, west, east))
    arrived = lax.all_to_all(outgoing, "lon", split_axis=0, concat_axis=0, tiled=True)
    south, north = neighbours(*with_corners(bottom, top, west, east), "lat", False)
    initial, coef, pieces = adjoint_window(
        wet_tiles, control_map, *fields, west, east, south, north, devices
    )
    gathered = lax.all_to_all(pieces, ("lat", "lon"), split_axis=0, concat_axis=0, tiled=True)
    total = jnp.sum(gathered, axis=0)[: COARSE // 2]
    total = jnp.stack([total[:, :60], total[:, 64:124]]).reshape(2, COARSE // 2, 2, COARSE)
    control = total.transpose(2, 0, 1, 3).reshape(1, 2, COARSE * COARSE)

    state, low, high, bottom, top = unpack_tiles(arrived)
    west, east = neighbours(low, high, "lon", True)
    south, north = neighbours(*with_corners(bottom, top, west, east), "lat", False)
    final = forward_window(state, coef, west, east, south, north)
    return final, initial, control


def solution(mesh):
    grid = P("lat", "lon")
    return jax.shard_map(
        per_device,
        mesh=mesh,
        in_specs=(
            P(("lat", "lon"), None, None), P(("lat", "lon")), grid, grid, grid, grid, grid, grid, grid,
            P(None, "lat", "lon"), P(None, None, "lat", "lon"),
        ),
        out_specs=(
            P(None, None, "lat", "lon"), P(None, None, "lat", "lon"), P(("lat", "lon"), None, None),
        ),
        check_vma=False,
    )
```

time: 624 us -> 261 us (0.42)
  the two profiles are of different devices: /device:TPU:96 before, /device:TPU:24 now
where the time goes in v1:
time: 261 us; the launch traced here: 260 us
  waiting for transfers between devices  124 us (48%)
  Pallas kernels  66 us (25%)
  starting transfers between devices  26.1 us (10%)
  blocking collectives  22.7 us (9%)
  local copies, waits for them, and re-layouts  19.3 us (7%)
    all_to_all x1, waiting for transfers between devices, per_device(): lax.all_to_all(outgoing, 'lon', split_axis=0, concat_axis=0, tiled=True)  108 us
    pallas_call x1, Pallas kernels, adjoint_window(): pl.pallas_call(adjoint_kernel, out_shape=(jax.ShapeDtypeStruct((2, LEV, N...  26.9 us
    all_to_all x1, blocking collectives, per_device(): lax.all_to_all(pieces, ('lat', 'lon'), split_axis=0, concat_axis=0, tiled...  22.7 us
    ppermute x8, starting transfers between devices, neighbours(): return (lax.ppermute(high, axis, up), lax.ppermute(low, axis, down))  21.3 us
    pallas_call x1, Pallas kernels, forward_window(): pl.pallas_call(forward_kernel, out_shape=jax.ShapeDtypeStruct((2, LEV, N,...  19.9 us
    unnamed x20, local copies, waits for them, and re-layouts  18.4 us
    ppermute x8, waiting for transfers between devices, neighbours(): return (lax.ppermute(high, axis, up), lax.ppermute(low, axis, down))  16.9 us
    pallas_call x1, Pallas kernels, unpack_tiles(): pl.pallas_call(unpack_kernel, out_shape=(jax.ShapeDtypeStruct((8, ROWS, L...  6.98 us
  transfers between devices with their start and end apart: 9, of which 6 were waited for; matrix products, arithmetic and copies ran while one was open for 2% of the time, Pallas kernels for 2%

profile of v1, /device:TPU:24, one launch (start us, length us, event | category | flops | bytes accessed | tf_op | source)
XLA Modules:
  0.0 259.5 jit_solution(3054002123202361966)
XLA Ops:
  0.6 2.1 copy.20.forcing
  2.7 3.9 %copy.21.adjoint = f32[2,4,270,270]{3,2,1,0:T(8,128)} copy(f32[2,4,270,270]{3,1,2,0:T(4,128)} %param.21) | data formatting | bytes 4665600 | tf_op args[10]
  6.6 4.8 %edge_strips.1 = (f32[48,272]{1,0:T(8,128)}, f32[48,272]{1,0:T(8,128)}, f32[48,272]{1,0:T(8,128)}, f32[48,272]{1,0:T(8,128)}) custom-call(s32[3,3]{1,0:T(4,128)} %wet.3, f32[270,270]{1,0:T(8,128)} %zd.3, f32[270,270]{1,0:T(8,128)} %zf.3, f32[270,270]{1,0:T(8,128)} %md.3, f32[270,270]{1,0:T(8,128)} %mf.3, f32[270,270]{1,0:T(8,128)} %vm.3, ...), custom_call_target="tpu_custom_call" | custom-call | tf_op jit(solution)/shard_map/edge_strips/pallas_call | solution.py:194
  11.5 3.9 %collective-permute-start.1 = (f32[48,272]{1,0:T(8,128)}, f32[48,272]{1,0:T(8,128)S(1)}, u32[]{:S(2)}, u32[]{:S(2)}) collective-permute-start(f32[48,272]{1,0:T(8,128)} %get-tuple-element.22.after), channel_id=1, source_target_pairs={{1,0},{2,1},{3,2},{4,3},{5,4},{6,5},{7,6},{8,7},{9,8},{10,9},{11,1... | collective-permute-start | bytes 156680 | tf_op jit(solution)/shard_map/ppermute | solution.py:554
  15.3 4.0 %pack_tiles.1 = f32[16,2,8,8192]{3,2,1,0:T(8,128)} custom-call(s32[27]{0:T(128)} %ids.1, f32[27,8,8100]{2,1,0:T(8,128)} %stored.1, f32[48,272]{1,0:T(8,128)} %get-tuple-element.22.after), custom_call_target="tpu_custom_call" | custom-call | tf_op jit(solution)/shard_map/pack_tiles/pallas_call | solution.py:117
  20.1 1.7 row_strips.2
  21.8 5.5 %collective-permute-start.2 = (f32[48,384]{1,0:T(8,128)}, f32[48,384]{1,0:T(8,128)S(1)}, u32[]{:S(2)}, u32[]{:S(2)}) collective-permute-start(f32[48,384]{1,0:T(8,128)} %get-tuple-element.30), channel_id=1, source_target_pairs={{0,16},{16,32},{32,48},{48,64},{64,80},{80,96},{96,112},{1,17},{17... | collective-permute-start | bytes 221192 | tf_op jit(solution)/shard_map/ppermute | solution.py:554
  27.3 1.9 collective-permute-start.3
  29.6 7.8 %collective-permute-done.3.north = f32[48,384]{1,0:T(8,128)S(1)} collective-permute-done((f32[48,384]{1,0:T(8,128)}, f32[48,384]{1,0:T(8,128)S(1)}, u32[]{:S(2)}, u32[]{:S(2)}) %collective-permute-start.3) | collective-permute-done | bytes 73760 | tf_op jit(solution)/shard_map/ppermute | solution.py:554
  38.1 26.9 %adjoint_window.1 = (f32[2,4,270,270]{3,2,1,0:T(8,128)}, f32[8,296,384]{2,1,0:T(8,128)}, f32[128,16,128]{2,1,0:T(8,128)}) custom-call(s32[3,3]{1,0:T(4,128)} %wet.3, s32[3,3]{1,0:T(4,128)} %labels.1, f32[270,270]{1,0:T(8,128)} %zd.3, f32[270,270]{1,0:T(8,128)} %zf.3, f32[270,270]{1,0:T(8,128)} %md.3, f32[270,270]{1,0:T(8,128)} %mf.3, f32[270,270]{1,0:T(8,128)} %vm.3, ...), custom_call_target="tpu_custom_call" | custom-call | tf_op jit(solution)/shard_map/adjoint_window/pallas_call | solution.py:397
  65.0 22.7 %all_to_all.10 = f32[128,16,128]{2,1,0:T(8,128)S(1)} all-to-all(f32[128,16,128]{2,1,0:T(8,128)} %get-tuple-element.40), channel_id=1, replica_groups=mesh['lat'=8,'lon'=16] {'lat','lon'}, dimensions={0} | all-to-all | bytes 2097152 | tf_op jit(solution)/shard_map/all_to_all | solution.py:576
  87.7 4.8 %all-to-all-start = ((f32[16,2,8,8192]{3,2,1,0:T(8,128)}), f32[16,2,8,8192]{3,2,1,0:T(8,128)}, u32[]{:S(2)}, u32[]{:S(2)}) async-start(f32[16,2,8,8192]{3,2,1,0:T(8,128)} %pack_tiles.1), calls=%async_computation | async-start | bytes 16777216 | tf_op jit(solution)/shard_map/all_to_all | solution.py:571
  92.5 4.9 %copy.26 = f32[2,4,270,270]{3,1,2,0:T(4,128)} copy(f32[2,4,270,270]{3,2,1,0:T(8,128)} %get-tuple-element.45) | data formatting | bytes 4665600
  97.6 107.6 %all-to-all-done.arrived = f32[16,2,8,8192]{3,2,1,0:T(8,128)} async-done(((f32[16,2,8,8192]{3,2,1,0:T(8,128)}), f32[16,2,8,8192]{3,2,1,0:T(8,128)}, u32[]{:S(2)}, u32[]{:S(2)}) %all-to-all-start) | async-done | bytes 8388640 | tf_op jit(solution)/shard_map/all_to_all | solution.py:571
  205.2 7.0 %unpack_tiles.1 = (f32[8,296,384]{2,1,0:T(8,128)}, f32[24,272]{1,0:T(8,128)}, f32[24,272]{1,0:T(8,128)}, f32[24,272]{1,0:T(8,128)}, f32[24,272]{1,0:T(8,128)}) custom-call(f32[16,2,8,8192]{3,2,1,0:T(8,128)} %all-to-all-done.arrived), custom_call_target="tpu_custom_call" | custom-call | tf_op jit(solution)/shard_map/unpack_tiles/pallas_call | solution.py:483
  212.3 3.8 %collective-permute-start.5 = (f32[24,272]{1,0:T(8,128)}, f32[24,272]{1,0:T(8,128)S(1)}, u32[]{:S(2)}, u32[]{:S(2)}) collective-permute-start(f32[24,272]{1,0:T(8,128)} %get-tuple-element.34), channel_id=1, source_target_pairs={{1,0},{2,1},{3,2},{4,3},{5,4},{6,5},{7,6},{8,7},{9,8},{10,9},{11,1... | collective-permute-start | bytes 78344 | tf_op jit(solution)/shard_map/ppermute | solution.py:554
  216.4 1.6 collective-permute-done.4.west
  218.7 1.5 row_strips.3
  220.2 4.2 %collective-permute-start.6 = (f32[24,384]{1,0:T(8,128)}, f32[24,384]{1,0:T(8,128)S(1)}, u32[]{:S(2)}, u32[]{:S(2)}) collective-permute-start(f32[24,384]{1,0:T(8,128)} %get-tuple-element.37), channel_id=1, source_target_pairs={{0,16},{16,32},{32,48},{48,64},{64,80},{80,96},{96,112},{1,17},{17... | collective-permute-start | bytes 110600 | tf_op jit(solution)/shard_map/ppermute | solution.py:554
  224.4 1.9 collective-permute-start.7
  226.4 0.7 reshape.14
  227.1 7.0 %collective-permute-done.7.north = f32[24,384]{1,0:T(8,128)S(1)} collective-permute-done((f32[24,384]{1,0:T(8,128)}, f32[24,384]{1,0:T(8,128)S(1)}, u32[]{:S(2)}, u32[]{:S(2)}) %collective-permute-start.7) | collective-permute-done | bytes 36896 | tf_op jit(solution)/shard_map/ppermute | solution.py:554
  234.7 19.9 %forward_window.1 = f32[2,4,270,270]{3,2,1,0:T(8,128)} custom-call(f32[8,296,384]{2,1,0:T(8,128)} %get-tuple-element.25.state, f32[8,296,384]{2,1,0:T(8,128)} %get-tuple-element.32.coef, f32[24,272]{1,0:T(8,128)} %copy-done.2, f32[24,272]{1,0:T(8,128)} %copy-done.3, f32[24,384]{1,0:T(8,128)} %copy-done.6, f32[24,384]{1,0:T(8,128)} %copy-done.7), custom_call_target="tpu_custom_call" | custom-call | tf_op jit(solution)/shard_map/forward_window/pallas_call | solution.py:536
  254.6 4.9 %copy.25 = f32[2,4,270,270]{3,1,2,0:T(4,128)} copy(f32[2,4,270,270]{3,2,1,0:T(8,128)} %forward_window.1) | data formatting | bytes 4665600
  (29 shorter events, 3.4 us)
Async XLA Ops:
  11.5 7.9 %collective-permute-start = (f32[48,272]{1,0:T(8,128)}, f32[48,272]{1,0:T(8,128)S(1)}, u32[]{:S(2)}, u32[]{:S(2)}) collective-permute-start(f32[48,272]{1,0:T(8,128)} %get-tuple-element.23), channel_id=1, source_target_pairs={{0,1},{1,2},{2,3},{3,4},{4,5},{5,6},{6,7},{7,8},{8,9},{9,10},{10,1... | collective-permute-start | bytes 156680 | tf_op jit(solution)/shard_map/ppermute | solution.py:554
  11.5 7.9 %collective-permute-start.1 = (f32[48,272]{1,0:T(8,128)}, f32[48,272]{1,0:T(8,128)S(1)}, u32[]{:S(2)}, u32[]{:S(2)}) collective-permute-start(f32[48,272]{1,0:T(8,128)} %get-tuple-element.22.after), channel_id=1, source_target_pairs={{1,0},{2,1},{3,2},{4,3},{5,4},{6,5},{7,6},{8,7},{9,8},{10,9},{11,1... | collective-permute-start | bytes 156680 | tf_op jit(solution)/shard_map/ppermute | solution.py:554
  19.4 0.6 copy-start
  19.4 0.6 copy-start.1
  21.8 7.8 %collective-permute-start.2 = (f32[48,384]{1,0:T(8,128)}, f32[48,384]{1,0:T(8,128)S(1)}, u32[]{:S(2)}, u32[]{:S(2)}) collective-permute-start(f32[48,384]{1,0:T(8,128)} %get-tuple-element.30), channel_id=1, source_target_pairs={{0,16},{16,32},{32,48},{48,64},{64,80},{80,96},{96,112},{1,17},{17... | collective-permute-start | bytes 221192 | tf_op jit(solution)/shard_map/ppermute | solution.py:554
  27.3 10.1 %collective-permute-start.3 = (f32[48,384]{1,0:T(8,128)}, f32[48,384]{1,0:T(8,128)S(1)}, u32[]{:S(2)}, u32[]{:S(2)}) collective-permute-start(f32[48,384]{1,0:T(8,128)} %get-tuple-element.31), channel_id=1, source_target_pairs={{16,0},{32,16},{48,32},{64,48},{80,64},{96,80},{112,96},{17,1},{33... | collective-permute-start | bytes 221192 | tf_op jit(solution)/shard_map/ppermute | solution.py:554
  29.6 7.8 %copy-start.4 = (f32[48,384]{1,0:T(8,128)}, f32[48,384]{1,0:T(8,128)S(1)}, u32[]{:S(2)}) copy-start(f32[48,384]{1,0:T(8,128)S(1)} %collective-permute-done.2.south) | copy-start | bytes 221188
  37.4 0.6 copy-start.5
  87.7 117.5 %all-to-all-start = ((f32[16,2,8,8192]{3,2,1,0:T(8,128)}), f32[16,2,8,8192]{3,2,1,0:T(8,128)}, u32[]{:S(2)}, u32[]{:S(2)}) async-start(f32[16,2,8,8192]{3,2,1,0:T(8,128)} %pack_tiles.1), calls=%async_computation | async-start | bytes 16777216 | tf_op jit(solution)/shard_map/all_to_all | solution.py:571
  212.2 5.8 %collective-permute-start.4 = (f32[24,272]{1,0:T(8,128)}, f32[24,272]{1,0:T(8,128)S(1)}, u32[]{:S(2)}, u32[]{:S(2)}) collective-permute-start(f32[24,272]{1,0:T(8,128)} %get-tuple-element.33), channel_id=1, source_target_pairs={{0,1},{1,2},{2,3},{3,4},{4,5},{5,6},{6,7},{7,8},{8,9},{9,10},{10,1... | collective-permute-start | bytes 78344 | tf_op jit(solution)/shard_map/ppermute | solution.py:554
  212.3 5.8 %collective-permute-start.5 = (f32[24,272]{1,0:T(8,128)}, f32[24,272]{1,0:T(8,128)S(1)}, u32[]{:S(2)}, u32[]{:S(2)}) collective-permute-start(f32[24,272]{1,0:T(8,128)} %get-tuple-element.34), channel_id=1, source_target_pairs={{1,0},{2,1},{3,2},{4,3},{5,4},{6,5},{7,6},{8,7},{9,8},{10,9},{11,1... | collective-permute-start | bytes 78344 | tf_op jit(solution)/shard_map/ppermute | solution.py:554
  218.0 0.6 copy-start.2
  218.1 0.6 copy-start.3
  220.2 6.8 %collective-permute-start.6 = (f32[24,384]{1,0:T(8,128)}, f32[24,384]{1,0:T(8,128)S(1)}, u32[]{:S(2)}, u32[]{:S(2)}) collective-permute-start(f32[24,384]{1,0:T(8,128)} %get-tuple-element.37), channel_id=1, source_target_pairs={{0,16},{16,32},{32,48},{48,64},{64,80},{80,96},{96,112},{1,17},{17... | collective-permute-start | bytes 110600 | tf_op jit(solution)/shard_map/ppermute | solution.py:554
  224.4 9.7 %collective-permute-start.7 = (f32[24,384]{1,0:T(8,128)}, f32[24,384]{1,0:T(8,128)S(1)}, u32[]{:S(2)}, u32[]{:S(2)}) collective-permute-start(f32[24,384]{1,0:T(8,128)} %get-tuple-element.38), channel_id=1, source_target_pairs={{16,0},{32,16},{48,32},{64,48},{80,64},{96,80},{112,96},{17,1},{33... | collective-permute-start | bytes 110600 | tf_op jit(solution)/shard_map/ppermute | solution.py:554
  227.1 7.0 %copy-start.6 = (f32[24,384]{1,0:T(8,128)}, f32[24,384]{1,0:T(8,128)S(1)}, u32[]{:S(2)}) copy-start(f32[24,384]{1,0:T(8,128)S(1)} %collective-permute-done.6.south) | copy-start | bytes 110596
  234.1 0.6 copy-start.7

commit v2 on v1

--- a/solution.py
+++ b/solution.py
@@ -5,13 +5,13 @@
 from jax.experimental.pallas import tpu as pltpu
 from jax.sharding import PartitionSpec as P
 
+
 F32 = jnp.float32
 I32 = jnp.int32
 TILE = 90
 SIDE = 3
 COLUMNS = 48
 HALO = 3
-STEPS = 3
 SLOTS = 27
 PAIR = 2
 LEV = 4
@@ -155,34 +155,46 @@
 
 def edges_kernel(wet, zd, zf, md, mf, vm, forcing, adjoint, west, east, south, north, held):
     views = [zd, zf, md, mf, vm]
-
-    def plane(f):
-        if f < 6:
-            return views[f - 1]
-        if f < 8:
-            return forcing.at[f - 6]
-        return adjoint.at[(f - 8) // LEV, (f - 8) % LEV]
-
     full = wet_field(wet, N + 2, 0)
-    held[0] = full[:, 0:128]
-    held[1] = full[:, 256:384]
+    held[0, 0] = full[:, 0:128]
+    held[1, 0] = full[:, 256:384]
     south[0:HALO, 0:N] = full[0:HALO, 0:N]
     north[0:HALO, 0:N] = full[N - HALO : N, 0:N]
-    for f in range(1, 16):
-        ref = plane(f)
+    for f in range(1, 6):
+        ref = views[f - 1]
         south[HALO * f : HALO * f + HALO, 0:N] = ref[0:HALO, :]
         north[HALO * f : HALO * f + HALO, 0:N] = ref[N - HALO : N, :]
+        held[0, f, 0:N, :] = ref[:, 0:128]
+        held[1, f, 0:N, 0 : N - 256] = ref[:, 256:N]
+    for out, first in ((south, 0), (north, N - HALO)):
+        for y in range(HALO):
+            row = forcing[first + y]
+            for f in range(2):
+                out[HALO * (6 + f) + y, 0:N] = row[f]
+            for t in range(2):
+                row = adjoint[t, first + y]
+                for k in range(LEV):
+                    out[HALO * (8 + LEV * t + k) + y, 0:N] = row[k]
+
+    def lines(at, start):
+        for side, width in ((0, 128), (1, N - 256)):
+            lanes = slice(256 * side, 256 * side + width)
+            for base, ref, depth in ((6, forcing, 2), (8, adjoint.at[0], LEV), (8 + LEV, adjoint.at[1], LEV)):
+                block = jnp.swapaxes(ref[pl.ds(start, 8), :, lanes], 0, 1)
+                for k in range(depth):
+                    held[side, base + k, at, 0:width] = block[k]
+
+    @pl.loop(0, N // 8)
+    def _(g):
+        lines(pl.ds(aligned(8 * g), 8), 8 * g)
+
+    lines(slice(N - 8, N), N - 8)
 
     def low(f):
-        if f == 0:
-            return held[0]
-        return jnp.concatenate([plane(f)[:, 0:128], jnp.zeros((2, 128), F32)], axis=0)
+        return held[0, f]
 
     def high(f):
-        if f == 0:
-            return held[1]
-        part = jnp.concatenate([plane(f)[:, 256:N], jnp.zeros((N, LANES - N), F32)], axis=1)
-        return jnp.concatenate([part, jnp.zeros((2, 128), F32)], axis=0)
+        return held[1, f]
 
     west[...] = strip_columns(low, 16, 0)
     east[...] = strip_columns(high, 16, N - HALO - 256)
@@ -196,7 +208,7 @@
         out_shape=(columns, columns, rows, rows),
         in_specs=[SMEM] + [VMEM] * 7,
         out_specs=(VMEM,) * 4,
-        scratch_shapes=[pltpu.VMEM((2, N + 2, 128), F32)],
+        scratch_shapes=[pltpu.VMEM((2, 16, N + 2, 128), F32)],
         name="edge_strips",
     )(wet, zd, zf, md, mf, vm, forcing, adjoint)
 
@@ -271,21 +283,33 @@
     return result
 
 
+def store_levels(out, values, i, rows):
+    for t in range(2):
+        block = jnp.swapaxes(jnp.stack(values[LEV * t : LEV * t + LEV]), 0, 1)
+        out[t, pl.ds(8 * i, rows)] = block[0:rows, :, 0:N]
+
+
 def adjoint_kernel(
     wet, labels, zd, zf, md, mf, vm, forcing, adjoint, west, east, south, north,
-    initial, forward_coef, control,
+    initial, forward_coef, keep, give,
     ext, other, coef, surface, coarse, piece,
 ):
     views = [zd, zf, md, mf, vm]
     ext[0, TOP : TOP + N + 2, :] = wet_field(wet, N + 2, 0)
-    for f in range(1, 16):
-        if f < 6:
-            value = views[f - 1]
-        elif f < 8:
-            value = forcing.at[f - 6]
-        else:
-            value = adjoint.at[(f - 8) // LEV, (f - 8) % LEV]
-        ext[f, TOP : TOP + N, 0:N] = value[...]
+    for f in range(1, 6):
+        ext[f, TOP : TOP + N, 0:N] = views[f - 1][...]
+
+    def lines(at, start):
+        for base, ref, depth in ((6, forcing, 2), (8, adjoint.at[0], LEV), (8 + LEV, adjoint.at[1], LEV)):
+            block = jnp.swapaxes(ref[pl.ds(start, 8)], 0, 1)
+            for k in range(depth):
+                ext[base + k, at, 0:N] = block[k]
+
+    @pl.loop(0, N // 8)
+    def _(g):
+        lines(pl.ds(aligned(TOP + 8 * g), 8), 8 * g)
+
+    lines(slice(TOP + N - 8, TOP + N), N - 8)
     insert_halos(ext, 0, 16, west, east, south, north)
 
     def coefficients(r, carry):
@@ -341,14 +365,10 @@
     def finish(i, rows):
         b = aligned(TOP + 8 * i)
         w = ext[0, pl.ds(b, 8), :]
-        for f, (old, new) in enumerate(stencil(lam, b, load_coef(b))):
-            t, k = f // LEV, f % LEV
-            if rows == 8:
-                initial[t, k, pl.ds(aligned(8 * i), 8), :] = (w * new)[:, 0:N]
-            else:
-                initial[t, k, 8 * i : 8 * i + rows, :] = (w * new)[0:rows, 0:N]
-            if k == 0:
-                surface[t, pl.ds(b, 8), :] = w * (surface[t, pl.ds(b, 8), :] + old)
+        values = stencil(lam, b, load_coef(b))
+        store_levels(initial, [w * new for _, new in values], i, rows)
+        for t in range(2):
+            surface[t, pl.ds(b, 8), :] = w * (surface[t, pl.ds(b, 8), :] + values[LEV * t][0])
 
     @pl.loop(0, N // 8)
     def _(i):
@@ -378,7 +398,10 @@
         half = sum(jnp.dot(by_row, p, preferred_element_type=F32) for p in parts(cells))
         full = sum(jnp.dot(p, by_lane, preferred_element_type=F32) for p in parts(half))
         coarse[t] = full / 9.0
-    control[...] = jnp.zeros(control.shape, F32)
+    owners = keep.shape[0] // 4
+    here = lax.axis_index("lat")
+    keep[...] = jnp.zeros(keep.shape, F32)
+    give[...] = jnp.zeros(give.shape, F32)
     piece[...] = jnp.zeros((16, 128), F32)
     part = COARSE // 2
     for r in range(SIDE):
@@ -390,19 +413,31 @@
                     piece[0:part, lane : lane + COARSE] = coarse[
                         t, at : at + part, COARSE * c : COARSE * c + COARSE
                     ]
-            control[labels[r, c]] = piece[...]
+            label = labels[r, c]
+            row = label // owners
+            away = row ^ here
+            at = ((away & 1) * 2 + (away >> 2)) * owners + label - row * owners
+
+            @pl.when((away & 2) == 0)
+            def _():
+                keep[at] = piece[...]
+
+            @pl.when((away & 2) != 0)
+            def _():
+                give[at] = piece[...]
 
 
 def adjoint_window(wet, labels, zd, zf, md, mf, vm, forcing, adjoint, west, east, south, north, owners):
     return pl.pallas_call(
         adjoint_kernel,
         out_shape=(
-            jax.ShapeDtypeStruct((2, LEV, N, N), F32),
+            jax.ShapeDtypeStruct((2, N, LEV, N), F32),
             jax.ShapeDtypeStruct((8, ROWS, LANES), F32),
-            jax.ShapeDtypeStruct((owners, 16, 128), F32),
+            jax.ShapeDtypeStruct((4 * owners, 16, 128), F32),
+            jax.ShapeDtypeStruct((4 * owners, 16, 128), F32),
         ),
         in_specs=[SMEM, SMEM] + [VMEM] * 11,
-        out_specs=(VMEM,) * 3,
+        out_specs=(VMEM,) * 4,
         scratch_shapes=[
             pltpu.VMEM((16, ROWS, LANES), F32),
             pltpu.VMEM((8, ROWS, LANES), F32),
@@ -524,18 +559,15 @@
 
     @pl.loop(0, N // 8)
     def _(i):
-        for f, new in enumerate(advanced(first, aligned(TOP + 8 * i))):
-            final[f // LEV, f % LEV, pl.ds(aligned(8 * i), 8), :] = new[:, 0:N]
-
-    i = N // 8
-    for f, new in enumerate(advanced(first, TOP + 8 * i)):
-        final[f // LEV, f % LEV, 8 * i : N, :] = new[0 : N % 8, 0:N]
+        store_levels(final, advanced(first, aligned(TOP + 8 * i)), i, 8)
+
+    store_levels(final, advanced(first, TOP + N // 8 * 8), N // 8, N % 8)
 
 
 def forward_window(state, coef, west, east, south, north):
     return pl.pallas_call(
         forward_kernel,
-        out_shape=jax.ShapeDtypeStruct((2, LEV, N, N), F32),
+        out_shape=jax.ShapeDtypeStruct((2, N, LEV, N), F32),
         in_specs=[ANY] + [VMEM] * 5,
         out_specs=VMEM,
         scratch_shapes=[
@@ -559,10 +591,9 @@
     zonal_flow, meridional_flow, vertical_mixing, forcing, final_adjoint,
 ):
     owners = lax.axis_size("lon")
-    devices = lax.axis_size(("lat", "lon"))
     fields = (
         zonal_diffusivity, zonal_flow, meridional_diffusivity, meridional_flow, vertical_mixing,
-        forcing, final_adjoint,
+        forcing.transpose(1, 0, 2), final_adjoint.transpose(0, 2, 1, 3),
     )
     low, high, bottom, top = edge_strips(wet_tiles, *fields)
     west, east = neighbours(low, high, "lon", True)
@@ -570,10 +601,15 @@
     outgoing, west, east = lax.optimization_barrier((outgoing, west, east))
     arrived = lax.all_to_all(outgoing, "lon", split_axis=0, concat_axis=0, tiled=True)
     south, north = neighbours(*with_corners(bottom, top, west, east), "lat", False)
-    initial, coef, pieces = adjoint_window(
-        wet_tiles, control_map, *fields, west, east, south, north, devices
+    initial, coef, keep, give = adjoint_window(
+        wet_tiles, control_map, *fields, west, east, south, north, owners
     )
-    gathered = lax.all_to_all(pieces, ("lat", "lon"), split_axis=0, concat_axis=0, tiled=True)
+    for bit in (2, 1, 4):
+        keep = keep + lax.ppermute(give, "lat", [(i, i ^ bit) for i in range(lax.axis_size("lat"))])
+        half = keep.shape[0] // 2
+        if bit != 4:
+            keep, give = keep[:half], keep[half:]
+    gathered = lax.all_to_all(keep, "lon", split_axis=0, concat_axis=0, tiled=True)
     total = jnp.sum(gathered, axis=0)[: COARSE // 2]
     total = jnp.stack([total[:, :60], total[:, 64:124]]).reshape(2, COARSE // 2, 2, COARSE)
     control = total.transpose(2, 0, 1, 3).reshape(1, 2, COARSE * COARSE)
@@ -582,7 +618,7 @@
     west, east = neighbours(low, high, "lon", True)
     south, north = neighbours(*with_corners(bottom, top, west, east), "lat", False)
     final = forward_window(state, coef, west, east, south, north)
-    return final, initial, control
+    return final.transpose(0, 2, 1, 3), initial.transpose(0, 2, 1, 3), control
 
 
 def solution(mesh):

time: 261 us -> 268 us (1.027)
  the two profiles are of different devices: /device:TPU:24 before, /device:TPU:96 now
where the time goes in v2:
time: 268 us; the launch traced here: 263 us
  waiting for transfers between devices  144 us (54%)
  Pallas kernels  68.8 us (26%)
  starting transfers between devices  36.4 us (14%)
  blocking collectives  8.23 us (3%)
  local copies, waits for them, and re-layouts  3.45 us (1%)
    all_to_all x1, waiting for transfers between devices, per_device(): lax.all_to_all(outgoing, 'lon', split_axis=0, concat_axis=0, tiled=True)  112 us
    pallas_call x1, Pallas kernels, adjoint_window(): pl.pallas_call(adjoint_kernel, out_shape=(jax.ShapeDtypeStruct((2, N, LEV...  29 us
    ppermute x8, starting transfers between devices, neighbours(): return (lax.ppermute(high, axis, up), lax.ppermute(low, axis, down))  27 us
    ppermute x3, waiting for transfers between devices, per_device(): lax.ppermute(give, 'lat', [(i, i ^ bit) for i in range(lax.axis_size('lat...  26.4 us
    pallas_call x1, Pallas kernels, forward_window(): pl.pallas_call(forward_kernel, out_shape=jax.ShapeDtypeStruct((2, N, LEV,...  20.4 us
    all_to_all x1, blocking collectives, per_device(): lax.all_to_all(keep, 'lon', split_axis=0, concat_axis=0, tiled=True)  8.23 us
    pallas_call x1, Pallas kernels, unpack_tiles(): pl.pallas_call(unpack_kernel, out_shape=(jax.ShapeDtypeStruct((8, ROWS, L...  6.89 us
    all_to_all x1, starting transfers between devices, per_device(): lax.all_to_all(outgoing, 'lon', split_axis=0, concat_axis=0, tiled=True)  6.06 us
  transfers between devices with their start and end apart: 12, of which 9 were waited for; matrix products, arithmetic and copies ran while one was open for 0% of the time, Pallas kernels for 1%

profile of v2, /device:TPU:96, one launch (start us, length us, event | category | flops | bytes accessed | tf_op | source)
XLA Modules:
  0.0 263.3 jit_solution(16666224135905031167)
XLA Ops:
  0.6 5.6 %edge_strips.1 = (f32[48,272]{1,0:T(8,128)}, f32[48,272]{1,0:T(8,128)}, f32[48,272]{1,0:T(8,128)}, f32[48,272]{1,0:T(8,128)}) custom-call(s32[3,3]{1,0:T(4,128)} %wet.3, f32[270,270]{1,0:T(8,128)} %zd.3, f32[270,270]{1,0:T(8,128)} %zf.3, f32[270,270]{1,0:T(8,128)} %md.3, f32[270,270]{1,0:T(8,128)} %mf.3, f32[270,270]{1,0:T(8,128)} %vm.3, ...), custom_call_target="tpu_custom_call" | custom-call | tf_op jit(solution)/shard_map/edge_strips/pallas_call | solution.py:206
  6.2 3.9 %collective-permute-start.1 = (f32[48,272]{1,0:T(8,128)}, f32[48,272]{1,0:T(8,128)S(1)}, u32[]{:S(2)}, u32[]{:S(2)}) collective-permute-start(f32[48,272]{1,0:T(8,128)} %get-tuple-element.23.after), channel_id=1, source_target_pairs={{1,0},{2,1},{3,2},{4,3},{5,4},{6,5},{7,6},{8,7},{9,8},{10,9},{11,1... | collective-permute-start | bytes 156680 | tf_op jit(solution)/shard_map/ppermute | solution.py:586
  10.1 3.7 %pack_tiles.1 = f32[16,2,8,8192]{3,2,1,0:T(8,128)} custom-call(s32[27]{0:T(128)} %ids.1, f32[27,8,8100]{2,1,0:T(8,128)} %stored.1, f32[48,272]{1,0:T(8,128)} %get-tuple-element.23.after), custom_call_target="tpu_custom_call" | custom-call | tf_op jit(solution)/shard_map/pack_tiles/pallas_call | solution.py:117
  14.5 1.7 row_strips.2
  16.2 4.1 %collective-permute-start.2 = (f32[48,384]{1,0:T(8,128)}, f32[48,384]{1,0:T(8,128)S(1)}, u32[]{:S(2)}, u32[]{:S(2)}) collective-permute-start(f32[48,384]{1,0:T(8,128)} %get-tuple-element.31), channel_id=1, source_target_pairs={{0,16},{16,32},{32,48},{48,64},{64,80},{80,96},{96,112},{1,17},{17... | collective-permute-start | bytes 221192 | tf_op jit(solution)/shard_map/ppermute | solution.py:586
  20.3 5.4 %collective-permute-start.3 = (f32[48,384]{1,0:T(8,128)}, f32[48,384]{1,0:T(8,128)S(1)}, u32[]{:S(2)}, u32[]{:S(2)}) collective-permute-start(f32[48,384]{1,0:T(8,128)} %get-tuple-element.32), channel_id=1, source_target_pairs={{16,0},{32,16},{48,32},{64,48},{80,64},{96,80},{112,96},{17,1},{33... | collective-permute-start | bytes 221192 | tf_op jit(solution)/shard_map/ppermute | solution.py:586
  26.8 1.8 collective-permute-done.3.north
  29.3 29.0 %adjoint_window.1 = (f32[2,270,4,270]{3,2,1,0:T(4,128)}, f32[8,296,384]{2,1,0:T(8,128)}, f32[64,16,128]{2,1,0:T(8,128)}, f32[64,16,128]{2,1,0:T(8,128)}) custom-call(s32[3,3]{1,0:T(4,128)} %wet.3, s32[3,3]{1,0:T(4,128)} %labels.1, f32[270,270]{1,0:T(8,128)} %zd.3, f32[270,270]{1,0:T(8,128)} %zf.3, f32[270,270]{1,0:T(8,128)} %md.3, f32[270,270]{1,0:T(8,128)} %mf.3, ...), custom_call_target="tpu_custom_call" | custom-call | tf_op jit(solution)/shard_map/adjoint_window/pallas_call | solution.py:431
  58.7 15.2 %collective-permute-done.8 = f32[64,16,128]{2,1,0:T(8,128)S(1)} collective-permute-done((f32[64,16,128]{2,1,0:T(8,128)}, f32[64,16,128]{2,1,0:T(8,128)S(1)}, u32[]{:S(2)}, u32[]{:S(2)}) %collective-permute-start.8) | collective-permute-done | bytes 524320 | tf_op jit(solution)/shard_map/ppermute | solution.py:608
  73.9 1.1 add.9
  75.1 7.5 %collective-permute-done.9 = f32[32,16,128]{2,1,0:T(8,128)S(1)} collective-permute-done((f32[32,16,128]{2,1,0:T(8,128)S(1)}, f32[32,16,128]{2,1,0:T(8,128)S(1)}, u32[]{:S(2)}, u32[]{:S(2)}) %collective-permute-start.9) | collective-permute-done | bytes 262176 | tf_op jit(solution)/shard_map/ppermute | solution.py:608
  82.7 2.8 %collective-permute-start.10 = (f32[16,16,128]{2,1,0:T(8,128)S(1)}, f32[16,16,128]{2,1,0:T(8,128)S(1)}, u32[]{:S(2)}, u32[]{:S(2)}) collective-permute-start(f32[16,16,128]{2,1,0:T(8,128)S(1)} %slice.30), channel_id=1, source_target_pairs={{0,64},{16,80},{32,96},{48,112},{64,0},{80,16},{96,32},{112,48},{1... | collective-permute-start | bytes 393224 | tf_op jit(solution)/shard_map/ppermute | solution.py:608
  85.4 3.8 %collective-permute-done.10 = f32[16,16,128]{2,1,0:T(8,128)S(1)} collective-permute-done((f32[16,16,128]{2,1,0:T(8,128)S(1)}, f32[16,16,128]{2,1,0:T(8,128)S(1)}, u32[]{:S(2)}, u32[]{:S(2)}) %collective-permute-start.10) | collective-permute-done | bytes 131104 | tf_op jit(solution)/shard_map/ppermute | solution.py:608
  89.2 8.2 %all_to_all.10 = f32[16,16,128]{2,1,0:T(8,128)S(1)} all-to-all(f32[16,16,128]{2,1,0:T(8,128)S(1)} %slice_add_fusion.1), channel_id=1, replica_groups=mesh['lat'=8,'lon'=16] {'lon'}, dimensions={0} | all-to-all | bytes 262144 | tf_op jit(solution)/shard_map/all_to_all | solution.py:612
  97.5 6.1 %all-to-all-start = ((f32[16,2,8,8192]{3,2,1,0:T(8,128)}), f32[16,2,8,8192]{3,2,1,0:T(8,128)}, u32[]{:S(2)}, u32[]{:S(2)}) async-start(f32[16,2,8,8192]{3,2,1,0:T(8,128)} %pack_tiles.1), calls=%async_computation | async-start | bytes 16777216 | tf_op jit(solution)/shard_map/all_to_all | solution.py:602
  103.5 112.1 %all-to-all-done.arrived = f32[16,2,8,8192]{3,2,1,0:T(8,128)} async-done(((f32[16,2,8,8192]{3,2,1,0:T(8,128)}), f32[16,2,8,8192]{3,2,1,0:T(8,128)}, u32[]{:S(2)}, u32[]{:S(2)}) %all-to-all-start) | async-done | bytes 8388640 | tf_op jit(solution)/shard_map/all_to_all | solution.py:602
  215.6 6.9 %unpack_tiles.1 = (f32[8,296,384]{2,1,0:T(8,128)}, f32[24,272]{1,0:T(8,128)}, f32[24,272]{1,0:T(8,128)}, f32[24,272]{1,0:T(8,128)}, f32[24,272]{1,0:T(8,128)}) custom-call(f32[16,2,8,8192]{3,2,1,0:T(8,128)} %all-to-all-done.arrived), custom_call_target="tpu_custom_call" | custom-call | tf_op jit(solution)/shard_map/unpack_tiles/pallas_call | solution.py:518
  222.6 3.8 %collective-permute-start.5 = (f32[24,272]{1,0:T(8,128)}, f32[24,272]{1,0:T(8,128)S(1)}, u32[]{:S(2)}, u32[]{:S(2)}) collective-permute-start(f32[24,272]{1,0:T(8,128)} %get-tuple-element.35), channel_id=1, source_target_pairs={{1,0},{2,1},{3,2},{4,3},{5,4},{6,5},{7,6},{8,7},{9,8},{10,9},{11,1... | collective-permute-start | bytes 78344 | tf_op jit(solution)/shard_map/ppermute | solution.py:586
  226.7 1.6 collective-permute-done.4.west
  229.0 1.5 row_strips.3
  230.5 2.8 %collective-permute-start.6 = (f32[24,384]{1,0:T(8,128)}, f32[24,384]{1,0:T(8,128)S(1)}, u32[]{:S(2)}, u32[]{:S(2)}) collective-permute-start(f32[24,384]{1,0:T(8,128)} %get-tuple-element.38), channel_id=1, source_target_pairs={{0,16},{16,32},{32,48},{48,64},{64,80},{80,96},{96,112},{1,17},{17... | collective-permute-start | bytes 110600 | tf_op jit(solution)/shard_map/ppermute | solution.py:586
  233.3 7.0 %collective-permute-start.7 = (f32[24,384]{1,0:T(8,128)}, f32[24,384]{1,0:T(8,128)S(1)}, u32[]{:S(2)}, u32[]{:S(2)}) collective-permute-start(f32[24,384]{1,0:T(8,128)} %get-tuple-element.39), channel_id=1, source_target_pairs={{16,0},{32,16},{48,32},{64,48},{80,64},{96,80},{112,96},{17,1},{33... | collective-permute-start | bytes 110600 | tf_op jit(solution)/shard_map/ppermute | solution.py:586
  241.1 1.2 collective-permute-done.7.north
  242.9 20.4 %forward_window.1 = f32[2,270,4,270]{3,2,1,0:T(4,128)} custom-call(f32[8,296,384]{2,1,0:T(8,128)} %get-tuple-element.26.state, f32[8,296,384]{2,1,0:T(8,128)} %get-tuple-element.33.coef, f32[24,272]{1,0:T(8,128)} %copy-done.2, f32[24,272]{1,0:T(8,128)} %copy-done.3, f32[24,384]{1,0:T(8,128)} %copy-done.6, f32[24,384]{1,0:T(8,128)} %copy-done.7), custom_call_target="tpu_custom_call" | custom-call | tf_op jit(solution)/shard_map/forward_window/pallas_call | solution.py:568
  (36 shorter events, 5.4 us)
Async XLA Ops:
  6.2 7.6 %collective-permute-start = (f32[48,272]{1,0:T(8,128)}, f32[48,272]{1,0:T(8,128)S(1)}, u32[]{:S(2)}, u32[]{:S(2)}) collective-permute-start(f32[48,272]{1,0:T(8,128)} %get-tuple-element.24), channel_id=1, source_target_pairs={{0,1},{1,2},{2,3},{3,4},{4,5},{5,6},{6,7},{7,8},{8,9},{9,10},{10,1... | collective-permute-start | bytes 156680 | tf_op jit(solution)/shard_map/ppermute | solution.py:586
  6.2 7.6 %collective-permute-start.1 = (f32[48,272]{1,0:T(8,128)}, f32[48,272]{1,0:T(8,128)S(1)}, u32[]{:S(2)}, u32[]{:S(2)}) collective-permute-start(f32[48,272]{1,0:T(8,128)} %get-tuple-element.23.after), channel_id=1, source_target_pairs={{1,0},{2,1},{3,2},{4,3},{5,4},{6,5},{7,6},{8,7},{9,8},{10,9},{11,1... | collective-permute-start | bytes 156680 | tf_op jit(solution)/shard_map/ppermute | solution.py:586
  13.8 0.6 copy-start
  13.9 0.6 copy-start.1
  16.2 10.6 %collective-permute-start.2 = (f32[48,384]{1,0:T(8,128)}, f32[48,384]{1,0:T(8,128)S(1)}, u32[]{:S(2)}, u32[]{:S(2)}) collective-permute-start(f32[48,384]{1,0:T(8,128)} %get-tuple-element.31), channel_id=1, source_target_pairs={{0,16},{16,32},{32,48},{48,64},{64,80},{80,96},{96,112},{1,17},{17... | collective-permute-start | bytes 221192 | tf_op jit(solution)/shard_map/ppermute | solution.py:586
  20.3 8.3 %collective-permute-start.3 = (f32[48,384]{1,0:T(8,128)}, f32[48,384]{1,0:T(8,128)S(1)}, u32[]{:S(2)}, u32[]{:S(2)}) collective-permute-start(f32[48,384]{1,0:T(8,128)} %get-tuple-element.32), channel_id=1, source_target_pairs={{16,0},{32,16},{48,32},{64,48},{80,64},{96,80},{112,96},{17,1},{33... | collective-permute-start | bytes 221192 | tf_op jit(solution)/shard_map/ppermute | solution.py:586
  26.8 1.8 copy-start.4
  28.6 0.6 copy-start.5
  58.2 15.7 %collective-permute-start.8 = (f32[64,16,128]{2,1,0:T(8,128)}, f32[64,16,128]{2,1,0:T(8,128)S(1)}, u32[]{:S(2)}, u32[]{:S(2)}) collective-permute-start(f32[64,16,128]{2,1,0:T(8,128)} %get-tuple-element.42), channel_id=1, source_target_pairs={{0,32},{16,48},{32,0},{48,16},{64,96},{80,112},{96,64},{112,80},{1... | collective-permute-start | bytes 1572872 | tf_op jit(solution)/shard_map/ppermute | solution.py:608
  75.1 7.6 %collective-permute-start.9 = (f32[32,16,128]{2,1,0:T(8,128)S(1)}, f32[32,16,128]{2,1,0:T(8,128)S(1)}, u32[]{:S(2)}, u32[]{:S(2)}) collective-permute-start(f32[32,16,128]{2,1,0:T(8,128)S(1)} %slice.28), channel_id=1, source_target_pairs={{0,16},{16,0},{32,48},{48,32},{64,80},{80,64},{96,112},{112,96},{1... | collective-permute-start | bytes 786440 | tf_op jit(solution)/shard_map/ppermute | solution.py:608
  82.7 6.6 %collective-permute-start.10 = (f32[16,16,128]{2,1,0:T(8,128)S(1)}, f32[16,16,128]{2,1,0:T(8,128)S(1)}, u32[]{:S(2)}, u32[]{:S(2)}) collective-permute-start(f32[16,16,128]{2,1,0:T(8,128)S(1)} %slice.30), channel_id=1, source_target_pairs={{0,64},{16,80},{32,96},{48,112},{64,0},{80,16},{96,32},{112,48},{1... | collective-permute-start | bytes 393224 | tf_op jit(solution)/shard_map/ppermute | solution.py:608
  97.5 118.2 %all-to-all-start = ((f32[16,2,8,8192]{3,2,1,0:T(8,128)}), f32[16,2,8,8192]{3,2,1,0:T(8,128)}, u32[]{:S(2)}, u32[]{:S(2)}) async-start(f32[16,2,8,8192]{3,2,1,0:T(8,128)} %pack_tiles.1), calls=%async_computation | async-start | bytes 16777216 | tf_op jit(solution)/shard_map/all_to_all | solution.py:602
  222.5 5.8 %collective-permute-start.4 = (f32[24,272]{1,0:T(8,128)}, f32[24,272]{1,0:T(8,128)S(1)}, u32[]{:S(2)}, u32[]{:S(2)}) collective-permute-start(f32[24,272]{1,0:T(8,128)} %get-tuple-element.34), channel_id=1, source_target_pairs={{0,1},{1,2},{2,3},{3,4},{4,5},{5,6},{6,7},{7,8},{8,9},{9,10},{10,1... | collective-permute-start | bytes 78344 | tf_op jit(solution)/shard_map/ppermute | solution.py:586
  222.6 5.8 %collective-permute-start.5 = (f32[24,272]{1,0:T(8,128)}, f32[24,272]{1,0:T(8,128)S(1)}, u32[]{:S(2)}, u32[]{:S(2)}) collective-permute-start(f32[24,272]{1,0:T(8,128)} %get-tuple-element.35), channel_id=1, source_target_pairs={{1,0},{2,1},{3,2},{4,3},{5,4},{6,5},{7,6},{8,7},{9,8},{10,9},{11,1... | collective-permute-start | bytes 78344 | tf_op jit(solution)/shard_map/ppermute | solution.py:586
  228.3 0.6 copy-start.2
  228.4 0.6 copy-start.3
  230.5 10.6 %collective-permute-start.6 = (f32[24,384]{1,0:T(8,128)}, f32[24,384]{1,0:T(8,128)S(1)}, u32[]{:S(2)}, u32[]{:S(2)}) collective-permute-start(f32[24,384]{1,0:T(8,128)} %get-tuple-element.38), channel_id=1, source_target_pairs={{0,16},{16,32},{32,48},{48,64},{64,80},{80,96},{96,112},{1,17},{17... | collective-permute-start | bytes 110600 | tf_op jit(solution)/shard_map/ppermute | solution.py:586
  233.3 9.0 %collective-permute-start.7 = (f32[24,384]{1,0:T(8,128)}, f32[24,384]{1,0:T(8,128)S(1)}, u32[]{:S(2)}, u32[]{:S(2)}) collective-permute-start(f32[24,384]{1,0:T(8,128)} %get-tuple-element.39), channel_id=1, source_target_pairs={{16,0},{32,16},{48,32},{64,48},{80,64},{96,80},{112,96},{17,1},{33... | collective-permute-start | bytes 110600 | tf_op jit(solution)/shard_map/ppermute | solution.py:586
  241.1 1.2 copy-start.6
  242.3 0.6 copy-start.7

commit v3 on v2

--- a/solution.py
+++ b/solution.py
@@ -21,8 +21,9 @@
 TAIL = 8064
 TAG = CELLS - TAIL
 TOP = 16
-ROWS = 296
+ROWS = 304
 LANES = 384
+BLOCKS = ((0, 128), (1, 128), (2, N - 256))
 CHUNKS = 34
 COARSE = 30
 VMEM = pl.BlockSpec(memory_space=pltpu.VMEM)
@@ -238,55 +239,56 @@
     blank = jnp.zeros((128 - HALO * count, 128), F32)
     low = jnp.concatenate([south[:, 256:384], blank], axis=0).T
     high = jnp.concatenate([north[:, 256:384], blank], axis=0).T
+    at = N - 256
     for f in range(count):
         s = slice(HALO * f, HALO * f + HALO)
         field = ext.at[base + f]
-        field[TOP : TOP + N + 2, LANES - HALO : LANES] = from_west[:, s]
-        field[TOP : TOP + N + 2, N : N + HALO] = from_east[:, s]
+        field[2, TOP : TOP + N + 2, 128 - HALO : 128] = from_west[:, s]
+        field[2, TOP : TOP + N + 2, at : at + HALO] = from_east[:, s]
         for first, rows, block in ((TOP - HALO, south, low), (TOP + N, north, high)):
-            at = N - 256
-            field[first : first + HALO, 0:N] = rows[s, 0:N]
-            field[first : first + HALO, LANES - HALO : LANES] = block[at : at + HALO, s]
-            field[first : first + HALO, N : N + HALO] = block[at + HALO : at + 2 * HALO, s]
-
-
-def row_mask(k):
-    return lax.broadcasted_iota(I32, (8, LANES), 0) == k
-
-
-def to_south(current, following):
-    return pltpu.roll(jnp.where(row_mask(0), following, current), 7, 0)
-
-
-def to_north(current, previous):
-    return pltpu.roll(jnp.where(row_mask(7), previous, current), 1, 0)
-
-
-def stencil(src, b, coef):
-    center, east, west, north, south, mix = coef
-    result = []
-    for t in range(2):
-        level = [src[t * LEV + k, pl.ds(b, 8), :] for k in range(LEV)]
-        flux = [mix * (level[k] - level[k + 1]) for k in range(LEV - 1)]
-        for k in range(LEV):
-            c = level[k]
-            f = t * LEV + k
-            up = to_south(c, src[f, pl.ds(aligned(b + 8), 8), :])
-            down = to_north(c, src[f, pl.ds(aligned(b - 8), 8), :])
-            new = center * c + east * pltpu.roll(c, LANES - 1, 1) + west * pltpu.roll(c, 1, 1)
-            new = new + (north * up + south * down)
-            if k > 0:
-                new = new + flux[k - 1]
-            if k < LEV - 1:
-                new = new - flux[k]
-            result.append((c, new))
-    return result
-
-
-def store_levels(out, values, i, rows):
-    for t in range(2):
-        block = jnp.swapaxes(jnp.stack(values[LEV * t : LEV * t + LEV]), 0, 1)
-        out[t, pl.ds(8 * i, rows)] = block[0:rows, :, 0:N]
+            for j, width in BLOCKS:
+                field[j, first : first + HALO, 0:width] = rows[s, 128 * j : 128 * j + width]
+            field[2, first : first + HALO, 128 - HALO : 128] = block[at : at + HALO, s]
+            field[2, first : first + HALO, at : at + HALO] = block[at + HALO : at + 2 * HALO, s]
+
+
+def from_east(block):
+    lane = lax.broadcasted_iota(I32, (8, 128), 1)
+    return lambda j: pltpu.roll(jnp.where(lane == 0, block((j + 1) % 3), block(j)), 127, 1)
+
+
+def from_west(block):
+    lane = lax.broadcasted_iota(I32, (8, 128), 1)
+    return lambda j: pltpu.roll(jnp.where(lane == 127, block((j + 2) % 3), block(j)), 1, 1)
+
+
+def stencil(src, b, coef, take):
+    rows = pl.ds(b, 8)
+    for j in range(3):
+        center, east, west, north, south, mix = coef(j)
+        for t in range(2):
+            fields = [src.at[t * LEV + k] for k in range(LEV)]
+            level = [field[j, rows, :] for field in fields]
+            flux = [mix * (level[k] - level[k + 1]) for k in range(LEV - 1)]
+            result = []
+            for k in range(LEV):
+                block = lambda i, field=fields[k]: field[i, rows, :]
+                new = center * level[k] + east * from_east(block)(j) + west * from_west(block)(j)
+                up = fields[k][j, pl.ds(b + 1, 8), :]
+                down = fields[k][j, pl.ds(b - 1, 8), :]
+                new = new + (north * up + south * down)
+                if k > 0:
+                    new = new + flux[k - 1]
+                if k < LEV - 1:
+                    new = new - flux[k]
+                result.append(new)
+            take(t, j, level, result)
+
+
+def store_levels(out, t, j, values, i, rows):
+    width = BLOCKS[j][1]
+    block = jnp.swapaxes(jnp.stack(values), 0, 1)
+    out[t, pl.ds(8 * i, rows), :, 128 * j : 128 * j + width] = block[0:rows, :, 0:width]
 
 
 def adjoint_kernel(
@@ -295,15 +297,18 @@
     ext, other, coef, surface, coarse, piece,
 ):
     views = [zd, zf, md, mf, vm]
-    ext[0, TOP : TOP + N + 2, :] = wet_field(wet, N + 2, 0)
-    for f in range(1, 6):
-        ext[f, TOP : TOP + N, 0:N] = views[f - 1][...]
+    full = wet_field(wet, N + 2, 0)
+    for j, width in BLOCKS:
+        ext[0, j, TOP : TOP + N + 2, :] = full[:, 128 * j : 128 * j + 128]
+        for f in range(1, 6):
+            ext[f, j, TOP : TOP + N, 0:width] = views[f - 1][:, 128 * j : 128 * j + width]
 
     def lines(at, start):
         for base, ref, depth in ((6, forcing, 2), (8, adjoint.at[0], LEV), (8 + LEV, adjoint.at[1], LEV)):
             block = jnp.swapaxes(ref[pl.ds(start, 8)], 0, 1)
             for k in range(depth):
-                ext[base + k, at, 0:N] = block[k]
+                for j, width in BLOCKS:
+                    ext[base + k, j, at, 0:width] = block[k, :, 128 * j : 128 * j + width]
 
     @pl.loop(0, N // 8)
     def _(g):
@@ -312,68 +317,85 @@
     lines(slice(TOP + N - 8, TOP + N), N - 8)
     insert_halos(ext, 0, 16, west, east, south, north)
 
-    def coefficients(r, carry):
-        north_a, north_b = carry
+    @pl.loop(1, CHUNKS + 2)
+    def _(r):
         b = aligned(r * 8)
-        w, z_d, z_f, m_d, m_f, v = [ext[f, pl.ds(b, 8), :] for f in range(6)]
-        east_open = w * pltpu.roll(w, LANES - 1, 1)
-        north_open = w * to_south(w, ext[0, pl.ds(aligned(b + 8), 8), :])
-        de = z_d * east_open
-        ue = 0.5 * z_f * east_open
-        dn = m_d * north_open
-        vn = 0.5 * m_f * north_open
-        ea, eb, na, nb = de + ue, ue - de, dn + vn, vn - dn
-        eb_west = pltpu.roll(eb, 1, 1)
-        nb_south = to_north(nb, north_b)
         rows = pl.ds(b, 8)
-        forward_coef[0, rows, :] = 1.0 + ((eb_west - ea) + (nb_south - na))
-        forward_coef[1, rows, :] = -eb
-        forward_coef[2, rows, :] = pltpu.roll(ea, 1, 1)
-        forward_coef[3, rows, :] = -nb
-        forward_coef[4, rows, :] = to_north(na, north_a)
-        forward_coef[5, rows, :] = v * w
-        forward_coef[6, rows, :] = ext[6, rows, :] * w
-        forward_coef[7, rows, :] = ext[7, rows, :] * w
-        coef[0, rows, :] = ea
-        coef[1, rows, :] = -eb_west
-        coef[2, rows, :] = na
-        coef[3, rows, :] = -nb_south
-        return na, nb
-
-    zero = jnp.zeros((8, LANES), F32)
-    lax.fori_loop(1, CHUNKS + 2, coefficients, (zero, zero))
+        faces = []
+        wets = [ext[0, j, rows, :] for j in range(3)]
+        for j in range(3):
+            w, z_d, z_f, m_d, m_f, v = [ext[f, j, rows, :] for f in range(6)]
+            east_open = w * from_east(wets.__getitem__)(j)
+            north_open = w * ext[0, j, pl.ds(b + 1, 8), :]
+            de = z_d * east_open
+            ue = 0.5 * z_f * east_open
+            dn = m_d * north_open
+            vn = 0.5 * m_f * north_open
+            faces.append((de + ue, ue - de))
+            coef[0, j, rows, :] = de + ue
+            coef[2, j, rows, :] = dn + vn
+            forward_coef[1, j, rows, :] = de - ue
+            forward_coef[3, j, rows, :] = dn - vn
+            forward_coef[5, j, rows, :] = v * w
+            forward_coef[6, j, rows, :] = ext[6, j, rows, :] * w
+            forward_coef[7, j, rows, :] = ext[7, j, rows, :] * w
+        for j in range(3):
+            ea_west = from_west(lambda i: faces[i][0])(j)
+            eb_west = from_west(lambda i: faces[i][1])(j)
+            na_south = coef[2, j, pl.ds(b - 1, 8), :]
+            minus_nb_south = forward_coef[3, j, pl.ds(b - 1, 8), :]
+            forward_coef[0, j, rows, :] = 1.0 + (
+                (eb_west - faces[j][0]) - (minus_nb_south + coef[2, j, rows, :])
+            )
+            forward_coef[2, j, rows, :] = ea_west
+            forward_coef[4, j, rows, :] = na_south
+            coef[1, j, rows, :] = -eb_west
+            coef[3, j, rows, :] = minus_nb_south
 
     def load_coef(b):
         rows = pl.ds(b, 8)
-        return [forward_coef[0, rows, :]] + [coef[i, rows, :] for i in range(4)] + [forward_coef[5, rows, :]]
+        return lambda j: (
+            [forward_coef[0, j, rows, :]]
+            + [coef[i, j, rows, :] for i in range(4)]
+            + [forward_coef[5, j, rows, :]]
+        )
 
     lam = ext.at[pl.ds(8, 8)]
 
     def step(src, dst, first):
-        @pl.loop(1, CHUNKS + 2)
+        @pl.loop(0, CHUNKS // 2 + 1)
         def _(r):
-            b = aligned(r * 8)
-            for f, (old, new) in enumerate(stencil(src, b, load_coef(b))):
-                dst[f, pl.ds(b, 8), :] = new
-                if f % LEV == 0:
-                    t = f // LEV
-                    surface[t, pl.ds(b, 8), :] = old if first else surface[t, pl.ds(b, 8), :] + old
+            for u in range(2):
+                b = aligned(r * 16 + 8 * u + 8)
+                rows = pl.ds(b, 8)
+
+                def take(t, j, old, new):
+                    for k in range(LEV):
+                        dst[t * LEV + k, j, rows, :] = new[k]
+                    surface[t, j, rows, :] = old[0] if first else surface[t, j, rows, :] + old[0]
+
+                stencil(src, b, load_coef(b), take)
 
     step(lam, other, True)
     step(other, lam, False)
 
-    def finish(i, rows):
+    def finish(i, count):
         b = aligned(TOP + 8 * i)
-        w = ext[0, pl.ds(b, 8), :]
-        values = stencil(lam, b, load_coef(b))
-        store_levels(initial, [w * new for _, new in values], i, rows)
-        for t in range(2):
-            surface[t, pl.ds(b, 8), :] = w * (surface[t, pl.ds(b, 8), :] + values[LEV * t][0])
-
-    @pl.loop(0, N // 8)
+        rows = pl.ds(b, 8)
+
+        def take(t, j, old, new):
+            w = ext[0, j, rows, :]
+            store_levels(initial, t, j, [w * value for value in new], i, count)
+            surface[t, j, rows, :] = w * (surface[t, j, rows, :] + old[0])
+
+        stencil(lam, b, load_coef(b), take)
+
+    @pl.loop(0, N // 16)
     def _(i):
-        finish(i, 8)
-
+        finish(2 * i, 8)
+        finish(2 * i + 1, 8)
+
+    finish(N // 8 - 1, 8)
     finish(N // 8, N % 8)
 
     BF = jnp.bfloat16
@@ -391,12 +413,17 @@
 
     by_row = band((96, N + 2), 0)
     by_lane = band((LANES, 128), 1)
-    shape = (N + 2, LANES)
-    inside = (lax.broadcasted_iota(I32, shape, 0) < N) & (lax.broadcasted_iota(I32, shape, 1) < N)
+    shape = (N + 2, 128)
     for t in range(2):
-        cells = jnp.where(inside, surface[t, TOP : TOP + N + 2, :], 0.0)
-        half = sum(jnp.dot(by_row, p, preferred_element_type=F32) for p in parts(cells))
-        full = sum(jnp.dot(p, by_lane, preferred_element_type=F32) for p in parts(half))
+        full = jnp.zeros((96, 128), F32)
+        for j, width in BLOCKS:
+            inside = (lax.broadcasted_iota(I32, shape, 0) < N) & (
+                lax.broadcasted_iota(I32, shape, 1) < width
+            )
+            cells = jnp.where(inside, surface[t, j, TOP : TOP + N + 2, :], 0.0)
+            half = sum(jnp.dot(by_row, p, preferred_element_type=F32) for p in parts(cells))
+            for p in parts(half):
+                full += jnp.dot(p, by_lane[128 * j : 128 * j + 128], preferred_element_type=F32)
         coarse[t] = full / 9.0
     owners = keep.shape[0] // 4
     here = lax.axis_index("lat")
@@ -432,17 +459,17 @@
         adjoint_kernel,
         out_shape=(
             jax.ShapeDtypeStruct((2, N, LEV, N), F32),
-            jax.ShapeDtypeStruct((8, ROWS, LANES), F32),
+            jax.ShapeDtypeStruct((8, 3, ROWS, 128), F32),
             jax.ShapeDtypeStruct((4 * owners, 16, 128), F32),
             jax.ShapeDtypeStruct((4 * owners, 16, 128), F32),
         ),
         in_specs=[SMEM, SMEM] + [VMEM] * 11,
         out_specs=(VMEM,) * 4,
         scratch_shapes=[
-            pltpu.VMEM((16, ROWS, LANES), F32),
-            pltpu.VMEM((8, ROWS, LANES), F32),
-            pltpu.VMEM((4, ROWS, LANES), F32),
-            pltpu.VMEM((2, ROWS, LANES), F32),
+            pltpu.VMEM((16, 3, ROWS, 128), F32),
+            pltpu.VMEM((8, 3, ROWS, 128), F32),
+            pltpu.VMEM((4, 3, ROWS, 128), F32),
+            pltpu.VMEM((2, 3, ROWS, 128), F32),
             pltpu.VMEM((2, 96, 128), F32),
             pltpu.VMEM((16, 128), F32),
         ],
@@ -504,20 +531,25 @@
 
     @pl.loop(0, CHUNKS)
     def _(g):
-        state[:, pl.ds(aligned(TOP + 8 * g), 8), :] = jnp.swapaxes(lined[pl.ds(8 * g, 8)], 0, 1)
-
-    west[...] = strip_columns(lambda f: state[f, TOP : TOP + N + 2, 0:128], 8, 0)
-    east[...] = strip_columns(lambda f: state[f, TOP : TOP + N + 2, 256:384], 8, N - HALO - 256)
+        block = jnp.swapaxes(lined[pl.ds(8 * g, 8)], 0, 1)
+        for j in range(3):
+            state[:, j, pl.ds(aligned(TOP + 8 * g), 8), :] = block[:, :, 128 * j : 128 * j + 128]
+
+    west[...] = strip_columns(lambda f: state[f, 0, TOP : TOP + N + 2, :], 8, 0)
+    east[...] = strip_columns(lambda f: state[f, 2, TOP : TOP + N + 2, :], 8, N - HALO - 256)
     for f in range(8):
-        south[HALO * f : HALO * f + HALO, 0:N] = state[f, TOP : TOP + HALO, 0:N]
-        north[HALO * f : HALO * f + HALO, 0:N] = state[f, TOP + N - HALO : TOP + N, 0:N]
+        for j, width in BLOCKS:
+            lanes = slice(128 * j, 128 * j + width)
+            rows = slice(HALO * f, HALO * f + HALO)
+            south[rows, lanes] = state[f, j, TOP : TOP + HALO, 0:width]
+            north[rows, lanes] = state[f, j, TOP + N - HALO : TOP + N, 0:width]
 
 
 def unpack_tiles(arrived):
     strip = jax.ShapeDtypeStruct((24, N + 2), F32)
     return pl.pallas_call(
         unpack_kernel,
-        out_shape=(jax.ShapeDtypeStruct((8, ROWS, LANES), F32),) + (strip,) * 4,
+        out_shape=(jax.ShapeDtypeStruct((8, 3, ROWS, 128), F32),) + (strip,) * 4,
         in_specs=[ANY],
         out_specs=(VMEM,) * 5,
         scratch_shapes=[
@@ -538,30 +570,43 @@
     copy.wait()
     insert_halos(first, 0, 8, west, east, south, north)
 
-    def advanced(src, b):
+    def load_coef(b):
         rows = pl.ds(b, 8)
-        result = []
-        for f, (_, new) in enumerate(stencil(src, b, [coef[i, rows, :] for i in range(6)])):
-            if f % LEV == 0:
-                new = new + coef[6 + f // LEV, rows, :]
-            result.append(new)
-        return result
+        return lambda j: [coef[i, j, rows, :] for i in range(6)]
 
     def step(src, dst):
-        @pl.loop(1, CHUNKS + 2)
+        @pl.loop(0, CHUNKS // 2 + 1)
         def _(r):
-            b = aligned(r * 8)
-            for f, new in enumerate(advanced(src, b)):
-                dst[f, pl.ds(b, 8), :] = new
+            for u in range(2):
+                b = aligned(r * 16 + 8 * u + 8)
+                rows = pl.ds(b, 8)
+
+                def take(t, j, old, new):
+                    dst[t * LEV, j, rows, :] = new[0] + coef[6 + t, j, rows, :]
+                    for k in range(1, LEV):
+                        dst[t * LEV + k, j, rows, :] = new[k]
+
+                stencil(src, b, load_coef(b), take)
 
     step(first, second)
     step(second, first)
 
-    @pl.loop(0, N // 8)
+    def finish(i, count):
+        b = aligned(TOP + 8 * i)
+
+        def take(t, j, old, new):
+            top = new[0] + coef[6 + t, j, pl.ds(b, 8), :]
+            store_levels(final, t, j, [top] + new[1:], i, count)
+
+        stencil(first, b, load_coef(b), take)
+
+    @pl.loop(0, N // 16)
     def _(i):
-        store_levels(final, advanced(first, aligned(TOP + 8 * i)), i, 8)
-
-    store_levels(final, advanced(first, TOP + N // 8 * 8), N // 8, N % 8)
+        finish(2 * i, 8)
+        finish(2 * i + 1, 8)
+
+    finish(N // 8 - 1, 8)
+    finish(N // 8, N % 8)
 
 
 def forward_window(state, coef, west, east, south, north):
@@ -571,8 +616,8 @@
         in_specs=[ANY] + [VMEM] * 5,
         out_specs=VMEM,
         scratch_shapes=[
-            pltpu.VMEM((8, ROWS, LANES), F32),
-            pltpu.VMEM((8, ROWS, LANES), F32),
+            pltpu.VMEM((8, 3, ROWS, 128), F32),
+            pltpu.VMEM((8, 3, ROWS, 128), F32),
             pltpu.SemaphoreType.DMA,
         ],
         name="forward_window",

time: 268 us -> 261 us (0.974)
  Pallas kernels: 68.8 us -> 61.6 us
    pallas_call x1, Pallas kernels: 20.4 us -> 16.3 us  [forward_window(): pl.pallas_call(forward_kernel, out_shape=jax.ShapeDtypeStruct((2, N, LEV,...]
    pallas_call x1, Pallas kernels: 29 us -> 25.8 us  [adjoint_window(): pl.pallas_call(adjoint_kernel, out_shape=(jax.ShapeDtypeStruct((2, N, LEV...]
where the time goes in v3:
time: 261 us; the launch traced here: 256 us
  waiting for transfers between devices  144 us (55%)
  Pallas kernels  61.6 us (24%)
  starting transfers between devices  36.4 us (14%)
  blocking collectives  8.23 us (3%)
  local copies, waits for them, and re-layouts  3.45 us (1%)
    all_to_all x1, waiting for transfers between devices, per_device(): lax.all_to_all(outgoing, 'lon', split_axis=0, concat_axis=0, tiled=True)  112 us
    ppermute x8, starting transfers between devices, neighbours(): return (lax.ppermute(high, axis, up), lax.ppermute(low, axis, down))  27 us
    ppermute x3, waiting for transfers between devices, per_device(): lax.ppermute(give, 'lat', [(i, i ^ bit) for i in range(lax.axis_size('lat...  26.4 us
    pallas_call x1, Pallas kernels, adjoint_window(): pl.pallas_call(adjoint_kernel, out_shape=(jax.ShapeDtypeStruct((2, N, LEV...  25.8 us
    pallas_call x1, Pallas kernels, forward_window(): pl.pallas_call(forward_kernel, out_shape=jax.ShapeDtypeStruct((2, N, LEV,...  16.3 us
    all_to_all x1, blocking collectives, per_device(): lax.all_to_all(keep, 'lon', split_axis=0, concat_axis=0, tiled=True)  8.23 us
    pallas_call x1, Pallas kernels, unpack_tiles(): pl.pallas_call(unpack_kernel, out_shape=(jax.ShapeDtypeStruct((8, 3, ROWS...  6.94 us
    all_to_all x1, starting transfers between devices, per_device(): lax.all_to_all(outgoing, 'lon', split_axis=0, concat_axis=0, tiled=True)  6.06 us
  transfers between devices with their start and end apart: 12, of which 9 were waited for; matrix products, arithmetic and copies ran while one was open for 0% of the time, Pallas kernels for 1%

profile of v3, /device:TPU:96, one launch (start us, length us, event | category | flops | bytes accessed | tf_op | source)
XLA Modules:
  0.0 256.1 jit_solution(6166232881743554042)
XLA Ops:
  0.6 5.6 %edge_strips.1 = (f32[48,272]{1,0:T(8,128)}, f32[48,272]{1,0:T(8,128)}, f32[48,272]{1,0:T(8,128)}, f32[48,272]{1,0:T(8,128)}) custom-call(s32[3,3]{1,0:T(4,128)} %wet.3, f32[270,270]{1,0:T(8,128)} %zd.3, f32[270,270]{1,0:T(8,128)} %zf.3, f32[270,270]{1,0:T(8,128)} %md.3, f32[270,270]{1,0:T(8,128)} %mf.3, f32[270,270]{1,0:T(8,128)} %vm.3, ...), custom_call_target="tpu_custom_call" | custom-call | tf_op jit(solution)/shard_map/edge_strips/pallas_call | solution.py:207
  6.2 3.9 %collective-permute-start.1 = (f32[48,272]{1,0:T(8,128)}, f32[48,272]{1,0:T(8,128)S(1)}, u32[]{:S(2)}, u32[]{:S(2)}) collective-permute-start(f32[48,272]{1,0:T(8,128)} %get-tuple-element.23.after), channel_id=1, source_target_pairs={{1,0},{2,1},{3,2},{4,3},{5,4},{6,5},{7,6},{8,7},{9,8},{10,9},{11,1... | collective-permute-start | bytes 156680 | tf_op jit(solution)/shard_map/ppermute | solution.py:631
  10.1 3.7 %pack_tiles.1 = f32[16,2,8,8192]{3,2,1,0:T(8,128)} custom-call(s32[27]{0:T(128)} %ids.1, f32[27,8,8100]{2,1,0:T(8,128)} %stored.1, f32[48,272]{1,0:T(8,128)} %get-tuple-element.23.after), custom_call_target="tpu_custom_call" | custom-call | tf_op jit(solution)/shard_map/pack_tiles/pallas_call | solution.py:118
  14.5 1.7 row_strips.2
  16.2 4.1 %collective-permute-start.2 = (f32[48,384]{1,0:T(8,128)}, f32[48,384]{1,0:T(8,128)S(1)}, u32[]{:S(2)}, u32[]{:S(2)}) collective-permute-start(f32[48,384]{1,0:T(8,128)} %get-tuple-element.31), channel_id=1, source_target_pairs={{0,16},{16,32},{32,48},{48,64},{64,80},{80,96},{96,112},{1,17},{17... | collective-permute-start | bytes 221192 | tf_op jit(solution)/shard_map/ppermute | solution.py:631
  20.3 5.4 %collective-permute-start.3 = (f32[48,384]{1,0:T(8,128)}, f32[48,384]{1,0:T(8,128)S(1)}, u32[]{:S(2)}, u32[]{:S(2)}) collective-permute-start(f32[48,384]{1,0:T(8,128)} %get-tuple-element.32), channel_id=1, source_target_pairs={{16,0},{32,16},{48,32},{64,48},{80,64},{96,80},{112,96},{17,1},{33... | collective-permute-start | bytes 221192 | tf_op jit(solution)/shard_map/ppermute | solution.py:631
  26.8 1.8 collective-permute-done.3.north
  29.3 25.8 %adjoint_window.1 = (f32[2,270,4,270]{3,2,1,0:T(4,128)}, f32[8,3,304,128]{3,2,1,0:T(8,128)}, f32[64,16,128]{2,1,0:T(8,128)}, f32[64,16,128]{2,1,0:T(8,128)}) custom-call(s32[3,3]{1,0:T(4,128)} %wet.3, s32[3,3]{1,0:T(4,128)} %labels.1, f32[270,270]{1,0:T(8,128)} %zd.3, f32[270,270]{1,0:T(8,128)} %zf.3, f32[270,270]{1,0:T(8,128)} %md.3, f32[270,270]{1,0:T(8,128)} %mf.3, ...), custom_call_target="tpu_custom_call" | custom-call | tf_op jit(solution)/shard_map/adjoint_window/pallas_call | solution.py:458
  55.6 15.2 %collective-permute-done.8 = f32[64,16,128]{2,1,0:T(8,128)S(1)} collective-permute-done((f32[64,16,128]{2,1,0:T(8,128)}, f32[64,16,128]{2,1,0:T(8,128)S(1)}, u32[]{:S(2)}, u32[]{:S(2)}) %collective-permute-start.8) | collective-permute-done | bytes 524320 | tf_op jit(solution)/shard_map/ppermute | solution.py:653
  70.8 1.1 add.9
  72.0 7.5 %collective-permute-done.9 = f32[32,16,128]{2,1,0:T(8,128)S(1)} collective-permute-done((f32[32,16,128]{2,1,0:T(8,128)S(1)}, f32[32,16,128]{2,1,0:T(8,128)S(1)}, u32[]{:S(2)}, u32[]{:S(2)}) %collective-permute-start.9) | collective-permute-done | bytes 262176 | tf_op jit(solution)/shard_map/ppermute | solution.py:653
  79.5 2.8 %collective-permute-start.10 = (f32[16,16,128]{2,1,0:T(8,128)S(1)}, f32[16,16,128]{2,1,0:T(8,128)S(1)}, u32[]{:S(2)}, u32[]{:S(2)}) collective-permute-start(f32[16,16,128]{2,1,0:T(8,128)S(1)} %slice.30), channel_id=1, source_target_pairs={{0,64},{16,80},{32,96},{48,112},{64,0},{80,16},{96,32},{112,48},{1... | collective-permute-start | bytes 393224 | tf_op jit(solution)/shard_map/ppermute | solution.py:653
  82.3 3.8 %collective-permute-done.10 = f32[16,16,128]{2,1,0:T(8,128)S(1)} collective-permute-done((f32[16,16,128]{2,1,0:T(8,128)S(1)}, f32[16,16,128]{2,1,0:T(8,128)S(1)}, u32[]{:S(2)}, u32[]{:S(2)}) %collective-permute-start.10) | collective-permute-done | bytes 131104 | tf_op jit(solution)/shard_map/ppermute | solution.py:653
  86.1 8.2 %all_to_all.10 = f32[16,16,128]{2,1,0:T(8,128)S(1)} all-to-all(f32[16,16,128]{2,1,0:T(8,128)S(1)} %slice_add_fusion.1), channel_id=1, replica_groups=mesh['lat'=8,'lon'=16] {'lon'}, dimensions={0} | all-to-all | bytes 262144 | tf_op jit(solution)/shard_map/all_to_all | solution.py:657
  94.3 6.1 %all-to-all-start = ((f32[16,2,8,8192]{3,2,1,0:T(8,128)}), f32[16,2,8,8192]{3,2,1,0:T(8,128)}, u32[]{:S(2)}, u32[]{:S(2)}) async-start(f32[16,2,8,8192]{3,2,1,0:T(8,128)} %pack_tiles.1), calls=%async_computation | async-start | bytes 16777216 | tf_op jit(solution)/shard_map/all_to_all | solution.py:647
  100.4 112.1 %all-to-all-done.arrived = f32[16,2,8,8192]{3,2,1,0:T(8,128)} async-done(((f32[16,2,8,8192]{3,2,1,0:T(8,128)}), f32[16,2,8,8192]{3,2,1,0:T(8,128)}, u32[]{:S(2)}, u32[]{:S(2)}) %all-to-all-start) | async-done | bytes 8388640 | tf_op jit(solution)/shard_map/all_to_all | solution.py:647
  212.5 6.9 %unpack_tiles.1 = (f32[8,3,304,128]{3,2,1,0:T(8,128)}, f32[24,272]{1,0:T(8,128)}, f32[24,272]{1,0:T(8,128)}, f32[24,272]{1,0:T(8,128)}, f32[24,272]{1,0:T(8,128)}) custom-call(f32[16,2,8,8192]{3,2,1,0:T(8,128)} %all-to-all-done.arrived), custom_call_target="tpu_custom_call" | custom-call | tf_op jit(solution)/shard_map/unpack_tiles/pallas_call | solution.py:550
  219.5 3.8 %collective-permute-start.5 = (f32[24,272]{1,0:T(8,128)}, f32[24,272]{1,0:T(8,128)S(1)}, u32[]{:S(2)}, u32[]{:S(2)}) collective-permute-start(f32[24,272]{1,0:T(8,128)} %get-tuple-element.35), channel_id=1, source_target_pairs={{1,0},{2,1},{3,2},{4,3},{5,4},{6,5},{7,6},{8,7},{9,8},{10,9},{11,1... | collective-permute-start | bytes 78344 | tf_op jit(solution)/shard_map/ppermute | solution.py:631
  223.6 1.6 collective-permute-done.4.west
  225.9 1.5 row_strips.3
  227.4 2.8 %collective-permute-start.6 = (f32[24,384]{1,0:T(8,128)}, f32[24,384]{1,0:T(8,128)S(1)}, u32[]{:S(2)}, u32[]{:S(2)}) collective-permute-start(f32[24,384]{1,0:T(8,128)} %get-tuple-element.38), channel_id=1, source_target_pairs={{0,16},{16,32},{32,48},{48,64},{64,80},{80,96},{96,112},{1,17},{17... | collective-permute-start | bytes 110600 | tf_op jit(solution)/shard_map/ppermute | solution.py:631
  230.2 7.0 %collective-permute-start.7 = (f32[24,384]{1,0:T(8,128)}, f32[24,384]{1,0:T(8,128)S(1)}, u32[]{:S(2)}, u32[]{:S(2)}) collective-permute-start(f32[24,384]{1,0:T(8,128)} %get-tuple-element.39), channel_id=1, source_target_pairs={{16,0},{32,16},{48,32},{64,48},{80,64},{96,80},{112,96},{17,1},{33... | collective-permute-start | bytes 110600 | tf_op jit(solution)/shard_map/ppermute | solution.py:631
  238.0 1.2 collective-permute-done.7.north
  239.8 16.3 %forward_window.1 = f32[2,270,4,270]{3,2,1,0:T(4,128)} custom-call(f32[8,3,304,128]{3,2,1,0:T(8,128)} %get-tuple-element.26.state, f32[8,3,304,128]{3,2,1,0:T(8,128)} %get-tuple-element.33.coef, f32[24,272]{1,0:T(8,128)} %copy-done.2, f32[24,272]{1,0:T(8,128)} %copy-done.3, f32[24,384]{1,0:T(8,128)} %copy-done.6, f32[24,384]{1,0:T(8,128)} %copy-done.7), custom_call_target="tpu_custom_call" | custom-call | tf_op jit(solution)/shard_map/forward_window/pallas_call | solution.py:613
  (36 shorter events, 5.4 us)
Async XLA Ops:
  6.2 7.6 %collective-permute-start = (f32[48,272]{1,0:T(8,128)}, f32[48,272]{1,0:T(8,128)S(1)}, u32[]{:S(2)}, u32[]{:S(2)}) collective-permute-start(f32[48,272]{1,0:T(8,128)} %get-tuple-element.24), channel_id=1, source_target_pairs={{0,1},{1,2},{2,3},{3,4},{4,5},{5,6},{6,7},{7,8},{8,9},{9,10},{10,1... | collective-permute-start | bytes 156680 | tf_op jit(solution)/shard_map/ppermute | solution.py:631
  6.2 7.6 %collective-permute-start.1 = (f32[48,272]{1,0:T(8,128)}, f32[48,272]{1,0:T(8,128)S(1)}, u32[]{:S(2)}, u32[]{:S(2)}) collective-permute-start(f32[48,272]{1,0:T(8,128)} %get-tuple-element.23.after), channel_id=1, source_target_pairs={{1,0},{2,1},{3,2},{4,3},{5,4},{6,5},{7,6},{8,7},{9,8},{10,9},{11,1... | collective-permute-start | bytes 156680 | tf_op jit(solution)/shard_map/ppermute | solution.py:631
  13.8 0.6 copy-start
  13.9 0.6 copy-start.1
  16.2 10.6 %collective-permute-start.2 = (f32[48,384]{1,0:T(8,128)}, f32[48,384]{1,0:T(8,128)S(1)}, u32[]{:S(2)}, u32[]{:S(2)}) collective-permute-start(f32[48,384]{1,0:T(8,128)} %get-tuple-element.31), channel_id=1, source_target_pairs={{0,16},{16,32},{32,48},{48,64},{64,80},{80,96},{96,112},{1,17},{17... | collective-permute-start | bytes 221192 | tf_op jit(solution)/shard_map/ppermute | solution.py:631
  20.3 8.3 %collective-permute-start.3 = (f32[48,384]{1,0:T(8,128)}, f32[48,384]{1,0:T(8,128)S(1)}, u32[]{:S(2)}, u32[]{:S(2)}) collective-permute-start(f32[48,384]{1,0:T(8,128)} %get-tuple-element.32), channel_id=1, source_target_pairs={{16,0},{32,16},{48,32},{64,48},{80,64},{96,80},{112,96},{17,1},{33... | collective-permute-start | bytes 221192 | tf_op jit(solution)/shard_map/ppermute | solution.py:631
  26.8 1.8 copy-start.4
  28.6 0.6 copy-start.5
  55.1 15.7 %collective-permute-start.8 = (f32[64,16,128]{2,1,0:T(8,128)}, f32[64,16,128]{2,1,0:T(8,128)S(1)}, u32[]{:S(2)}, u32[]{:S(2)}) collective-permute-start(f32[64,16,128]{2,1,0:T(8,128)} %get-tuple-element.42), channel_id=1, source_target_pairs={{0,32},{16,48},{32,0},{48,16},{64,96},{80,112},{96,64},{112,80},{1... | collective-permute-start | bytes 1572872 | tf_op jit(solution)/shard_map/ppermute | solution.py:653
  71.9 7.5 %collective-permute-start.9 = (f32[32,16,128]{2,1,0:T(8,128)S(1)}, f32[32,16,128]{2,1,0:T(8,128)S(1)}, u32[]{:S(2)}, u32[]{:S(2)}) collective-permute-start(f32[32,16,128]{2,1,0:T(8,128)S(1)} %slice.28), channel_id=1, source_target_pairs={{0,16},{16,0},{32,48},{48,32},{64,80},{80,64},{96,112},{112,96},{1... | collective-permute-start | bytes 786440 | tf_op jit(solution)/shard_map/ppermute | solution.py:653
  79.5 6.6 %collective-permute-start.10 = (f32[16,16,128]{2,1,0:T(8,128)S(1)}, f32[16,16,128]{2,1,0:T(8,128)S(1)}, u32[]{:S(2)}, u32[]{:S(2)}) collective-permute-start(f32[16,16,128]{2,1,0:T(8,128)S(1)} %slice.30), channel_id=1, source_target_pairs={{0,64},{16,80},{32,96},{48,112},{64,0},{80,16},{96,32},{112,48},{1... | collective-permute-start | bytes 393224 | tf_op jit(solution)/shard_map/ppermute | solution.py:653
  94.3 118.2 %all-to-all-start = ((f32[16,2,8,8192]{3,2,1,0:T(8,128)}), f32[16,2,8,8192]{3,2,1,0:T(8,128)}, u32[]{:S(2)}, u32[]{:S(2)}) async-start(f32[16,2,8,8192]{3,2,1,0:T(8,128)} %pack_tiles.1), calls=%async_computation | async-start | bytes 16777216 | tf_op jit(solution)/shard_map/all_to_all | solution.py:647
  219.4 5.8 %collective-permute-start.4 = (f32[24,272]{1,0:T(8,128)}, f32[24,272]{1,0:T(8,128)S(1)}, u32[]{:S(2)}, u32[]{:S(2)}) collective-permute-start(f32[24,272]{1,0:T(8,128)} %get-tuple-element.34), channel_id=1, source_target_pairs={{0,1},{1,2},{2,3},{3,4},{4,5},{5,6},{6,7},{7,8},{8,9},{9,10},{10,1... | collective-permute-start | bytes 78344 | tf_op jit(solution)/shard_map/ppermute | solution.py:631
  219.5 5.8 %collective-permute-start.5 = (f32[24,272]{1,0:T(8,128)}, f32[24,272]{1,0:T(8,128)S(1)}, u32[]{:S(2)}, u32[]{:S(2)}) collective-permute-start(f32[24,272]{1,0:T(8,128)} %get-tuple-element.35), channel_id=1, source_target_pairs={{1,0},{2,1},{3,2},{4,3},{5,4},{6,5},{7,6},{8,7},{9,8},{10,9},{11,1... | collective-permute-start | bytes 78344 | tf_op jit(solution)/shard_map/ppermute | solution.py:631
  225.2 0.6 copy-start.2
  225.3 0.6 copy-start.3
  227.4 10.6 %collective-permute-start.6 = (f32[24,384]{1,0:T(8,128)}, f32[24,384]{1,0:T(8,128)S(1)}, u32[]{:S(2)}, u32[]{:S(2)}) collective-permute-start(f32[24,384]{1,0:T(8,128)} %get-tuple-element.38), channel_id=1, source_target_pairs={{0,16},{16,32},{32,48},{48,64},{64,80},{80,96},{96,112},{1,17},{17... | collective-permute-start | bytes 110600 | tf_op jit(solution)/shard_map/ppermute | solution.py:631
  230.2 9.0 %collective-permute-start.7 = (f32[24,384]{1,0:T(8,128)}, f32[24,384]{1,0:T(8,128)S(1)}, u32[]{:S(2)}, u32[]{:S(2)}) collective-permute-start(f32[24,384]{1,0:T(8,128)} %get-tuple-element.39), channel_id=1, source_target_pairs={{16,0},{32,16},{48,32},{64,48},{80,64},{96,80},{112,96},{17,1},{33... | collective-permute-start | bytes 110600 | tf_op jit(solution)/shard_map/ppermute | solution.py:631
  238.0 1.2 copy-start.6
  239.2 0.6 copy-start.7

commit v4 on v3

--- a/solution.py
+++ b/solution.py
@@ -1,3 +1,5 @@
+import functools
+
 import jax
 import jax.numpy as jnp
 from jax import lax
@@ -135,6 +137,182 @@
     )(ids, stored, after)
 
 
+def split_kernel(ids, stored, after, first, own, cross, held, tail, empty, count, route, filled, in_sem, out_sem, tail_sem, empty_sem):
+    owners = first.shape[0]
+    chips = own.shape[0]
+    me = lax.axis_index("lon")
+    outs = [(first, owners), (own, chips), (cross, chips)]
+
+    def fetch(s):
+        return pltpu.make_async_copy(stored.at[s], held.at[s], in_sem.at[s])
+
+    def each(s, act):
+        for kind, (out, _) in enumerate(outs):
+
+            @pl.when(route[s, 0] == kind)
+            def _():
+                to = out.at[route[s, 1]]
+                act(pltpu.make_async_copy(held.at[s, :, pl.ds(0, TAIL)], to.at[:, pl.ds(0, TAIL)], out_sem.at[s]))
+                act(pltpu.make_async_copy(tail.at[s], to.at[:, pl.ds(TAIL, 128)], tail_sem.at[s]))
+
+    def each_empty(act):
+        for kind, (out, size) in enumerate(outs):
+
+            @pl.loop(0, size)
+            def _(i):
+                @pl.when(filled[kind, i] == 0)
+                def _():
+                    act(
+                        pltpu.make_async_copy(
+                            empty, out.at[i, :, pl.ds(TAIL, 128)], empty_sem.at[kind, i]
+                        )
+                    )
+
+    @pl.loop(0, SLOTS)
+    def _(s):
+        @pl.when(ids[s] >= 0)
+        def _():
+            fetch(s).start()
+
+    @pl.loop(0, owners)
+    def _(o):
+        count[o] = 0
+        for kind in range(3):
+            filled[kind, o] = 0
+
+    empty[...] = jnp.full((8, 128), -1.0, F32)
+    lane = lax.broadcasted_iota(I32, (8, 128), 1)
+
+    @pl.loop(0, SLOTS)
+    def _(s):
+        tile = ids[s]
+
+        @pl.when(tile >= 0)
+        def _():
+            row = tile // COLUMNS
+            column = tile - row * COLUMNS
+            owner = column // SIDE
+            rank = count[owner]
+            count[owner] = rank + 1
+            away = owner ^ me
+            kind = jnp.where(rank == 0, 0, 1 + (away & 1))
+            index = jnp.where(rank == 0, owner, away >> 1)
+            route[s, 0] = kind
+            route[s, 1] = index
+            filled[kind, index] = 1
+            place = row * SIDE + column - owner * SIDE
+            fetch(s).wait()
+            last = jnp.concatenate([held[s, :, TAIL:CELLS], jnp.zeros((8, 128 - TAG), F32)], axis=1)
+            tail[s] = jnp.where(lane < TAG, last, place.astype(F32))
+            each(s, lambda copy: copy.start())
+
+    each_empty(lambda copy: copy.start())
+
+    @pl.loop(0, SLOTS)
+    def _(s):
+        @pl.when(ids[s] >= 0)
+        def _():
+            each(s, lambda copy: copy.wait())
+
+    each_empty(lambda copy: copy.wait())
+
+
+def split_tiles(ids, stored, after, owners):
+    chips = owners // 2
+    return pl.pallas_call(
+        split_kernel,
+        out_shape=tuple(jax.ShapeDtypeStruct((n, 8, FLAT), F32) for n in (owners, chips, chips)),
+        in_specs=[SMEM, ANY, ANY],
+        out_specs=(ANY,) * 3,
+        scratch_shapes=[
+            pltpu.VMEM((SLOTS, 8, CELLS), F32),
+            pltpu.VMEM((SLOTS, 8, 128), F32),
+            pltpu.VMEM((8, 128), F32),
+            pltpu.SMEM((owners,), I32),
+            pltpu.SMEM((SLOTS, 2), I32),
+            pltpu.SMEM((3, owners), I32),
+            pltpu.SemaphoreType.DMA((SLOTS,)),
+            pltpu.SemaphoreType.DMA((SLOTS,)),
+            pltpu.SemaphoreType.DMA((SLOTS,)),
+            pltpu.SemaphoreType.DMA((3, owners)),
+        ],
+        name="split_tiles",
+    )(ids, stored, after)
+
+
+def merge_kernel(own, cross, *refs):
+    chips = own.shape[0]
+    outs = refs[:chips]
+    clash, held, empty, own_tags, cross_tags, sem, in_sem, out_sem = refs[chips:]
+    copies = [
+        pltpu.make_async_copy(x.at[:, pl.ds(0, 1), pl.ds(TAIL, 128)], tags, sem.at[i])
+        for i, (x, tags) in enumerate(((own, own_tags), (cross, cross_tags)))
+    ]
+    for copy in copies:
+        copy.start()
+    empty[...] = jnp.full((8, 128), -1.0, F32)
+    for copy in copies:
+        copy.wait()
+    total = jnp.int32(0)
+    has = []
+    for c in range(chips):
+        mine = own_tags[c, 0, TAG] >= 0
+        other = cross_tags[c, 0, TAG] >= 0
+        total = total + jnp.where(mine & other, 1, 0)
+        has.append((mine, other))
+    clash[0] = total
+
+    def filling(c, act):
+        mine, other = has[c]
+
+        @pl.when(mine)
+        def _():
+            act(pltpu.make_async_copy(own.at[c], held.at[c], in_sem.at[c]))
+
+        @pl.when(other & ~mine)
+        def _():
+            act(pltpu.make_async_copy(cross.at[c], held.at[c], in_sem.at[c]))
+
+    def leaving(c, act):
+        mine, other = has[c]
+
+        @pl.when(mine | other)
+        def _():
+            act(pltpu.make_async_copy(held.at[c], outs[c], out_sem.at[c]))
+
+        @pl.when(~(mine | other))
+        def _():
+            act(pltpu.make_async_copy(empty, outs[c].at[:, pl.ds(TAIL, 128)], out_sem.at[c]))
+
+    for c in range(chips):
+        filling(c, lambda copy: copy.start())
+    for c in range(chips):
+        filling(c, lambda copy: copy.wait())
+        leaving(c, lambda copy: copy.start())
+    for c in range(chips):
+        leaving(c, lambda copy: copy.wait())
+
+
+def merge_tiles(own, cross):
+    chips = own.shape[0]
+    return pl.pallas_call(
+        merge_kernel,
+        out_shape=(jax.ShapeDtypeStruct((8, FLAT), F32),) * chips + (jax.ShapeDtypeStruct((1,), I32),),
+        in_specs=[ANY, ANY],
+        out_specs=(ANY,) * chips + (SMEM,),
+        scratch_shapes=[
+            pltpu.VMEM((chips, 8, FLAT), F32),
+            pltpu.VMEM((8, 128), F32),
+            pltpu.SMEM((chips, 1, 128), F32),
+            pltpu.SMEM((chips, 1, 128), F32),
+            pltpu.SemaphoreType.DMA((2,)),
+            pltpu.SemaphoreType.DMA((chips,)),
+            pltpu.SemaphoreType.DMA((chips,)),
+        ],
+        name="merge_tiles",
+    )(own, cross)
+
+
 def strip_columns(load, count, first):
     lane = lax.broadcasted_iota(I32, (N + 2, 128), 1)
     strip = jnp.zeros((N + 2, 128), F32)
@@ -292,7 +470,7 @@
 
 
 def adjoint_kernel(
-    wet, labels, zd, zf, md, mf, vm, forcing, adjoint, west, east, south, north,
+    wet, labels, clash, zd, zf, md, mf, vm, forcing, adjoint, west, east, south, north,
     initial, forward_coef, keep, give,
     ext, other, coef, surface, coarse, piece,
 ):
@@ -427,9 +605,10 @@
         coarse[t] = full / 9.0
     owners = keep.shape[0] // 4
     here = lax.axis_index("lat")
-    keep[...] = jnp.zeros(keep.shape, F32)
-    give[...] = jnp.zeros(give.shape, F32)
-    piece[...] = jnp.zeros((16, 128), F32)
+    last = lax.broadcasted_iota(I32, (16, 128), 0) == 15
+    piece[...] = jnp.where(last, clash[0].astype(F32), 0.0)
+    keep[...] = jnp.broadcast_to(piece[...], keep.shape)
+    give[...] = jnp.broadcast_to(piece[...], give.shape)
     part = COARSE // 2
     for r in range(SIDE):
         for c in range(SIDE):
@@ -454,7 +633,7 @@
                 give[at] = piece[...]
 
 
-def adjoint_window(wet, labels, zd, zf, md, mf, vm, forcing, adjoint, west, east, south, north, owners):
+def adjoint_window(wet, labels, clash, zd, zf, md, mf, vm, forcing, adjoint, west, east, south, north, owners):
     return pl.pallas_call(
         adjoint_kernel,
         out_shape=(
@@ -463,7 +642,7 @@
             jax.ShapeDtypeStruct((4 * owners, 16, 128), F32),
             jax.ShapeDtypeStruct((4 * owners, 16, 128), F32),
         ),
-        in_specs=[SMEM, SMEM] + [VMEM] * 11,
+        in_specs=[SMEM] * 3 + [VMEM] * 11,
         out_specs=(VMEM,) * 4,
         scratch_shapes=[
             pltpu.VMEM((16, 3, ROWS, 128), F32),
@@ -474,44 +653,50 @@
             pltpu.VMEM((16, 128), F32),
         ],
         name="adjoint_window",
-    )(wet, labels, zd, zf, md, mf, vm, forcing, adjoint, west, east, south, north)
-
-
-def unpack_kernel(arrived, state, west, east, south, north, tags, slot_of, tiles, lined, tag_sem, tile_sem):
-    sources = arrived.shape[0]
-    copy = pltpu.make_async_copy(
-        arrived.at[:, :, pl.ds(0, 1), pl.ds(TAIL, 128)], tags, tag_sem
-    )
-    copy.start()
+    )(wet, labels, clash, zd, zf, md, mf, vm, forcing, adjoint, west, east, south, north)
+
+
+def unpack_kernel(extra, first, *refs):
+    seconds = refs[:extra]
+    state, west, east, south, north, tags, more_tags, present, tiles, lined, tag_sem, tile_sem = refs[extra:]
+    slots = first.shape[0]
+    copies = [pltpu.make_async_copy(first.at[:, pl.ds(0, 1), pl.ds(TAIL, 128)], tags, tag_sem.at[0])]
+    for c, second in enumerate(seconds):
+        copies.append(
+            pltpu.make_async_copy(second.at[pl.ds(0, 1), pl.ds(TAIL, 128)], more_tags.at[c], tag_sem.at[1 + c])
+        )
+    for copy in copies:
+        copy.start()
     places = SIDE * SIDE
 
     @pl.loop(0, places)
     def _(p):
-        slot_of[p] = -1
-
-    copy.wait()
-
-    @pl.loop(0, sources * PAIR)
+        present[p] = 0
+
+    for copy in copies:
+        copy.wait()
+
+    def fetch(source, p):
+        return pltpu.make_async_copy(source, tiles.at[p], tile_sem.at[p])
+
+    def take(source, tag):
+        place = tag.astype(I32)
+
+        @pl.when(place >= 0)
+        def _():
+            present[place] = 1
+            fetch(source, place).start()
+
+    @pl.loop(0, slots)
     def _(i):
-        source = i // PAIR
-        place = tags[source, i - source * PAIR, 0, TAG].astype(I32)
-
-        @pl.when(place >= 0)
-        def _():
-            slot_of[place] = i
-
-    def fetch(p):
-        slot = slot_of[p]
-        source = slot // PAIR
-        return pltpu.make_async_copy(arrived.at[source, slot - source * PAIR], tiles.at[p], tile_sem.at[p])
+        take(first.at[i], tags[i, 0, TAG])
+
+    for c, second in enumerate(seconds):
+        take(second, more_tags[c, 0, TAG])
 
     @pl.loop(0, places)
     def _(p):
-        @pl.when(slot_of[p] >= 0)
-        def _():
-            fetch(p).start()
-
-        @pl.when(slot_of[p] < 0)
+        @pl.when(present[p] == 0)
         def _():
             tiles[p] = jnp.zeros((8, FLAT), F32)
 
@@ -519,9 +704,9 @@
     def _(r):
         for c in range(SIDE):
 
-            @pl.when(slot_of[r * SIDE + c] >= 0)
+            @pl.when(present[r * SIDE + c] != 0)
             def _():
-                fetch(r * SIDE + c).wait()
+                fetch(first.at[0], r * SIDE + c).wait()
 
         for y in range(TILE):
             for c in range(SIDE):
@@ -545,23 +730,25 @@
             north[rows, lanes] = state[f, j, TOP + N - HALO : TOP + N, 0:width]
 
 
-def unpack_tiles(arrived):
+def unpack_tiles(first, *seconds):
     strip = jax.ShapeDtypeStruct((24, N + 2), F32)
+    extra = len(seconds)
     return pl.pallas_call(
-        unpack_kernel,
+        functools.partial(unpack_kernel, extra),
         out_shape=(jax.ShapeDtypeStruct((8, 3, ROWS, 128), F32),) + (strip,) * 4,
-        in_specs=[ANY],
+        in_specs=[ANY] * (1 + extra),
         out_specs=(VMEM,) * 5,
         scratch_shapes=[
-            pltpu.SMEM((arrived.shape[0], PAIR, 1, 128), F32),
+            pltpu.SMEM((first.shape[0], 1, 128), F32),
+            pltpu.SMEM((8, 1, 128), F32),
             pltpu.SMEM((SIDE * SIDE,), I32),
             pltpu.VMEM((SIDE * SIDE, 8, FLAT), F32),
             pltpu.VMEM((8 * CHUNKS, 8, LANES), F32),
-            pltpu.SemaphoreType.DMA,
+            pltpu.SemaphoreType.DMA((9,)),
             pltpu.SemaphoreType.DMA((SIDE * SIDE,)),
         ],
         name="unpack_tiles",
-    )(arrived)
+    )(first, *seconds)
 
 
 def forward_kernel(state, coef, west, east, south, north, final, first, second, sem):
@@ -631,6 +818,10 @@
     return lax.ppermute(high, axis, up), lax.ppermute(low, axis, down)
 
 
+def xor_permute(x, axis, bits):
+    return lax.ppermute(x, axis, [(i, i ^ bits) for i in range(lax.axis_size(axis))])
+
+
 def per_device(
     stored_tiles, stored_ids, wet_tiles, control_map, zonal_diffusivity, meridional_diffusivity,
     zonal_flow, meridional_flow, vertical_mixing, forcing, final_adjoint,
@@ -642,27 +833,45 @@
     )
     low, high, bottom, top = edge_strips(wet_tiles, *fields)
     west, east = neighbours(low, high, "lon", True)
-    outgoing = pack_tiles(stored_ids, stored_tiles, low, owners)
-    outgoing, west, east = lax.optimization_barrier((outgoing, west, east))
-    arrived = lax.all_to_all(outgoing, "lon", split_axis=0, concat_axis=0, tiled=True)
+    first, own, cross = split_tiles(stored_ids, stored_tiles, low, owners)
+    first, west, east = lax.optimization_barrier((first, west, east))
+    first = lax.all_to_all(first, "lon", split_axis=0, concat_axis=0, tiled=True)
+    cross = xor_permute(cross, "lon", 1)
     south, north = neighbours(*with_corners(bottom, top, west, east), "lat", False)
+    *seconds, clash = merge_tiles(own, cross)
+    seconds = [seconds[0]] + [xor_permute(x, "lon", 2 * c) for c, x in enumerate(seconds) if c > 0]
     initial, coef, keep, give = adjoint_window(
-        wet_tiles, control_map, *fields, west, east, south, north, owners
+        wet_tiles, control_map, clash, *fields, west, east, south, north, owners
     )
     for bit in (2, 1, 4):
-        keep = keep + lax.ppermute(give, "lat", [(i, i ^ bit) for i in range(lax.axis_size("lat"))])
+        keep = keep + xor_permute(give, "lat", bit)
         half = keep.shape[0] // 2
         if bit != 4:
             keep, give = keep[:half], keep[half:]
     gathered = lax.all_to_all(keep, "lon", split_axis=0, concat_axis=0, tiled=True)
-    total = jnp.sum(gathered, axis=0)[: COARSE // 2]
+    total = jnp.sum(gathered, axis=0)
+    clashes = total[15, 0]
+    total = total[: COARSE // 2]
     total = jnp.stack([total[:, :60], total[:, 64:124]]).reshape(2, COARSE // 2, 2, COARSE)
     control = total.transpose(2, 0, 1, 3).reshape(1, 2, COARSE * COARSE)
 
-    state, low, high, bottom, top = unpack_tiles(arrived)
-    west, east = neighbours(low, high, "lon", True)
-    south, north = neighbours(*with_corners(bottom, top, west, east), "lat", False)
-    final = forward_window(state, coef, west, east, south, north)
+    def halos(low, high, bottom, top):
+        west, east = neighbours(low, high, "lon", True)
+        return (west, east) + neighbours(*with_corners(bottom, top, west, east), "lat", False)
+
+    state, *strips = unpack_tiles(first, *seconds)
+    strips = halos(*strips)
+
+    def ready(ids, stored, coef, state, *strips):
+        return forward_window(state, coef, *strips)
+
+    def complete(ids, stored, coef, state, *strips):
+        outgoing = pack_tiles(ids, stored, coef, owners)
+        arrived = lax.all_to_all(outgoing, "lon", split_axis=0, concat_axis=0, tiled=True)
+        state, *strips = unpack_tiles(arrived.reshape(owners * PAIR, 8, FLAT))
+        return forward_window(state, coef, *halos(*strips))
+
+    final = lax.cond(clashes > 0, complete, ready, stored_ids, stored_tiles, coef, state, *strips)
     return final.transpose(0, 2, 1, 3), initial.transpose(0, 2, 1, 3), control
 
 

time: 261 us -> 237 us (0.908)
  the two profiles are of different devices: /device:TPU:96 before, /device:TPU:25 now
where the time goes in v4:
time: 237 us
  waiting for transfers between devices  108 us (46%)
  Pallas kernels  63.5 us (27%)
  starting transfers between devices  37.7 us (16%)
  blocking collectives  18 us (8%)
  local copies, waits for them, and re-layouts  6.58 us (3%)
    ppermute x11, waiting for transfers between devices, xor_permute(): lax.ppermute(x, axis, [(i, i ^ bits) for i in range(lax.axis_size(axis))])  92.9 us
    pallas_call x1, Pallas kernels, adjoint_window(): pl.pallas_call(adjoint_kernel, out_shape=(jax.ShapeDtypeStruct((2, N, LEV...  26.4 us
    ppermute x8, starting transfers between devices, neighbours(): return (lax.ppermute(high, axis, up), lax.ppermute(low, axis, down))  20.2 us
    all_to_all x1, blocking collectives, per_device(): lax.all_to_all(keep, 'lon', split_axis=0, concat_axis=0, tiled=True)  18 us
    ppermute x8, waiting for transfers between devices, neighbours(): return (lax.ppermute(high, axis, up), lax.ppermute(low, axis, down))  15.3 us
    pallas_call x1, Pallas kernels, forward_window(): pl.pallas_call(forward_kernel, out_shape=jax.ShapeDtypeStruct((2, N, LEV,...  14.5 us
    ppermute x11, starting transfers between devices, xor_permute(): lax.ppermute(x, axis, [(i, i ^ bits) for i in range(lax.axis_size(axis))])  12.5 us
    pallas_call x1, Pallas kernels, unpack_tiles(): pl.pallas_call(functools.partial(unpack_kernel, extra), out_shape=(jax.Sh...  6.8 us
  transfers between devices with their start and end apart: 20, of which 13 were waited for; matrix products, arithmetic and copies ran while one was open for 1% of the time, Pallas kernels for 2%

profile of v4, /device:TPU:25, one launch (start us, length us, event | category | flops | bytes accessed | tf_op | source)
XLA Modules:
  0.0 236.8 jit_solution(10778263972488632412)
XLA Ops:
  0.6 5.6 %edge_strips.1 = (f32[48,272]{1,0:T(8,128)}, f32[48,272]{1,0:T(8,128)}, f32[48,272]{1,0:T(8,128)}, f32[48,272]{1,0:T(8,128)}) custom-call(s32[3,3]{1,0:T(4,128)} %wet.3, f32[270,270]{1,0:T(8,128)} %zd.3, f32[270,270]{1,0:T(8,128)} %zf.3, f32[270,270]{1,0:T(8,128)} %md.3, f32[270,270]{1,0:T(8,128)} %mf.3, f32[270,270]{1,0:T(8,128)} %vm.3, ...), custom_call_target="tpu_custom_call" | custom-call | tf_op jit(solution)/shard_map/edge_strips/pallas_call | solution.py:385
  6.3 4.8 %split_tiles.1 = (f32[16,8,8192]{2,1,0:T(8,128)}, f32[8,8,8192]{2,1,0:T(8,128)}, f32[8,8,8192]{2,1,0:T(8,128)}) custom-call(s32[27]{0:T(128)S(1)} %copy-done.18, f32[27,8,8100]{2,1,0:T(8,128)} %stored.1, f32[48,272]{1,0:T(8,128)} %get-tuple-element.72.after), custom_call_target="tpu_custom_call" | custom-call | tf_op jit(solution)/shard_map/split_tiles/pallas_call | solution.py:222
  12.8 2.8 %collective-permute-done.5.west = f32[48,272]{1,0:T(8,128)S(1)} collective-permute-done((f32[48,272]{1,0:T(8,128)S(1)}, f32[48,272]{1,0:T(8,128)S(1)}, u32[]{:S(2)}, u32[]{:S(2)}) %collective-permute-start.5) | collective-permute-done | bytes 52256 | tf_op jit(solution)/shard_map/ppermute | solution.py:818
  18.9 5.3 %collective-permute-start.7 = (f32[48,384]{1,0:T(8,128)}, f32[48,384]{1,0:T(8,128)S(1)}, u32[]{:S(2)}, u32[]{:S(2)}) collective-permute-start(f32[48,384]{1,0:T(8,128)} %get-tuple-element.82), channel_id=1, source_target_pairs={{0,16},{16,32},{32,48},{48,64},{64,80},{80,96},{96,112},{1,17},{17... | collective-permute-start | bytes 221192 | tf_op jit(solution)/shard_map/ppermute | solution.py:818
  29.7 3.5 %collective-permute-done.8.north = f32[48,384]{1,0:T(8,128)S(1)} collective-permute-done((f32[48,384]{1,0:T(8,128)}, f32[48,384]{1,0:T(8,128)S(1)}, u32[]{:S(2)}, u32[]{:S(2)}) %collective-permute-start.8) | collective-permute-done | bytes 73760 | tf_op jit(solution)/shard_map/ppermute | solution.py:818
  33.8 26.4 %adjoint_window.1 = (f32[2,270,4,270]{3,2,1,0:T(4,128)}, f32[8,3,304,128]{3,2,1,0:T(8,128)}, f32[64,16,128]{2,1,0:T(8,128)}, f32[64,16,128]{2,1,0:T(8,128)}) custom-call(s32[3,3]{1,0:T(4,128)} %wet.3, s32[3,3]{1,0:T(4,128)} %labels.1, s32[1]{0:T(128)} %get-tuple-element.75.clash, f32[270,270]{1,0:T(8,128)} %zd.3, f32[270,270]{1,0:T(8,128)} %zf.3, ...), custom_call_target="tpu_custom_call" | custom-call | tf_op jit(solution)/shard_map/adjoint_window/pallas_call | solution.py:637
  60.2 13.2 %collective-permute-done.9 = f32[64,16,128]{2,1,0:T(8,128)S(1)} collective-permute-done((f32[64,16,128]{2,1,0:T(8,128)}, f32[64,16,128]{2,1,0:T(8,128)S(1)}, u32[]{:S(2)}, u32[]{:S(2)}) %collective-permute-start.9) | collective-permute-done | bytes 524320 | tf_op jit(solution)/shard_map/ppermute | solution.py:822
  74.7 5.2 %collective-permute-done.10 = f32[32,16,128]{2,1,0:T(8,128)S(1)} collective-permute-done((f32[32,16,128]{2,1,0:T(8,128)S(1)}, f32[32,16,128]{2,1,0:T(8,128)S(1)}, u32[]{:S(2)}, u32[]{:S(2)}) %collective-permute-start.10) | collective-permute-done | bytes 262176 | tf_op jit(solution)/shard_map/ppermute | solution.py:822
  80.0 3.3 %collective-permute-start.11 = (f32[16,16,128]{2,1,0:T(8,128)S(1)}, f32[16,16,128]{2,1,0:T(8,128)S(1)}, u32[]{:S(2)}, u32[]{:S(2)}) collective-permute-start(f32[16,16,128]{2,1,0:T(8,128)S(1)} %slice.34), channel_id=1, source_target_pairs={{0,64},{16,80},{32,96},{48,112},{64,0},{80,16},{96,32},{112,48},{1... | collective-permute-start | bytes 393224 | tf_op jit(solution)/shard_map/ppermute | solution.py:822
  83.3 2.4 collective-permute-done.11
  85.7 18.0 %all_to_all.15 = f32[16,16,128]{2,1,0:T(8,128)S(1)} all-to-all(f32[16,16,128]{2,1,0:T(8,128)S(1)} %slice_add_fusion.1), channel_id=1, replica_groups=mesh['lat'=8,'lon'=16] {'lon'}, dimensions={0} | all-to-all | bytes 262144 | tf_op jit(solution)/shard_map/all_to_all | solution.py:851
  103.7 5.0 %all-to-all-start.2 = ((f32[16,8,8192]{2,1,0:T(8,128)}), f32[16,8,8192]{2,1,0:T(8,128)}, u32[]{:S(2)}, u32[]{:S(2)}) async-start(f32[16,8,8192]{2,1,0:T(8,128)} %get-tuple-element.86), calls=%async_computation.2 | async-start | bytes 8388608 | tf_op jit(solution)/shard_map/all_to_all | solution.py:838
  110.1 2.4 %collective-permute-start.13 = (f32[8,8192]{1,0:T(8,128)S(1)}, f32[8,8192]{1,0:T(8,128)S(1)}, u32[]{:S(2)}, u32[]{:S(2)}) collective-permute-start(f32[8,8192]{1,0:T(8,128)S(1)} %copy-done.24), channel_id=1, source_target_pairs={{0,4},{1,5},{2,6},{3,7},{4,0},{5,1},{6,2},{7,3},{8,12},{9,13},{10,... | collective-permute-start | bytes 786440 | tf_op jit(solution)/shard_map/ppermute | solution.py:822
  114.0 55.9 %collective-permute-done.12.refs_1_ = f32[8,8192]{1,0:T(8,128)S(1)} collective-permute-done((f32[8,8192]{1,0:T(8,128)S(1)}, f32[8,8192]{1,0:T(8,128)S(1)}, u32[]{:S(2)}, u32[]{:S(2)}) %collective-permute-start.12) | collective-permute-done | bytes 262176 | tf_op jit(solution)/shard_map/ppermute | solution.py:822
  169.9 2.7 %collective-permute-start.17 = (f32[8,8192]{1,0:T(8,128)S(1)}, f32[8,8192]{1,0:T(8,128)S(1)}, u32[]{:S(2)}, u32[]{:S(2)}) collective-permute-start(f32[8,8192]{1,0:T(8,128)S(1)} %copy-done.20), channel_id=1, source_target_pairs={{0,12},{1,13},{2,14},{3,15},{4,8},{5,9},{6,10},{7,11},{8,4},{9,5},... | collective-permute-start | bytes 786440 | tf_op jit(solution)/shard_map/ppermute | solution.py:822
  172.6 2.9 %collective-permute-done.13.refs_2_ = f32[8,8192]{1,0:T(8,128)S(1)} collective-permute-done((f32[8,8192]{1,0:T(8,128)S(1)}, f32[8,8192]{1,0:T(8,128)S(1)}, u32[]{:S(2)}, u32[]{:S(2)}) %collective-permute-start.13) | collective-permute-done | bytes 262176 | tf_op jit(solution)/shard_map/ppermute | solution.py:822
  176.4 7.3 %collective-permute-done.16.refs_5_ = f32[8,8192]{1,0:T(8,128)S(1)} collective-permute-done((f32[8,8192]{1,0:T(8,128)S(1)}, f32[8,8192]{1,0:T(8,128)S(1)}, u32[]{:S(2)}, u32[]{:S(2)}) %collective-permute-start.16) | collective-permute-done | bytes 262176 | tf_op jit(solution)/shard_map/ppermute | solution.py:822
  183.7 6.0 %collective-permute-done.17.refs_6_ = f32[8,8192]{1,0:T(8,128)S(1)} collective-permute-done((f32[8,8192]{1,0:T(8,128)S(1)}, f32[8,8192]{1,0:T(8,128)S(1)}, u32[]{:S(2)}, u32[]{:S(2)}) %collective-permute-start.17) | collective-permute-done | bytes 262176 | tf_op jit(solution)/shard_map/ppermute | solution.py:822
  190.5 6.8 %unpack_tiles.3 = (f32[8,3,304,128]{3,2,1,0:T(8,128)}, f32[24,272]{1,0:T(8,128)}, f32[24,272]{1,0:T(8,128)}, f32[24,272]{1,0:T(8,128)}, f32[24,272]{1,0:T(8,128)}) custom-call(f32[16,8,8192]{2,1,0:T(8,128)} %all-to-all-done.2.first, f32[8,8192]{1,0:T(8,128)} %get-tuple-element.87.refs_0_, f32[8,8192]{1,0:T(8,128)} %copy-done.4, f32[8,8192]{1,0:T(8,128)} %copy-done.5, ...), custom_call_target="tpu_custom_call" | custom-call | tf_op jit(solution)/shard_map/unpack_tiles/pallas_call | solution.py:736
  197.3 6.3 %collective-permute-start.19 = (f32[24,272]{1,0:T(8,128)}, f32[24,272]{1,0:T(8,128)S(1)}, u32[]{:S(2)}, u32[]{:S(2)}) collective-permute-start(f32[24,272]{1,0:T(8,128)} %get-tuple-element.97), channel_id=1, source_target_pairs={{0,1},{1,2},{2,3},{3,4},{4,5},{5,6},{6,7},{7,8},{8,9},{9,10},{10,1... | collective-permute-start | bytes 78344 | tf_op jit(solution)/shard_map/ppermute | solution.py:818
  208.6 3.3 %collective-permute-start.21 = (f32[24,384]{1,0:T(8,128)}, f32[24,384]{1,0:T(8,128)S(1)}, u32[]{:S(2)}, u32[]{:S(2)}) collective-permute-start(f32[24,384]{1,0:T(8,128)} %get-tuple-element.101), channel_id=1, source_target_pairs={{0,16},{16,32},{32,48},{48,64},{64,80},{80,96},{96,112},{1,17},{17... | collective-permute-start | bytes 110600 | tf_op jit(solution)/shard_map/ppermute | solution.py:818
  215.8 4.7 %collective-permute-done.22 = f32[24,384]{1,0:T(8,128)S(1)} collective-permute-done((f32[24,384]{1,0:T(8,128)}, f32[24,384]{1,0:T(8,128)S(1)}, u32[]{:S(2)}, u32[]{:S(2)}) %collective-permute-start.22) | collective-permute-done | bytes 36896 | tf_op jit(solution)/shard_map/ppermute | solution.py:818
  220.5 14.5 %conditional.1 = (f32[2,270,4,270]{3,2,1,0:T(4,128)S(1)}) conditional(s32[]{:T(128)} %bitcast.3, (f32[8,3,304,128]{3,2,1,0:T(8,128)}, f32[8,3,304,128]{3,2,1,0:T(8,128)}, f32[24,272]{1,0:T(8,128)S(1)}, f32[24,272]{1,0:T(8,128)S(1)}, f32[24,384]{1,0:T(8,128)S(1)}, /*index=5*/f32[24,384]{1,0:T(8,128)S(1)}) %tuple.16, (s32[27]{0:T(128)S(1)}, ...), branch_computations={%region_1.0_spmd, %region_2.0_spmd} | conditional | bytes 17785112 | solution.py:874
  220.5 14.5 %forward_window.2 = f32[2,270,4,270]{3,2,1,0:T(4,128)S(1)} custom-call(f32[8,3,304,128]{3,2,1,0:T(8,128)} %get-tuple-element.14.state, f32[8,3,304,128]{3,2,1,0:T(8,128)} %get-tuple-element.22.coef, f32[24,272]{1,0:T(8,128)S(1)} %get-tuple-element.23.west, f32[24,272]{1,0:T(8,128)S(1)} %get-tuple-element.24.east, f32[24,384]{1,0:T(8,128)S(1)} %get-tuple-element.25.south, ...), custom_call_target="tpu_custom_call" | custom-call | tf_op jit(solution)/shard_map/cond/branch_0_fun/forward_window/pallas_call | solution.py:800
  (85 shorter events, 26.8 us)
Async XLA Ops:
  11.1 15.1 %collective-permute-start.4 = (f32[8,8,8192]{2,1,0:T(8,128)}, f32[8,8,8192]{2,1,0:T(8,128)S(1)}, u32[]{:S(2)}, u32[]{:S(2)}) collective-permute-start(f32[8,8,8192]{2,1,0:T(8,128)} %get-tuple-element.74), channel_id=1, source_target_pairs={{0,1},{1,0},{2,3},{3,2},{4,5},{5,4},{6,7},{7,6},{8,9},{9,8},{10,11... | collective-permute-start | bytes 6291464 | tf_op jit(solution)/shard_map/ppermute | solution.py:822
  11.4 4.2 %collective-permute-start.5 = (f32[48,272]{1,0:T(8,128)S(1)}, f32[48,272]{1,0:T(8,128)S(1)}, u32[]{:S(2)}, u32[]{:S(2)}) collective-permute-start(f32[48,272]{1,0:T(8,128)S(1)} %copy-done.26), channel_id=1, source_target_pairs={{0,1},{1,2},{2,3},{3,4},{4,5},{5,6},{6,7},{7,8},{8,9},{9,10},{10,1... | collective-permute-start | bytes 156680 | tf_op jit(solution)/shard_map/ppermute | solution.py:818
  12.8 3.8 %collective-permute-start.6 = (f32[48,272]{1,0:T(8,128)S(1)}, f32[48,272]{1,0:T(8,128)S(1)}, u32[]{:S(2)}, u32[]{:S(2)}) collective-permute-start(f32[48,272]{1,0:T(8,128)S(1)} %copy-done.15), channel_id=1, source_target_pairs={{1,0},{2,1},{3,2},{4,3},{5,4},{6,5},{7,6},{8,7},{9,8},{10,9},{11,1... | collective-permute-start | bytes 156680 | tf_op jit(solution)/shard_map/ppermute | solution.py:818
  18.9 10.8 %collective-permute-start.7 = (f32[48,384]{1,0:T(8,128)}, f32[48,384]{1,0:T(8,128)S(1)}, u32[]{:S(2)}, u32[]{:S(2)}) collective-permute-start(f32[48,384]{1,0:T(8,128)} %get-tuple-element.82), channel_id=1, source_target_pairs={{0,16},{16,32},{32,48},{48,64},{64,80},{80,96},{96,112},{1,17},{17... | collective-permute-start | bytes 221192 | tf_op jit(solution)/shard_map/ppermute | solution.py:818
  24.3 8.9 %collective-permute-start.8 = (f32[48,384]{1,0:T(8,128)}, f32[48,384]{1,0:T(8,128)S(1)}, u32[]{:S(2)}, u32[]{:S(2)}) collective-permute-start(f32[48,384]{1,0:T(8,128)} %get-tuple-element.83), channel_id=1, source_target_pairs={{16,0},{32,16},{48,32},{64,48},{80,64},{96,80},{112,96},{17,1},{33... | collective-permute-start | bytes 221192 | tf_op jit(solution)/shard_map/ppermute | solution.py:818
  60.2 13.3 %collective-permute-start.9 = (f32[64,16,128]{2,1,0:T(8,128)}, f32[64,16,128]{2,1,0:T(8,128)S(1)}, u32[]{:S(2)}, u32[]{:S(2)}) collective-permute-start(f32[64,16,128]{2,1,0:T(8,128)} %get-tuple-element.85), channel_id=1, source_target_pairs={{0,32},{16,48},{32,0},{48,16},{64,96},{80,112},{96,64},{112,80},{1... | collective-permute-start | bytes 1572872 | tf_op jit(solution)/shard_map/ppermute | solution.py:822
  74.6 5.3 %collective-permute-start.10 = (f32[32,16,128]{2,1,0:T(8,128)S(1)}, f32[32,16,128]{2,1,0:T(8,128)S(1)}, u32[]{:S(2)}, u32[]{:S(2)}) collective-permute-start(f32[32,16,128]{2,1,0:T(8,128)S(1)} %slice.32), channel_id=1, source_target_pairs={{0,16},{16,0},{32,48},{48,32},{64,80},{80,64},{96,112},{112,96},{1... | collective-permute-start | bytes 786440 | tf_op jit(solution)/shard_map/ppermute | solution.py:822
  80.0 5.7 %collective-permute-start.11 = (f32[16,16,128]{2,1,0:T(8,128)S(1)}, f32[16,16,128]{2,1,0:T(8,128)S(1)}, u32[]{:S(2)}, u32[]{:S(2)}) collective-permute-start(f32[16,16,128]{2,1,0:T(8,128)S(1)} %slice.34), channel_id=1, source_target_pairs={{0,64},{16,80},{32,96},{48,112},{64,0},{80,16},{96,32},{112,48},{1... | collective-permute-start | bytes 393224 | tf_op jit(solution)/shard_map/ppermute | solution.py:822
  103.7 66.2 %copy-start.20 = (f32[8,8192]{1,0:T(8,128)S(1)}, f32[8,8192]{1,0:T(8,128)}, u32[]{:S(2)}) copy-start(f32[8,8192]{1,0:T(8,128)} %get-tuple-element.93) | copy-start | bytes 786436
  103.7 71.8 %copy-start.19 = (f32[8,8192]{1,0:T(8,128)S(1)}, f32[8,8192]{1,0:T(8,128)}, u32[]{:S(2)}) copy-start(f32[8,8192]{1,0:T(8,128)} %get-tuple-element.94) | copy-start | bytes 786436
  103.7 85.9 %all-to-all-start.2 = ((f32[16,8,8192]{2,1,0:T(8,128)}), f32[16,8,8192]{2,1,0:T(8,128)}, u32[]{:S(2)}, u32[]{:S(2)}) async-start(f32[16,8,8192]{2,1,0:T(8,128)} %get-tuple-element.86), calls=%async_computation.2 | async-start | bytes 8388608 | tf_op jit(solution)/shard_map/all_to_all | solution.py:838
  108.7 61.2 %collective-permute-start.12 = (f32[8,8192]{1,0:T(8,128)S(1)}, f32[8,8192]{1,0:T(8,128)S(1)}, u32[]{:S(2)}, u32[]{:S(2)}) collective-permute-start(f32[8,8192]{1,0:T(8,128)S(1)} %copy-done.25), channel_id=1, source_target_pairs={{0,2},{1,3},{2,0},{3,1},{4,6},{5,7},{6,4},{7,5},{8,10},{9,11},{10,... | collective-permute-start | bytes 786440 | tf_op jit(solution)/shard_map/ppermute | solution.py:822
  110.1 65.4 %collective-permute-start.13 = (f32[8,8192]{1,0:T(8,128)S(1)}, f32[8,8192]{1,0:T(8,128)S(1)}, u32[]{:S(2)}, u32[]{:S(2)}) collective-permute-start(f32[8,8192]{1,0:T(8,128)S(1)} %copy-done.24), channel_id=1, source_target_pairs={{0,4},{1,5},{2,6},{3,7},{4,0},{5,1},{6,2},{7,3},{8,12},{9,13},{10,... | collective-permute-start | bytes 786440 | tf_op jit(solution)/shard_map/ppermute | solution.py:822
  112.6 63.8 %collective-permute-start.14 = (f32[8,8192]{1,0:T(8,128)S(1)}, f32[8,8192]{1,0:T(8,128)S(1)}, u32[]{:S(2)}, u32[]{:S(2)}) collective-permute-start(f32[8,8192]{1,0:T(8,128)S(1)} %copy-done.23), channel_id=1, source_target_pairs={{0,6},{1,7},{2,4},{3,5},{4,2},{5,3},{6,0},{7,1},{8,14},{9,15},{10,... | collective-permute-start | bytes 786440 | tf_op jit(solution)/shard_map/ppermute | solution.py:822
  112.6 63.7 %collective-permute-start.15 = (f32[8,8192]{1,0:T(8,128)S(1)}, f32[8,8192]{1,0:T(8,128)S(1)}, u32[]{:S(2)}, u32[]{:S(2)}) collective-permute-start(f32[8,8192]{1,0:T(8,128)S(1)} %copy-done.22), channel_id=1, source_target_pairs={{0,8},{1,9},{2,10},{3,11},{4,12},{5,13},{6,14},{7,15},{8,0},{9,1},... | collective-permute-start | bytes 786440 | tf_op jit(solution)/shard_map/ppermute | solution.py:822
  114.0 69.6 %collective-permute-start.16 = (f32[8,8192]{1,0:T(8,128)S(1)}, f32[8,8192]{1,0:T(8,128)S(1)}, u32[]{:S(2)}, u32[]{:S(2)}) collective-permute-start(f32[8,8192]{1,0:T(8,128)S(1)} %copy-done.21), channel_id=1, source_target_pairs={{0,10},{1,11},{2,8},{3,9},{4,14},{5,15},{6,12},{7,13},{8,2},{9,3},... | collective-permute-start | bytes 786440 | tf_op jit(solution)/shard_map/ppermute | solution.py:822
  169.9 19.8 %copy-start.4 = (f32[8,8192]{1,0:T(8,128)}, f32[8,8192]{1,0:T(8,128)S(1)}, u32[]{:S(2)}) copy-start(f32[8,8192]{1,0:T(8,128)S(1)} %collective-permute-done.12.refs_1_) | copy-start | bytes 786436
  169.9 19.7 %collective-permute-start.17 = (f32[8,8192]{1,0:T(8,128)S(1)}, f32[8,8192]{1,0:T(8,128)S(1)}, u32[]{:S(2)}, u32[]{:S(2)}) collective-permute-start(f32[8,8192]{1,0:T(8,128)S(1)} %copy-done.20), channel_id=1, source_target_pairs={{0,12},{1,13},{2,14},{3,15},{4,8},{5,9},{6,10},{7,11},{8,4},{9,5},... | collective-permute-start | bytes 786440 | tf_op jit(solution)/shard_map/ppermute | solution.py:822
  175.5 14.2 %copy-start.5 = (f32[8,8192]{1,0:T(8,128)}, f32[8,8192]{1,0:T(8,128)S(1)}, u32[]{:S(2)}) copy-start(f32[8,8192]{1,0:T(8,128)S(1)} %collective-permute-done.13.refs_2_) | copy-start | bytes 786436
  175.5 14.1 %collective-permute-start.18 = (f32[8,8192]{1,0:T(8,128)S(1)}, f32[8,8192]{1,0:T(8,128)S(1)}, u32[]{:S(2)}, u32[]{:S(2)}) collective-permute-start(f32[8,8192]{1,0:T(8,128)S(1)} %copy-done.19), channel_id=1, source_target_pairs={{0,14},{1,15},{2,12},{3,13},{4,10},{5,11},{6,8},{7,9},{8,6},{9,7},... | collective-permute-start | bytes 786440 | tf_op jit(solution)/shard_map/ppermute | solution.py:822
  197.3 7.7 %collective-permute-start.19 = (f32[24,272]{1,0:T(8,128)}, f32[24,272]{1,0:T(8,128)S(1)}, u32[]{:S(2)}, u32[]{:S(2)}) collective-permute-start(f32[24,272]{1,0:T(8,128)} %get-tuple-element.97), channel_id=1, source_target_pairs={{0,1},{1,2},{2,3},{3,4},{4,5},{5,6},{6,7},{7,8},{8,9},{9,10},{10,1... | collective-permute-start | bytes 78344 | tf_op jit(solution)/shard_map/ppermute | solution.py:818
  203.6 3.6 %collective-permute-start.20 = (f32[24,272]{1,0:T(8,128)}, f32[24,272]{1,0:T(8,128)S(1)}, u32[]{:S(2)}, u32[]{:S(2)}) collective-permute-start(f32[24,272]{1,0:T(8,128)} %get-tuple-element.98), channel_id=1, source_target_pairs={{1,0},{2,1},{3,2},{4,3},{5,4},{6,5},{7,6},{8,7},{9,8},{10,9},{11,1... | collective-permute-start | bytes 78344 | tf_op jit(solution)/shard_map/ppermute | solution.py:818
  208.6 7.2 %collective-permute-start.21 = (f32[24,384]{1,0:T(8,128)}, f32[24,384]{1,0:T(8,128)S(1)}, u32[]{:S(2)}, u32[]{:S(2)}) collective-permute-start(f32[24,384]{1,0:T(8,128)} %get-tuple-element.101), channel_id=1, source_target_pairs={{0,16},{16,32},{32,48},{48,64},{64,80},{80,96},{96,112},{1,17},{17... | collective-permute-start | bytes 110600 | tf_op jit(solution)/shard_map/ppermute | solution.py:818
  212.0 8.5 %collective-permute-start.22 = (f32[24,384]{1,0:T(8,128)}, f32[24,384]{1,0:T(8,128)S(1)}, u32[]{:S(2)}, u32[]{:S(2)}) collective-permute-start(f32[24,384]{1,0:T(8,128)} %get-tuple-element.102), channel_id=1, source_target_pairs={{16,0},{32,16},{48,32},{64,48},{80,64},{96,80},{112,96},{17,1},{33... | collective-permute-start | bytes 110600 | tf_op jit(solution)/shard_map/ppermute | solution.py:818
  (19 other events, 99.9 us)

commit v5 on v4

--- a/solution.py
+++ b/solution.py
@@ -603,8 +603,10 @@
             for p in parts(half):
                 full += jnp.dot(p, by_lane[128 * j : 128 * j + 128], preferred_element_type=F32)
         coarse[t] = full / 9.0
-    owners = keep.shape[0] // 4
+    chips = keep.shape[0] // 8
+    owners = 2 * chips
     here = lax.axis_index("lat")
+    me = lax.axis_index("lon")
     last = lax.broadcasted_iota(I32, (16, 128), 0) == 15
     piece[...] = jnp.where(last, clash[0].astype(F32), 0.0)
     keep[...] = jnp.broadcast_to(piece[...], keep.shape)
@@ -622,13 +624,15 @@
             label = labels[r, c]
             row = label // owners
             away = row ^ here
-            at = ((away & 1) * 2 + (away >> 2)) * owners + label - row * owners
-
-            @pl.when((away & 2) == 0)
+            column = label - row * owners
+            at = ((away & 2) * 2 + (away & 1) * 2 + (away >> 2)) * chips + (column >> 1)
+            other = (column ^ me) & 1
+
+            @pl.when(other == 0)
             def _():
                 keep[at] = piece[...]
 
-            @pl.when((away & 2) != 0)
+            @pl.when(other != 0)
             def _():
                 give[at] = piece[...]
 
@@ -843,12 +847,14 @@
     initial, coef, keep, give = adjoint_window(
         wet_tiles, control_map, clash, *fields, west, east, south, north, owners
     )
+    keep = keep + xor_permute(give, "lon", 1)
     for bit in (2, 1, 4):
-        keep = keep + xor_permute(give, "lat", bit)
         half = keep.shape[0] // 2
-        if bit != 4:
-            keep, give = keep[:half], keep[half:]
-    gathered = lax.all_to_all(keep, "lon", split_axis=0, concat_axis=0, tiled=True)
+        keep = keep[:half] + xor_permute(keep[half:], "lat", bit)
+    parity = [list(range(c, owners, 2)) for c in range(2)]
+    gathered = lax.all_to_all(
+        keep, "lon", split_axis=0, concat_axis=0, axis_index_groups=parity, tiled=True
+    )
     total = jnp.sum(gathered, axis=0)
     clashes = total[15, 0]
     total = total[: COARSE // 2]
@@ -857,21 +863,20 @@
 
     def halos(low, high, bottom, top):
         west, east = neighbours(low, high, "lon", True)
-        return (west, east) + neighbours(*with_corners(bottom, top, west, east), "lat", False)
+        to_south, to_north = with_corners(bottom, top, west, east)
+        return (west, east) + neighbours(to_south, to_north, "lat", False)
 
     state, *strips = unpack_tiles(first, *seconds)
     strips = halos(*strips)
-
-    def ready(ids, stored, coef, state, *strips):
-        return forward_window(state, coef, *strips)
-
-    def complete(ids, stored, coef, state, *strips):
-        outgoing = pack_tiles(ids, stored, coef, owners)
+    final = forward_window(state, coef, *strips)
+
+    def complete(carry):
+        outgoing = pack_tiles(stored_ids, stored_tiles, carry[0], owners)
         arrived = lax.all_to_all(outgoing, "lon", split_axis=0, concat_axis=0, tiled=True)
         state, *strips = unpack_tiles(arrived.reshape(owners * PAIR, 8, FLAT))
-        return forward_window(state, coef, *halos(*strips))
-
-    final = lax.cond(clashes > 0, complete, ready, stored_ids, stored_tiles, coef, state, *strips)
+        return forward_window(state, coef, *halos(*strips)), jnp.float32(0)
+
+    final, _ = lax.while_loop(lambda carry: carry[1] > 0, complete, (final, clashes))
     return final.transpose(0, 2, 1, 3), initial.transpose(0, 2, 1, 3), control
 
 

time: 237 us -> 236 us (level)
  the two profiles are of different devices: /device:TPU:25 before, /device:TPU:24 now
where the time goes in v5:
time: 236 us; the launch traced here: 235 us
  waiting for transfers between devices  114 us (48%)
  Pallas kernels  63.3 us (27%)
  starting transfers between devices  38.3 us (16%)
  blocking collectives  8.73 us (4%)
  local copies, waits for them, and re-layouts  7.69 us (3%)
    ppermute x12, waiting for transfers between devices, xor_permute(): lax.ppermute(x, axis, [(i, i ^ bits) for i in range(lax.axis_size(axis))])  97.2 us
    pallas_call x1, Pallas kernels, adjoint_window(): pl.pallas_call(adjoint_kernel, out_shape=(jax.ShapeDtypeStruct((2, N, LEV...  26.4 us
    ppermute x8, starting transfers between devices, neighbours(): return (lax.ppermute(high, axis, up), lax.ppermute(low, axis, down))  22.5 us
    ppermute x8, waiting for transfers between devices, neighbours(): return (lax.ppermute(high, axis, up), lax.ppermute(low, axis, down))  17.1 us
    pallas_call x1, Pallas kernels, forward_window(): pl.pallas_call(forward_kernel, out_shape=jax.ShapeDtypeStruct((2, N, LEV,...  14.6 us
    ppermute x12, starting transfers between devices, xor_permute(): lax.ppermute(x, axis, [(i, i ^ bits) for i in range(lax.axis_size(axis))])  11.1 us
    all_to_all x1, blocking collectives, per_device(): lax.all_to_all(keep, 'lon', split_axis=0, concat_axis=0, axis_index_group...  8.73 us
    pallas_call x1, Pallas kernels, unpack_tiles(): pl.pallas_call(functools.partial(unpack_kernel, extra), out_shape=(jax.Sh...  6.86 us
  transfers between devices with their start and end apart: 21, of which 14 were waited for; matrix products, arithmetic and copies ran while one was open for 1% of the time, Pallas kernels for 2%

profile of v5, /device:TPU:24, one launch (start us, length us, event | category | flops | bytes accessed | tf_op | source)
XLA Modules:
  0.0 234.9 jit_solution(12773739257207300056)
XLA Ops:
  0.6 5.6 %edge_strips.1 = (f32[48,272]{1,0:T(8,128)}, f32[48,272]{1,0:T(8,128)}, f32[48,272]{1,0:T(8,128)}, f32[48,272]{1,0:T(8,128)}) custom-call(s32[3,3]{1,0:T(4,128)} %wet.3, f32[270,270]{1,0:T(8,128)} %zd.3, f32[270,270]{1,0:T(8,128)} %zf.3, f32[270,270]{1,0:T(8,128)} %md.3, f32[270,270]{1,0:T(8,128)} %mf.3, f32[270,270]{1,0:T(8,128)} %vm.3, ...), custom_call_target="tpu_custom_call" | custom-call | tf_op jit(solution)/shard_map/edge_strips/pallas_call | solution.py:385
  6.3 4.4 %split_tiles.1 = (f32[16,8,8192]{2,1,0:T(8,128)}, f32[8,8,8192]{2,1,0:T(8,128)}, f32[8,8,8192]{2,1,0:T(8,128)}) custom-call(s32[27]{0:T(128)S(1)} %copy-done.22, f32[27,8,8100]{2,1,0:T(8,128)} %stored.1, f32[48,272]{1,0:T(8,128)} %get-tuple-element.68.after), custom_call_target="tpu_custom_call" | custom-call | tf_op jit(solution)/shard_map/split_tiles/pallas_call | solution.py:222
  11.0 6.7 %collective-permute-start.5 = (f32[48,272]{1,0:T(8,128)S(1)}, f32[48,272]{1,0:T(8,128)S(1)}, u32[]{:S(2)}, u32[]{:S(2)}) collective-permute-start(f32[48,272]{1,0:T(8,128)S(1)} %copy-done.19), channel_id=1, source_target_pairs={{1,0},{2,1},{3,2},{4,3},{5,4},{6,5},{7,6},{8,7},{9,8},{10,9},{11,1... | collective-permute-start | bytes 156680 | tf_op jit(solution)/shard_map/ppermute | solution.py:822
  19.7 3.9 %collective-permute-done.4.west = f32[48,272]{1,0:T(8,128)S(1)} collective-permute-done((f32[48,272]{1,0:T(8,128)S(1)}, f32[48,272]{1,0:T(8,128)S(1)}, u32[]{:S(2)}, u32[]{:S(2)}) %collective-permute-start.4) | collective-permute-done | bytes 52256 | tf_op jit(solution)/shard_map/ppermute | solution.py:822
  26.0 2.2 collective-permute-start.14
  28.2 3.6 %collective-permute-start.15 = (f32[48,384]{1,0:T(8,128)}, f32[48,384]{1,0:T(8,128)S(1)}, u32[]{:S(2)}, u32[]{:S(2)}) collective-permute-start(f32[48,384]{1,0:T(8,128)} %get-tuple-element.89), channel_id=1, source_target_pairs={{16,0},{32,16},{48,32},{64,48},{80,64},{96,80},{112,96},{17,1},{33... | collective-permute-start | bytes 221192 | tf_op jit(solution)/shard_map/ppermute | solution.py:822
  35.3 3.0 %collective-permute-done.15.north = f32[48,384]{1,0:T(8,128)S(1)} collective-permute-done((f32[48,384]{1,0:T(8,128)}, f32[48,384]{1,0:T(8,128)S(1)}, u32[]{:S(2)}, u32[]{:S(2)}) %collective-permute-start.15) | collective-permute-done | bytes 73760 | tf_op jit(solution)/shard_map/ppermute | solution.py:822
  38.9 26.4 %adjoint_window.1 = (f32[2,270,4,270]{3,2,1,0:T(4,128)}, f32[8,3,304,128]{3,2,1,0:T(8,128)}, f32[64,16,128]{2,1,0:T(8,128)}, f32[64,16,128]{2,1,0:T(8,128)}) custom-call(s32[3,3]{1,0:T(4,128)} %wet.3, s32[3,3]{1,0:T(4,128)} %labels.1, s32[1]{0:T(128)} %get-tuple-element.83.clash, f32[270,270]{1,0:T(8,128)} %zd.3, f32[270,270]{1,0:T(8,128)} %zf.3, ...), custom_call_target="tpu_custom_call" | custom-call | tf_op jit(solution)/shard_map/adjoint_window/pallas_call | solution.py:641
  68.7 9.8 %collective-permute-done.21 = f32[32,16,128]{2,1,0:T(8,128)S(1)} collective-permute-done((f32[32,16,128]{2,1,0:T(8,128)S(1)}, f32[32,16,128]{2,1,0:T(8,128)S(1)}, u32[]{:S(2)}, u32[]{:S(2)}) %collective-permute-start.21) | collective-permute-done | bytes 262176 | tf_op jit(solution)/shard_map/ppermute | solution.py:826
  78.7 5.0 %collective-permute-done.22 = f32[16,16,128]{2,1,0:T(8,128)S(1)} collective-permute-done((f32[16,16,128]{2,1,0:T(8,128)S(1)}, f32[16,16,128]{2,1,0:T(8,128)S(1)}, u32[]{:S(2)}, u32[]{:S(2)}) %collective-permute-start.22) | collective-permute-done | bytes 131104 | tf_op jit(solution)/shard_map/ppermute | solution.py:826
  83.8 5.8 %collective-permute-done.23 = f32[8,16,128]{2,1,0:T(8,128)S(1)} collective-permute-done((f32[8,16,128]{2,1,0:T(8,128)S(1)}, f32[8,16,128]{2,1,0:T(8,128)S(1)}, u32[]{:S(2)}, u32[]{:S(2)}) %collective-permute-start.23) | collective-permute-done | bytes 65568 | tf_op jit(solution)/shard_map/ppermute | solution.py:826
  89.5 8.7 %all_to_all.15 = f32[8,16,128]{2,1,0:T(8,128)S(1)} all-to-all(f32[8,16,128]{2,1,0:T(8,128)S(1)} %slice_add_fusion.2), channel_id=1, replica_groups={{0,2,4,6,8,10,12,14},{1,3,5,7,9,11,13,15},{16,18,20,22,24,26,28,30},{17..., dimensions={0} | all-to-all | bytes 131072 | tf_op jit(solution)/shard_map/all_to_all | solution.py:855
  98.3 4.7 %all-to-all-start.1 = ((f32[16,8,8192]{2,1,0:T(8,128)}), f32[16,8,8192]{2,1,0:T(8,128)}, u32[]{:S(2)}, u32[]{:S(2)}) async-start(f32[16,8,8192]{2,1,0:T(8,128)} %get-tuple-element.71), calls=%async_computation.1 | async-start | bytes 8388608 | tf_op jit(solution)/shard_map/all_to_all | solution.py:842
  106.3 3.7 %collective-permute-start.12 = (f32[8,8192]{1,0:T(8,128)S(1)}, f32[8,8192]{1,0:T(8,128)S(1)}, u32[]{:S(2)}, u32[]{:S(2)}) collective-permute-start(f32[8,8192]{1,0:T(8,128)S(1)} %copy-done.27), channel_id=1, source_target_pairs={{0,12},{1,13},{2,14},{3,15},{4,8},{5,9},{6,10},{7,11},{8,4},{9,5},... | collective-permute-start | bytes 786440 | tf_op jit(solution)/shard_map/ppermute | solution.py:826
  110.7 62.7 %collective-permute-done.10.refs_4_ = f32[8,8192]{1,0:T(8,128)S(1)} collective-permute-done((f32[8,8192]{1,0:T(8,128)S(1)}, f32[8,8192]{1,0:T(8,128)S(1)}, u32[]{:S(2)}, u32[]{:S(2)}) %collective-permute-start.10) | collective-permute-done | bytes 262176 | tf_op jit(solution)/shard_map/ppermute | solution.py:826
  173.4 2.8 %collective-permute-start.9 = (f32[8,8192]{1,0:T(8,128)S(1)}, f32[8,8192]{1,0:T(8,128)S(1)}, u32[]{:S(2)}, u32[]{:S(2)}) collective-permute-start(f32[8,8192]{1,0:T(8,128)S(1)} %copy-done.23), channel_id=1, source_target_pairs={{0,6},{1,7},{2,4},{3,5},{4,2},{5,3},{6,0},{7,1},{8,14},{9,15},{10,... | collective-permute-start | bytes 786440 | tf_op jit(solution)/shard_map/ppermute | solution.py:826
  176.3 4.1 %collective-permute-done.7.refs_1_ = f32[8,8192]{1,0:T(8,128)S(1)} collective-permute-done((f32[8,8192]{1,0:T(8,128)S(1)}, f32[8,8192]{1,0:T(8,128)S(1)}, u32[]{:S(2)}, u32[]{:S(2)}) %collective-permute-start.7) | collective-permute-done | bytes 262176 | tf_op jit(solution)/shard_map/ppermute | solution.py:826
  180.4 5.4 %collective-permute-done.8.refs_2_ = f32[8,8192]{1,0:T(8,128)S(1)} collective-permute-done((f32[8,8192]{1,0:T(8,128)S(1)}, f32[8,8192]{1,0:T(8,128)S(1)}, u32[]{:S(2)}, u32[]{:S(2)}) %collective-permute-start.8) | collective-permute-done | bytes 262176 | tf_op jit(solution)/shard_map/ppermute | solution.py:826
  185.7 2.3 collective-permute-done.9.refs_3_
  188.8 6.9 %unpack_tiles.3 = (f32[8,3,304,128]{3,2,1,0:T(8,128)}, f32[24,272]{1,0:T(8,128)}, f32[24,272]{1,0:T(8,128)}, f32[24,272]{1,0:T(8,128)}, f32[24,272]{1,0:T(8,128)}) custom-call(f32[16,8,8192]{2,1,0:T(8,128)} %all-to-all-done.1.first, f32[8,8192]{1,0:T(8,128)} %get-tuple-element.74.refs_0_, f32[8,8192]{1,0:T(8,128)} %copy-done.12, f32[8,8192]{1,0:T(8,128)} %copy-done.13, ...), custom_call_target="tpu_custom_call" | custom-call | tf_op jit(solution)/shard_map/unpack_tiles/pallas_call | solution.py:740
  195.8 3.8 %collective-permute-start.17 = (f32[24,272]{1,0:T(8,128)}, f32[24,272]{1,0:T(8,128)S(1)}, u32[]{:S(2)}, u32[]{:S(2)}) collective-permute-start(f32[24,272]{1,0:T(8,128)} %get-tuple-element.92), channel_id=1, source_target_pairs={{1,0},{2,1},{3,2},{4,3},{5,4},{6,5},{7,6},{8,7},{9,8},{10,9},{11,1... | collective-permute-start | bytes 78344 | tf_op jit(solution)/shard_map/ppermute | solution.py:822
  203.7 4.1 %collective-permute-start.18 = (f32[24,384]{1,0:T(8,128)}, f32[24,384]{1,0:T(8,128)S(1)}, u32[]{:S(2)}, u32[]{:S(2)}) collective-permute-start(f32[24,384]{1,0:T(8,128)} %get-tuple-element.95), channel_id=1, source_target_pairs={{0,16},{16,32},{32,48},{48,64},{64,80},{80,96},{96,112},{1,17},{17... | collective-permute-start | bytes 110600 | tf_op jit(solution)/shard_map/ppermute | solution.py:822
  211.0 6.5 %collective-permute-done.19.north = f32[24,384]{1,0:T(8,128)S(1)} collective-permute-done((f32[24,384]{1,0:T(8,128)}, f32[24,384]{1,0:T(8,128)S(1)}, u32[]{:S(2)}, u32[]{:S(2)}) %collective-permute-start.19) | collective-permute-done | bytes 36896 | tf_op jit(solution)/shard_map/ppermute | solution.py:822
  218.1 14.6 %forward_window.3 = f32[2,270,4,270]{3,2,1,0:T(4,128)S(1)} custom-call(f32[8,3,304,128]{3,2,1,0:T(8,128)} %get-tuple-element.82.state, f32[8,3,304,128]{3,2,1,0:T(8,128)} %get-tuple-element.122.coef, f32[24,272]{1,0:T(8,128)} %copy-done.15, f32[24,272]{1,0:T(8,128)} %copy-done.16, f32[24,384]{1,0:T(8,128)} %copy-done.20, f32[24,384]{1,0:T(8,128)} %copy-done.21), custom_call_target="tpu_custom_call" | custom-call | tf_op jit(solution)/shard_map/forward_window/pallas_call | solution.py:804
  (97 shorter events, 27.3 us)
Async XLA Ops:
  10.7 21.2 %collective-permute-start.6 = (f32[8,8,8192]{2,1,0:T(8,128)}, f32[8,8,8192]{2,1,0:T(8,128)S(1)}, u32[]{:S(2)}, u32[]{:S(2)}) collective-permute-start(f32[8,8,8192]{2,1,0:T(8,128)} %get-tuple-element.73), channel_id=1, source_target_pairs={{0,1},{1,0},{2,3},{3,2},{4,5},{5,4},{6,7},{7,6},{8,9},{9,8},{10,11... | collective-permute-start | bytes 6291464 | tf_op jit(solution)/shard_map/ppermute | solution.py:826
  11.0 8.7 %collective-permute-start.5 = (f32[48,272]{1,0:T(8,128)S(1)}, f32[48,272]{1,0:T(8,128)S(1)}, u32[]{:S(2)}, u32[]{:S(2)}) collective-permute-start(f32[48,272]{1,0:T(8,128)S(1)} %copy-done.19), channel_id=1, source_target_pairs={{1,0},{2,1},{3,2},{4,3},{5,4},{6,5},{7,6},{8,7},{9,8},{10,9},{11,1... | collective-permute-start | bytes 156680 | tf_op jit(solution)/shard_map/ppermute | solution.py:822
  17.8 5.9 %collective-permute-start.4 = (f32[48,272]{1,0:T(8,128)S(1)}, f32[48,272]{1,0:T(8,128)S(1)}, u32[]{:S(2)}, u32[]{:S(2)}) collective-permute-start(f32[48,272]{1,0:T(8,128)S(1)} %copy-done.30), channel_id=1, source_target_pairs={{0,1},{1,2},{2,3},{3,4},{4,5},{5,6},{6,7},{7,8},{8,9},{9,10},{10,1... | collective-permute-start | bytes 156680 | tf_op jit(solution)/shard_map/ppermute | solution.py:822
  26.0 9.3 %collective-permute-start.14 = (f32[48,384]{1,0:T(8,128)}, f32[48,384]{1,0:T(8,128)S(1)}, u32[]{:S(2)}, u32[]{:S(2)}) collective-permute-start(f32[48,384]{1,0:T(8,128)} %get-tuple-element.88), channel_id=1, source_target_pairs={{0,16},{16,32},{32,48},{48,64},{64,80},{80,96},{96,112},{1,17},{17... | collective-permute-start | bytes 221192 | tf_op jit(solution)/shard_map/ppermute | solution.py:822
  28.2 10.1 %collective-permute-start.15 = (f32[48,384]{1,0:T(8,128)}, f32[48,384]{1,0:T(8,128)S(1)}, u32[]{:S(2)}, u32[]{:S(2)}) collective-permute-start(f32[48,384]{1,0:T(8,128)} %get-tuple-element.89), channel_id=1, source_target_pairs={{16,0},{32,16},{48,32},{64,48},{80,64},{96,80},{112,96},{17,1},{33... | collective-permute-start | bytes 221192 | tf_op jit(solution)/shard_map/ppermute | solution.py:822
  65.3 2.1 collective-permute-start.20
  68.6 9.9 %collective-permute-start.21 = (f32[32,16,128]{2,1,0:T(8,128)S(1)}, f32[32,16,128]{2,1,0:T(8,128)S(1)}, u32[]{:S(2)}, u32[]{:S(2)}) collective-permute-start(f32[32,16,128]{2,1,0:T(8,128)S(1)} %slice.40), channel_id=1, source_target_pairs={{0,32},{16,48},{32,0},{48,16},{64,96},{80,112},{96,64},{112,80},{1... | collective-permute-start | bytes 786440 | tf_op jit(solution)/shard_map/ppermute | solution.py:826
  78.6 5.0 %collective-permute-start.22 = (f32[16,16,128]{2,1,0:T(8,128)S(1)}, f32[16,16,128]{2,1,0:T(8,128)S(1)}, u32[]{:S(2)}, u32[]{:S(2)}) collective-permute-start(f32[16,16,128]{2,1,0:T(8,128)S(1)} %slice.42), channel_id=1, source_target_pairs={{0,16},{16,0},{32,48},{48,32},{64,80},{80,64},{96,112},{112,96},{1... | collective-permute-start | bytes 393224 | tf_op jit(solution)/shard_map/ppermute | solution.py:826
  83.7 5.8 %collective-permute-start.23 = (f32[8,16,128]{2,1,0:T(8,128)S(1)}, f32[8,16,128]{2,1,0:T(8,128)S(1)}, u32[]{:S(2)}, u32[]{:S(2)}) collective-permute-start(f32[8,16,128]{2,1,0:T(8,128)S(1)} %slice.44), channel_id=1, source_target_pairs={{0,64},{16,80},{32,96},{48,112},{64,0},{80,16},{96,32},{112,48},{1... | collective-permute-start | bytes 196616 | tf_op jit(solution)/shard_map/ppermute | solution.py:826
  98.3 75.1 %copy-start.24 = (f32[8,8192]{1,0:T(8,128)S(1)}, f32[8,8192]{1,0:T(8,128)}, u32[]{:S(2)}) copy-start(f32[8,8192]{1,0:T(8,128)} %get-tuple-element.76) | copy-start | bytes 786436
  98.3 75.1 %copy-start.23 = (f32[8,8192]{1,0:T(8,128)S(1)}, f32[8,8192]{1,0:T(8,128)}, u32[]{:S(2)}) copy-start(f32[8,8192]{1,0:T(8,128)} %get-tuple-element.77) | copy-start | bytes 786436
  98.3 89.8 %all-to-all-start.1 = ((f32[16,8,8192]{2,1,0:T(8,128)}), f32[16,8,8192]{2,1,0:T(8,128)}, u32[]{:S(2)}, u32[]{:S(2)}) async-start(f32[16,8,8192]{2,1,0:T(8,128)} %get-tuple-element.71), calls=%async_computation.1 | async-start | bytes 8388608 | tf_op jit(solution)/shard_map/all_to_all | solution.py:842
  103.0 70.4 %collective-permute-start.10 = (f32[8,8192]{1,0:T(8,128)S(1)}, f32[8,8192]{1,0:T(8,128)S(1)}, u32[]{:S(2)}, u32[]{:S(2)}) collective-permute-start(f32[8,8192]{1,0:T(8,128)S(1)} %copy-done.29), channel_id=1, source_target_pairs={{0,8},{1,9},{2,10},{3,11},{4,12},{5,13},{6,14},{7,15},{8,0},{9,1},... | collective-permute-start | bytes 786440 | tf_op jit(solution)/shard_map/ppermute | solution.py:826
  104.9 68.5 %collective-permute-start.11 = (f32[8,8192]{1,0:T(8,128)S(1)}, f32[8,8192]{1,0:T(8,128)S(1)}, u32[]{:S(2)}, u32[]{:S(2)}) collective-permute-start(f32[8,8192]{1,0:T(8,128)S(1)} %copy-done.28), channel_id=1, source_target_pairs={{0,10},{1,11},{2,8},{3,9},{4,14},{5,15},{6,12},{7,13},{8,2},{9,3},... | collective-permute-start | bytes 786440 | tf_op jit(solution)/shard_map/ppermute | solution.py:826
  106.3 69.9 %collective-permute-start.12 = (f32[8,8192]{1,0:T(8,128)S(1)}, f32[8,8192]{1,0:T(8,128)S(1)}, u32[]{:S(2)}, u32[]{:S(2)}) collective-permute-start(f32[8,8192]{1,0:T(8,128)S(1)} %copy-done.27), channel_id=1, source_target_pairs={{0,12},{1,13},{2,14},{3,15},{4,8},{5,9},{6,10},{7,11},{8,4},{9,5},... | collective-permute-start | bytes 786440 | tf_op jit(solution)/shard_map/ppermute | solution.py:826
  110.0 66.3 %collective-permute-start.13 = (f32[8,8192]{1,0:T(8,128)S(1)}, f32[8,8192]{1,0:T(8,128)S(1)}, u32[]{:S(2)}, u32[]{:S(2)}) collective-permute-start(f32[8,8192]{1,0:T(8,128)S(1)} %copy-done.26), channel_id=1, source_target_pairs={{0,14},{1,15},{2,12},{3,13},{4,10},{5,11},{6,8},{7,9},{8,6},{9,7},... | collective-permute-start | bytes 786440 | tf_op jit(solution)/shard_map/ppermute | solution.py:826
  110.2 70.2 %collective-permute-start.7 = (f32[8,8192]{1,0:T(8,128)S(1)}, f32[8,8192]{1,0:T(8,128)S(1)}, u32[]{:S(2)}, u32[]{:S(2)}) collective-permute-start(f32[8,8192]{1,0:T(8,128)S(1)} %copy-done.25), channel_id=1, source_target_pairs={{0,2},{1,3},{2,0},{3,1},{4,6},{5,7},{6,4},{7,5},{8,10},{9,11},{10,... | collective-permute-start | bytes 786440 | tf_op jit(solution)/shard_map/ppermute | solution.py:826
  173.4 14.7 %copy-start.8 = (f32[8,8192]{1,0:T(8,128)}, f32[8,8192]{1,0:T(8,128)S(1)}, u32[]{:S(2)}) copy-start(f32[8,8192]{1,0:T(8,128)S(1)} %collective-permute-done.10.refs_4_) | copy-start | bytes 786436
  173.4 12.3 %collective-permute-start.8 = (f32[8,8192]{1,0:T(8,128)S(1)}, f32[8,8192]{1,0:T(8,128)S(1)}, u32[]{:S(2)}, u32[]{:S(2)}) collective-permute-start(f32[8,8192]{1,0:T(8,128)S(1)} %copy-done.24), channel_id=1, source_target_pairs={{0,4},{1,5},{2,6},{3,7},{4,0},{5,1},{6,2},{7,3},{8,12},{9,13},{10,... | collective-permute-start | bytes 786440 | tf_op jit(solution)/shard_map/ppermute | solution.py:826
  173.4 14.7 %collective-permute-start.9 = (f32[8,8192]{1,0:T(8,128)S(1)}, f32[8,8192]{1,0:T(8,128)S(1)}, u32[]{:S(2)}, u32[]{:S(2)}) collective-permute-start(f32[8,8192]{1,0:T(8,128)S(1)} %copy-done.23), channel_id=1, source_target_pairs={{0,6},{1,7},{2,4},{3,5},{4,2},{5,3},{6,0},{7,1},{8,14},{9,15},{10,... | collective-permute-start | bytes 786440 | tf_op jit(solution)/shard_map/ppermute | solution.py:826
  195.7 5.8 %collective-permute-start.16 = (f32[24,272]{1,0:T(8,128)}, f32[24,272]{1,0:T(8,128)S(1)}, u32[]{:S(2)}, u32[]{:S(2)}) collective-permute-start(f32[24,272]{1,0:T(8,128)} %get-tuple-element.91), channel_id=1, source_target_pairs={{0,1},{1,2},{2,3},{3,4},{4,5},{5,6},{6,7},{7,8},{8,9},{9,10},{10,1... | collective-permute-start | bytes 78344 | tf_op jit(solution)/shard_map/ppermute | solution.py:822
  195.8 5.8 %collective-permute-start.17 = (f32[24,272]{1,0:T(8,128)}, f32[24,272]{1,0:T(8,128)S(1)}, u32[]{:S(2)}, u32[]{:S(2)}) collective-permute-start(f32[24,272]{1,0:T(8,128)} %get-tuple-element.92), channel_id=1, source_target_pairs={{1,0},{2,1},{3,2},{4,3},{5,4},{6,5},{7,6},{8,7},{9,8},{10,9},{11,1... | collective-permute-start | bytes 78344 | tf_op jit(solution)/shard_map/ppermute | solution.py:822
  203.7 7.3 %collective-permute-start.18 = (f32[24,384]{1,0:T(8,128)}, f32[24,384]{1,0:T(8,128)S(1)}, u32[]{:S(2)}, u32[]{:S(2)}) collective-permute-start(f32[24,384]{1,0:T(8,128)} %get-tuple-element.95), channel_id=1, source_target_pairs={{0,16},{16,32},{32,48},{48,64},{64,80},{80,96},{96,112},{1,17},{17... | collective-permute-start | bytes 110600 | tf_op jit(solution)/shard_map/ppermute | solution.py:822
  207.8 9.7 %collective-permute-start.19 = (f32[24,384]{1,0:T(8,128)}, f32[24,384]{1,0:T(8,128)S(1)}, u32[]{:S(2)}, u32[]{:S(2)}) collective-permute-start(f32[24,384]{1,0:T(8,128)} %get-tuple-element.96), channel_id=1, source_target_pairs={{16,0},{32,16},{48,32},{64,48},{80,64},{96,80},{112,96},{17,1},{33... | collective-permute-start | bytes 110600 | tf_op jit(solution)/shard_map/ppermute | solution.py:822
  (24 other events, 133.7 us)

commit v6 on v5

--- a/solution.py
+++ b/solution.py
@@ -137,7 +137,7 @@
     )(ids, stored, after)
 
 
-def split_kernel(ids, stored, after, first, own, cross, held, tail, empty, count, route, filled, in_sem, out_sem, tail_sem, empty_sem):
+def split_kernel(edges, ids, stored, first, own, cross, held, tail, empty, count, route, filled, in_sem, out_sem, tail_sem, empty_sem):
     owners = first.shape[0]
     chips = own.shape[0]
     me = lax.axis_index("lon")
@@ -180,6 +180,7 @@
         for kind in range(3):
             filled[kind, o] = 0
 
+    edges()
     empty[...] = jnp.full((8, 128), -1.0, F32)
     lane = lax.broadcasted_iota(I32, (8, 128), 1)
 
@@ -215,29 +216,6 @@
             each(s, lambda copy: copy.wait())
 
     each_empty(lambda copy: copy.wait())
-
-
-def split_tiles(ids, stored, after, owners):
-    chips = owners // 2
-    return pl.pallas_call(
-        split_kernel,
-        out_shape=tuple(jax.ShapeDtypeStruct((n, 8, FLAT), F32) for n in (owners, chips, chips)),
-        in_specs=[SMEM, ANY, ANY],
-        out_specs=(ANY,) * 3,
-        scratch_shapes=[
-            pltpu.VMEM((SLOTS, 8, CELLS), F32),
-            pltpu.VMEM((SLOTS, 8, 128), F32),
-            pltpu.VMEM((8, 128), F32),
-            pltpu.SMEM((owners,), I32),
-            pltpu.SMEM((SLOTS, 2), I32),
-            pltpu.SMEM((3, owners), I32),
-            pltpu.SemaphoreType.DMA((SLOTS,)),
-            pltpu.SemaphoreType.DMA((SLOTS,)),
-            pltpu.SemaphoreType.DMA((SLOTS,)),
-            pltpu.SemaphoreType.DMA((3, owners)),
-        ],
-        name="split_tiles",
-    )(ids, stored, after)
 
 
 def merge_kernel(own, cross, *refs):
@@ -379,17 +357,36 @@
     east[...] = strip_columns(high, 16, N - HALO - 256)
 
 
-def edge_strips(wet, zd, zf, md, mf, vm, forcing, adjoint):
-    columns = jax.ShapeDtypeStruct((48, N + 2), F32)
-    rows = jax.ShapeDtypeStruct((48, N + 2), F32)
+def head_kernel(ids, stored, *refs):
+    inputs, strips, tiles = refs[:8], refs[8:12], refs[12:15]
+    edge_scratch, scratch = refs[15], refs[16:]
+    split_kernel(lambda: edges_kernel(*inputs, *strips, edge_scratch), ids, stored, *tiles, *scratch)
+
+
+def strips_and_tiles(ids, stored, owners, *fields):
+    chips = owners // 2
+    strip = jax.ShapeDtypeStruct((48, N + 2), F32)
     return pl.pallas_call(
-        edges_kernel,
-        out_shape=(columns, columns, rows, rows),
-        in_specs=[SMEM] + [VMEM] * 7,
-        out_specs=(VMEM,) * 4,
-        scratch_shapes=[pltpu.VMEM((2, 16, N + 2, 128), F32)],
-        name="edge_strips",
-    )(wet, zd, zf, md, mf, vm, forcing, adjoint)
+        head_kernel,
+        out_shape=(strip,) * 4
+        + tuple(jax.ShapeDtypeStruct((n, 8, FLAT), F32) for n in (owners, chips, chips)),
+        in_specs=[SMEM, ANY, SMEM] + [VMEM] * 7,
+        out_specs=(VMEM,) * 4 + (ANY,) * 3,
+        scratch_shapes=[
+            pltpu.VMEM((2, 16, N + 2, 128), F32),
+            pltpu.VMEM((SLOTS, 8, CELLS), F32),
+            pltpu.VMEM((SLOTS, 8, 128), F32),
+            pltpu.VMEM((8, 128), F32),
+            pltpu.SMEM((owners,), I32),
+            pltpu.SMEM((SLOTS, 2), I32),
+            pltpu.SMEM((3, owners), I32),
+            pltpu.SemaphoreType.DMA((SLOTS,)),
+            pltpu.SemaphoreType.DMA((SLOTS,)),
+            pltpu.SemaphoreType.DMA((SLOTS,)),
+            pltpu.SemaphoreType.DMA((3, owners)),
+        ],
+        name="strips_and_tiles",
+    )(ids, stored, *fields)
 
 
 def corners_kernel(south, north, west, east, to_south, to_north):
@@ -755,7 +752,7 @@
     )(first, *seconds)
 
 
-def forward_kernel(state, coef, west, east, south, north, final, first, second, sem):
+def forward_kernel(state, coef, west, east, south, north, out, first, second, final, sem, out_sem):
     copy = pltpu.make_async_copy(state, first, sem)
     copy.start()
     copy.wait()
@@ -791,28 +788,67 @@
 
         stencil(first, b, load_coef(b), take)
 
-    @pl.loop(0, N // 16)
-    def _(i):
-        finish(2 * i, 8)
-        finish(2 * i + 1, 8)
-
-    finish(N // 8 - 1, 8)
-    finish(N // 8, N % 8)
+    cuts = (0, 96, 192, N)
+    copies = []
+    for part, (low, high) in enumerate(zip(cuts, cuts[1:])):
+        pairs = high // 16 - low // 16
+
+        @pl.loop(0, pairs)
+        def _(i):
+            finish(low // 8 + 2 * i, 8)
+            finish(low // 8 + 2 * i + 1, 8)
+
+        if high == N:
+            finish(N // 8 - 1, 8)
+            finish(N // 8, N % 8)
+        rows = pl.ds(low, high - low)
+        copies.append(pltpu.make_async_copy(final.at[:, rows], out.at[:, rows], out_sem.at[part]))
+        copies[-1].start()
+    for copy in copies:
+        copy.wait()
 
 
 def forward_window(state, coef, west, east, south, north):
+    shape = (2, N, LEV, N)
     return pl.pallas_call(
         forward_kernel,
-        out_shape=jax.ShapeDtypeStruct((2, N, LEV, N), F32),
+        out_shape=jax.ShapeDtypeStruct(shape, F32),
         in_specs=[ANY] + [VMEM] * 5,
-        out_specs=VMEM,
+        out_specs=ANY,
         scratch_shapes=[
             pltpu.VMEM((8, 3, ROWS, 128), F32),
             pltpu.VMEM((8, 3, ROWS, 128), F32),
+            pltpu.VMEM(shape, F32),
             pltpu.SemaphoreType.DMA,
+            pltpu.SemaphoreType.DMA((3,)),
         ],
         name="forward_window",
+        compiler_params=pltpu.CompilerParams(vmem_limit_bytes=67043328),
     )(state, coef, west, east, south, north)
+
+
+def control_kernel(gathered, control, clash):
+    total = jnp.sum(gathered[...], axis=0)
+    part = COARSE // 2
+    for i in range(part):
+        for h in range(2):
+            for t in range(2):
+                at = part * COARSE * h + COARSE * i
+                lane = 64 * h + COARSE * t
+                control[0, t : t + 1, at : at + COARSE] = total[i : i + 1, lane : lane + COARSE]
+    clash[0] = jnp.max(total[15:16])
+
+
+def control_rows(gathered):
+    return pl.pallas_call(
+        control_kernel,
+        out_shape=(
+            jax.ShapeDtypeStruct((1, 2, COARSE * COARSE), F32), jax.ShapeDtypeStruct((1,), F32)
+        ),
+        in_specs=[VMEM],
+        out_specs=(VMEM, SMEM),
+        name="control_rows",
+    )(gathered)
 
 
 def neighbours(low, high, axis, periodic):
@@ -835,10 +871,10 @@
         zonal_diffusivity, zonal_flow, meridional_diffusivity, meridional_flow, vertical_mixing,
         forcing.transpose(1, 0, 2), final_adjoint.transpose(0, 2, 1, 3),
     )
-    low, high, bottom, top = edge_strips(wet_tiles, *fields)
+    low, high, bottom, top, first, own, cross = strips_and_tiles(
+        stored_ids, stored_tiles, owners, wet_tiles, *fields
+    )
     west, east = neighbours(low, high, "lon", True)
-    first, own, cross = split_tiles(stored_ids, stored_tiles, low, owners)
-    first, west, east = lax.optimization_barrier((first, west, east))
     first = lax.all_to_all(first, "lon", split_axis=0, concat_axis=0, tiled=True)
     cross = xor_permute(cross, "lon", 1)
     south, north = neighbours(*with_corners(bottom, top, west, east), "lat", False)
@@ -855,11 +891,7 @@
     gathered = lax.all_to_all(
         keep, "lon", split_axis=0, concat_axis=0, axis_index_groups=parity, tiled=True
     )
-    total = jnp.sum(gathered, axis=0)
-    clashes = total[15, 0]
-    total = total[: COARSE // 2]
-    total = jnp.stack([total[:, :60], total[:, 64:124]]).reshape(2, COARSE // 2, 2, COARSE)
-    control = total.transpose(2, 0, 1, 3).reshape(1, 2, COARSE * COARSE)
+    control, clashes = control_rows(gathered)
 
     def halos(low, high, bottom, top):
         west, east = neighbours(low, high, "lon", True)
@@ -876,7 +908,7 @@
         state, *strips = unpack_tiles(arrived.reshape(owners * PAIR, 8, FLAT))
         return forward_window(state, coef, *halos(*strips)), jnp.float32(0)
 
-    final, _ = lax.while_loop(lambda carry: carry[1] > 0, complete, (final, clashes))
+    final, _ = lax.while_loop(lambda carry: carry[1] > 0, complete, (final, clashes[0]))
     return final.transpose(0, 2, 1, 3), initial.transpose(0, 2, 1, 3), control
 
 

time: 236 us -> 201 us (0.85)
  the two profiles are of different devices: /device:TPU:24 before, /device:TPU:26 now
where the time goes in v6:
time: 201 us; the launch traced here: 200 us
  waiting for transfers between devices  92.9 us (46%)
  Pallas kernels  65.6 us (33%)
  starting transfers between devices  33.7 us (17%)
  local copies, waits for them, and re-layouts  4.66 us (2%)
    ppermute x8, waiting for transfers between devices, neighbours(): return (lax.ppermute(high, axis, up), lax.ppermute(low, axis, down))  65.7 us
    ppermute x12, waiting for transfers between devices, xor_permute(): lax.ppermute(x, axis, [(i, i ^ bits) for i in range(lax.axis_size(axis))])  27.2 us
    pallas_call x1, Pallas kernels, adjoint_window(): pl.pallas_call(adjoint_kernel, out_shape=(jax.ShapeDtypeStruct((2, N, LEV...  26.5 us
    ppermute x8, starting transfers between devices, neighbours(): return (lax.ppermute(high, axis, up), lax.ppermute(low, axis, down))  17.9 us
    pallas_call x1, Pallas kernels, forward_window(): pl.pallas_call(forward_kernel, out_shape=jax.ShapeDtypeStruct(shape, F32)...  15.9 us
    pallas_call x1, Pallas kernels, strips_and_tiles(): pl.pallas_call(head_kernel, out_shape=(strip,) * 4 + tuple((jax.ShapeDtyp...  9.22 us
    pallas_call x1, Pallas kernels, unpack_tiles(): pl.pallas_call(functools.partial(unpack_kernel, extra), out_shape=(jax.Sh...  6.92 us
    all_to_all x1, starting transfers between devices, per_device(): lax.all_to_all(first, 'lon', split_axis=0, concat_axis=0, tiled=True)  6.43 us
  transfers between devices with their start and end apart: 22, of which 11 were waited for; matrix products, arithmetic and copies ran while one was open for 1% of the time, Pallas kernels for 20%

profile of v6, /device:TPU:26, one launch (start us, length us, event | category | flops | bytes accessed | tf_op | source)
XLA Modules:
  0.0 200.5 jit_solution(12307640421647926576)
XLA Ops:
  0.6 9.2 %strips_and_tiles.1 = (f32[48,272]{1,0:T(8,128)}, f32[48,272]{1,0:T(8,128)}, f32[48,272]{1,0:T(8,128)}, f32[48,272]{1,0:T(8,128)}, f32[16,8,8192]{2,1,0:T(8,128)...) custom-call(s32[27]{0:T(128)} %ids.1, f32[27,8,8100]{2,1,0:T(8,128)} %stored.1, s32[3,3]{1,0:T(4,128)} %wet.1, ...), custom_call_target="tpu_custom_call" | custom-call | tf_op jit(solution)/shard_map/strips_and_tiles/pallas_call | solution.py:369
  9.9 6.4 %all-to-all-start.1 = ((f32[16,8,8192]{2,1,0:T(8,128)}), f32[16,8,8192]{2,1,0:T(8,128)}, u32[]{:S(2)}, u32[]{:S(2)}) async-start(f32[16,8,8192]{2,1,0:T(8,128)} %get-tuple-element.67), calls=%async_computation.1 | async-start | bytes 8388608 | tf_op jit(solution)/shard_map/all_to_all | solution.py:878
  18.2 55.7 %collective-permute-done.12.west = f32[48,272]{1,0:T(8,128)S(1)} collective-permute-done((f32[48,272]{1,0:T(8,128)S(1)}, f32[48,272]{1,0:T(8,128)S(1)}, u32[]{:S(2)}, u32[]{:S(2)}) %collective-permute-start.12) | collective-permute-done | bytes 52256 | tf_op jit(solution)/shard_map/ppermute | solution.py:858
  74.5 1.7 row_strips.4
  76.3 5.3 %collective-permute-start.14 = (f32[48,384]{1,0:T(8,128)}, f32[48,384]{1,0:T(8,128)S(1)}, u32[]{:S(2)}, u32[]{:S(2)}) collective-permute-start(f32[48,384]{1,0:T(8,128)} %get-tuple-element.84), channel_id=1, source_target_pairs={{0,16},{16,32},{32,48},{48,64},{64,80},{80,96},{96,112},{1,17},{17... | collective-permute-start | bytes 221192 | tf_op jit(solution)/shard_map/ppermute | solution.py:858
  81.5 1.9 collective-permute-start.15
  84.8 2.2 %merge_tiles.1 = (f32[8,8192]{1,0:T(8,128)}, f32[8,8192]{1,0:T(8,128)}, f32[8,8192]{1,0:T(8,128)}, f32[8,8192]{1,0:T(8,128)}, f32[8,8192]{1,0:T(8,128)}, /*index...) custom-call(f32[8,8,8192]{2,1,0:T(8,128)} %get-tuple-element.68.own, f32[8,8,8192]{2,1,0:T(8,128)} %copy-done.2), custom_call_target="tpu_custom_call" | custom-call | tf_op jit(solution)/shard_map/merge_tiles/pallas_call | solution.py:276
  87.0 4.6 %collective-permute-done.15.north = f32[48,384]{1,0:T(8,128)S(1)} collective-permute-done((f32[48,384]{1,0:T(8,128)}, f32[48,384]{1,0:T(8,128)S(1)}, u32[]{:S(2)}, u32[]{:S(2)}) %collective-permute-start.15) | collective-permute-done | bytes 73760 | tf_op jit(solution)/shard_map/ppermute | solution.py:858
  92.3 26.5 %adjoint_window.1 = (f32[2,270,4,270]{3,2,1,0:T(4,128)}, f32[8,3,304,128]{3,2,1,0:T(8,128)}, f32[64,16,128]{2,1,0:T(8,128)}, f32[64,16,128]{2,1,0:T(8,128)}) custom-call(s32[3,3]{1,0:T(4,128)} %wet.1, s32[3,3]{1,0:T(4,128)} %labels.1, s32[1]{0:T(128)} %get-tuple-element.79.clash, f32[270,270]{1,0:T(8,128)} %zd.1, f32[270,270]{1,0:T(8,128)} %zf.1, ...), custom_call_target="tpu_custom_call" | custom-call | tf_op jit(solution)/shard_map/adjoint_window/pallas_call | solution.py:638
  118.8 2.1 %collective-permute-done.20 = f32[64,16,128]{2,1,0:T(8,128)S(1)} collective-permute-done((f32[64,16,128]{2,1,0:T(8,128)}, f32[64,16,128]{2,1,0:T(8,128)S(1)}, u32[]{:S(2)}, u32[]{:S(2)}) %collective-permute-start.20) | collective-permute-done | bytes 524320 | tf_op jit(solution)/shard_map/ppermute | solution.py:862
  122.5 9.5 %collective-permute-done.21 = f32[32,16,128]{2,1,0:T(8,128)S(1)} collective-permute-done((f32[32,16,128]{2,1,0:T(8,128)S(1)}, f32[32,16,128]{2,1,0:T(8,128)S(1)}, u32[]{:S(2)}, u32[]{:S(2)}) %collective-permute-start.21) | collective-permute-done | bytes 262176 | tf_op jit(solution)/shard_map/ppermute | solution.py:862
  133.4 2.4 %collective-permute-start.7 = (f32[8,8192]{1,0:T(8,128)S(1)}, f32[8,8192]{1,0:T(8,128)S(1)}, u32[]{:S(2)}, u32[]{:S(2)}) collective-permute-start(f32[8,8192]{1,0:T(8,128)S(1)} %copy-done.19), channel_id=1, source_target_pairs={{0,6},{1,7},{2,4},{3,5},{4,2},{5,3},{6,0},{7,1},{8,14},{9,15},{10,... | collective-permute-start | bytes 786440 | tf_op jit(solution)/shard_map/ppermute | solution.py:862
  135.8 2.9 %collective-permute-done.11.refs_7_ = f32[8,8192]{1,0:T(8,128)S(1)} collective-permute-done((f32[8,8192]{1,0:T(8,128)S(1)}, f32[8,8192]{1,0:T(8,128)S(1)}, u32[]{:S(2)}, u32[]{:S(2)}) %collective-permute-start.11) | collective-permute-done | bytes 262176 | tf_op jit(solution)/shard_map/ppermute | solution.py:862
  139.4 2.0 %collective-permute-done.5.refs_1_ = f32[8,8192]{1,0:T(8,128)S(1)} collective-permute-done((f32[8,8192]{1,0:T(8,128)S(1)}, f32[8,8192]{1,0:T(8,128)S(1)}, u32[]{:S(2)}, u32[]{:S(2)}) %collective-permute-start.5) | collective-permute-done | bytes 262176 | tf_op jit(solution)/shard_map/ppermute | solution.py:862
  141.4 3.8 %collective-permute-done.6.refs_2_ = f32[8,8192]{1,0:T(8,128)S(1)} collective-permute-done((f32[8,8192]{1,0:T(8,128)S(1)}, f32[8,8192]{1,0:T(8,128)S(1)}, u32[]{:S(2)}, u32[]{:S(2)}) %collective-permute-start.6) | collective-permute-done | bytes 262176 | tf_op jit(solution)/shard_map/ppermute | solution.py:862
  145.2 2.2 %collective-permute-done.7.refs_3_ = f32[8,8192]{1,0:T(8,128)S(1)} collective-permute-done((f32[8,8192]{1,0:T(8,128)S(1)}, f32[8,8192]{1,0:T(8,128)S(1)}, u32[]{:S(2)}, u32[]{:S(2)}) %collective-permute-start.7) | collective-permute-done | bytes 262176 | tf_op jit(solution)/shard_map/ppermute | solution.py:862
  147.4 3.6 %collective-permute-done.8.refs_4_ = f32[8,8192]{1,0:T(8,128)S(1)} collective-permute-done((f32[8,8192]{1,0:T(8,128)S(1)}, f32[8,8192]{1,0:T(8,128)S(1)}, u32[]{:S(2)}, u32[]{:S(2)}) %collective-permute-start.8) | collective-permute-done | bytes 262176 | tf_op jit(solution)/shard_map/ppermute | solution.py:862
  151.8 6.9 %unpack_tiles.3 = (f32[8,3,304,128]{3,2,1,0:T(8,128)}, f32[24,272]{1,0:T(8,128)}, f32[24,272]{1,0:T(8,128)}, f32[24,272]{1,0:T(8,128)}, f32[24,272]{1,0:T(8,128)}) custom-call(f32[16,8,8192]{2,1,0:T(8,128)} %all-to-all-done.1.first, f32[8,8192]{1,0:T(8,128)} %get-tuple-element.70.refs_0_, f32[8,8192]{1,0:T(8,128)} %copy-done.7, f32[8,8192]{1,0:T(8,128)} %copy-done.8, ...), custom_call_target="tpu_custom_call" | custom-call | tf_op jit(solution)/shard_map/unpack_tiles/pallas_call | solution.py:737
  158.8 1.7 collective-permute-start.17
  161.2 5.5 %all-to-all-start.2 = ((f32[8,16,128]{2,1,0:T(8,128)}), f32[8,16,128]{2,1,0:T(8,128)S(1)}, u32[]{:S(2)}, u32[]{:S(2)}) async-start(f32[8,16,128]{2,1,0:T(8,128)} %slice_add_fusion.2), calls=%async_computation.2 | async-start | bytes 131072 | tf_op jit(solution)/shard_map/all_to_all | solution.py:891
  168.9 5.1 %collective-permute-start.18 = (f32[24,384]{1,0:T(8,128)}, f32[24,384]{1,0:T(8,128)}, u32[]{:S(2)}, u32[]{:S(2)}) collective-permute-start(f32[24,384]{1,0:T(8,128)} %get-tuple-element.91), channel_id=1, source_target_pairs={{0,16},{16,32},{32,48},{48,64},{64,80},{80,96},{96,112},{1,17},{17... | collective-permute-start | bytes 110600 | tf_op jit(solution)/shard_map/ppermute | solution.py:858
  174.0 2.1 %collective-permute-start.19 = (f32[24,384]{1,0:T(8,128)}, f32[24,384]{1,0:T(8,128)}, u32[]{:S(2)}, u32[]{:S(2)}) collective-permute-start(f32[24,384]{1,0:T(8,128)} %get-tuple-element.92), channel_id=1, source_target_pairs={{16,0},{32,16},{48,32},{64,48},{80,64},{96,80},{112,96},{17,1},{33... | collective-permute-start | bytes 110600 | tf_op jit(solution)/shard_map/ppermute | solution.py:858
  178.3 5.4 %collective-permute-done.19.north = f32[24,384]{1,0:T(8,128)} collective-permute-done((f32[24,384]{1,0:T(8,128)}, f32[24,384]{1,0:T(8,128)}, u32[]{:S(2)}, u32[]{:S(2)}) %collective-permute-start.19) | collective-permute-done | bytes 36896 | tf_op jit(solution)/shard_map/ppermute | solution.py:858
  183.8 15.9 %forward_window.3 = f32[2,270,4,270]{3,2,1,0:T(4,128)} custom-call(f32[8,3,304,128]{3,2,1,0:T(8,128)} %get-tuple-element.78.state, f32[8,3,304,128]{3,2,1,0:T(8,128)} %get-tuple-element.118.coef, f32[24,272]{1,0:T(8,128)} %copy-done.13, f32[24,272]{1,0:T(8,128)} %copy-done.14, f32[24,384]{1,0:T(8,128)} %collective-permute-done.18.south, ...), custom_call_target="tpu_custom_call" | custom-call | tf_op jit(solution)/shard_map/forward_window/pallas_call | solution.py:813
  (84 shorter events, 14.5 us)
Async XLA Ops:
  9.9 141.2 %all-to-all-start.1 = ((f32[16,8,8192]{2,1,0:T(8,128)}), f32[16,8,8192]{2,1,0:T(8,128)}, u32[]{:S(2)}, u32[]{:S(2)}) async-start(f32[16,8,8192]{2,1,0:T(8,128)} %get-tuple-element.67), calls=%async_computation.1 | async-start | bytes 8388608 | tf_op jit(solution)/shard_map/all_to_all | solution.py:878
  16.3 67.2 %collective-permute-start.4 = (f32[8,8,8192]{2,1,0:T(8,128)}, f32[8,8,8192]{2,1,0:T(8,128)S(1)}, u32[]{:S(2)}, u32[]{:S(2)}) collective-permute-start(f32[8,8,8192]{2,1,0:T(8,128)} %get-tuple-element.69), channel_id=1, source_target_pairs={{0,1},{1,0},{2,3},{3,2},{4,5},{5,4},{6,7},{7,6},{8,9},{9,8},{10,11... | collective-permute-start | bytes 6291464 | tf_op jit(solution)/shard_map/ppermute | solution.py:862
  16.4 57.4 %collective-permute-start.12 = (f32[48,272]{1,0:T(8,128)S(1)}, f32[48,272]{1,0:T(8,128)S(1)}, u32[]{:S(2)}, u32[]{:S(2)}) collective-permute-start(f32[48,272]{1,0:T(8,128)S(1)} %copy-done.25), channel_id=1, source_target_pairs={{0,1},{1,2},{2,3},{3,4},{4,5},{5,6},{6,7},{7,8},{8,9},{9,10},{10,1... | collective-permute-start | bytes 156680 | tf_op jit(solution)/shard_map/ppermute | solution.py:858
  16.8 57.0 %collective-permute-start.13 = (f32[48,272]{1,0:T(8,128)S(1)}, f32[48,272]{1,0:T(8,128)S(1)}, u32[]{:S(2)}, u32[]{:S(2)}) collective-permute-start(f32[48,272]{1,0:T(8,128)S(1)} %copy-done.24), channel_id=1, source_target_pairs={{1,0},{2,1},{3,2},{4,3},{5,4},{6,5},{7,6},{8,7},{9,8},{10,9},{11,1... | collective-permute-start | bytes 156680 | tf_op jit(solution)/shard_map/ppermute | solution.py:858
  76.3 10.7 %collective-permute-start.14 = (f32[48,384]{1,0:T(8,128)}, f32[48,384]{1,0:T(8,128)S(1)}, u32[]{:S(2)}, u32[]{:S(2)}) collective-permute-start(f32[48,384]{1,0:T(8,128)} %get-tuple-element.84), channel_id=1, source_target_pairs={{0,16},{16,32},{32,48},{48,64},{64,80},{80,96},{96,112},{1,17},{17... | collective-permute-start | bytes 221192 | tf_op jit(solution)/shard_map/ppermute | solution.py:858
  81.5 10.1 %collective-permute-start.15 = (f32[48,384]{1,0:T(8,128)}, f32[48,384]{1,0:T(8,128)S(1)}, u32[]{:S(2)}, u32[]{:S(2)}) collective-permute-start(f32[48,384]{1,0:T(8,128)} %get-tuple-element.85), channel_id=1, source_target_pairs={{16,0},{32,16},{48,32},{64,48},{80,64},{96,80},{112,96},{17,1},{33... | collective-permute-start | bytes 221192 | tf_op jit(solution)/shard_map/ppermute | solution.py:858
  92.3 46.5 %copy-start.18 = (f32[8,8192]{1,0:T(8,128)S(1)}, f32[8,8192]{1,0:T(8,128)}, u32[]{:S(2)}) copy-start(f32[8,8192]{1,0:T(8,128)} %get-tuple-element.74) | copy-start | bytes 786436
  92.3 47.1 %copy-start.17 = (f32[8,8192]{1,0:T(8,128)S(1)}, f32[8,8192]{1,0:T(8,128)}, u32[]{:S(2)}) copy-start(f32[8,8192]{1,0:T(8,128)} %get-tuple-element.75) | copy-start | bytes 786436
  118.8 2.1 %collective-permute-start.20 = (f32[64,16,128]{2,1,0:T(8,128)}, f32[64,16,128]{2,1,0:T(8,128)S(1)}, u32[]{:S(2)}, u32[]{:S(2)}) collective-permute-start(f32[64,16,128]{2,1,0:T(8,128)} %get-tuple-element.94), channel_id=1, source_target_pairs={{0,1},{1,0},{2,3},{3,2},{4,5},{5,4},{6,7},{7,6},{8,9},{9,8},{10,11... | collective-permute-start | bytes 1572872 | tf_op jit(solution)/shard_map/ppermute | solution.py:862
  122.0 9.9 %collective-permute-start.21 = (f32[32,16,128]{2,1,0:T(8,128)S(1)}, f32[32,16,128]{2,1,0:T(8,128)S(1)}, u32[]{:S(2)}, u32[]{:S(2)}) collective-permute-start(f32[32,16,128]{2,1,0:T(8,128)S(1)} %slice.25), channel_id=1, source_target_pairs={{0,32},{16,48},{32,0},{48,16},{64,96},{80,112},{96,64},{112,80},{1... | collective-permute-start | bytes 786440 | tf_op jit(solution)/shard_map/ppermute | solution.py:862
  122.1 11.2 %collective-permute-start.10 = (f32[8,8192]{1,0:T(8,128)S(1)}, f32[8,8192]{1,0:T(8,128)S(1)}, u32[]{:S(2)}, u32[]{:S(2)}) collective-permute-start(f32[8,8192]{1,0:T(8,128)S(1)} %copy-done.23), channel_id=1, source_target_pairs={{0,12},{1,13},{2,14},{3,15},{4,8},{5,9},{6,10},{7,11},{8,4},{9,5},... | collective-permute-start | bytes 786440 | tf_op jit(solution)/shard_map/ppermute | solution.py:862
  122.3 16.5 %collective-permute-start.11 = (f32[8,8192]{1,0:T(8,128)S(1)}, f32[8,8192]{1,0:T(8,128)S(1)}, u32[]{:S(2)}, u32[]{:S(2)}) collective-permute-start(f32[8,8192]{1,0:T(8,128)S(1)} %copy-done.22), channel_id=1, source_target_pairs={{0,14},{1,15},{2,12},{3,13},{4,10},{5,11},{6,8},{7,9},{8,6},{9,7},... | collective-permute-start | bytes 786440 | tf_op jit(solution)/shard_map/ppermute | solution.py:862
  132.0 7.3 %collective-permute-start.22 = (f32[16,16,128]{2,1,0:T(8,128)S(1)}, f32[16,16,128]{2,1,0:T(8,128)S(1)}, u32[]{:S(2)}, u32[]{:S(2)}) collective-permute-start(f32[16,16,128]{2,1,0:T(8,128)S(1)} %slice.27), channel_id=1, source_target_pairs={{0,16},{16,0},{32,48},{48,32},{64,80},{80,64},{96,112},{112,96},{1... | collective-permute-start | bytes 393224 | tf_op jit(solution)/shard_map/ppermute | solution.py:862
  132.1 9.3 %collective-permute-start.5 = (f32[8,8192]{1,0:T(8,128)S(1)}, f32[8,8192]{1,0:T(8,128)S(1)}, u32[]{:S(2)}, u32[]{:S(2)}) collective-permute-start(f32[8,8192]{1,0:T(8,128)S(1)} %copy-done.21), channel_id=1, source_target_pairs={{0,2},{1,3},{2,0},{3,1},{4,6},{5,7},{6,4},{7,5},{8,10},{9,11},{10,... | collective-permute-start | bytes 786440 | tf_op jit(solution)/shard_map/ppermute | solution.py:862
  132.2 13.0 %collective-permute-start.6 = (f32[8,8192]{1,0:T(8,128)S(1)}, f32[8,8192]{1,0:T(8,128)S(1)}, u32[]{:S(2)}, u32[]{:S(2)}) collective-permute-start(f32[8,8192]{1,0:T(8,128)S(1)} %copy-done.20), channel_id=1, source_target_pairs={{0,4},{1,5},{2,6},{3,7},{4,0},{5,1},{6,2},{7,3},{8,12},{9,13},{10,... | collective-permute-start | bytes 786440 | tf_op jit(solution)/shard_map/ppermute | solution.py:862
  133.4 14.0 %collective-permute-start.7 = (f32[8,8192]{1,0:T(8,128)S(1)}, f32[8,8192]{1,0:T(8,128)S(1)}, u32[]{:S(2)}, u32[]{:S(2)}) collective-permute-start(f32[8,8192]{1,0:T(8,128)S(1)} %copy-done.19), channel_id=1, source_target_pairs={{0,6},{1,7},{2,4},{3,5},{4,2},{5,3},{6,0},{7,1},{8,14},{9,15},{10,... | collective-permute-start | bytes 786440 | tf_op jit(solution)/shard_map/ppermute | solution.py:862
  138.7 12.3 %collective-permute-start.8 = (f32[8,8192]{1,0:T(8,128)S(1)}, f32[8,8192]{1,0:T(8,128)S(1)}, u32[]{:S(2)}, u32[]{:S(2)}) collective-permute-start(f32[8,8192]{1,0:T(8,128)S(1)} %copy-done.18), channel_id=1, source_target_pairs={{0,8},{1,9},{2,10},{3,11},{4,12},{5,13},{6,14},{7,15},{8,0},{9,1},... | collective-permute-start | bytes 786440 | tf_op jit(solution)/shard_map/ppermute | solution.py:862
  139.3 11.7 %collective-permute-start.9 = (f32[8,8192]{1,0:T(8,128)S(1)}, f32[8,8192]{1,0:T(8,128)S(1)}, u32[]{:S(2)}, u32[]{:S(2)}) collective-permute-start(f32[8,8192]{1,0:T(8,128)S(1)} %copy-done.17), channel_id=1, source_target_pairs={{0,10},{1,11},{2,8},{3,9},{4,14},{5,15},{6,12},{7,13},{8,2},{9,3},... | collective-permute-start | bytes 786440 | tf_op jit(solution)/shard_map/ppermute | solution.py:862
  141.4 19.2 %collective-permute-start.23 = (f32[8,16,128]{2,1,0:T(8,128)S(1)}, f32[8,16,128]{2,1,0:T(8,128)S(1)}, u32[]{:S(2)}, u32[]{:S(2)}) collective-permute-start(f32[8,16,128]{2,1,0:T(8,128)S(1)} %slice.29), channel_id=1, source_target_pairs={{0,64},{16,80},{32,96},{48,112},{64,0},{80,16},{96,32},{112,48},{1... | collective-permute-start | bytes 196616 | tf_op jit(solution)/shard_map/ppermute | solution.py:862
  158.7 8.0 %collective-permute-start.16 = (f32[24,272]{1,0:T(8,128)}, f32[24,272]{1,0:T(8,128)S(1)}, u32[]{:S(2)}, u32[]{:S(2)}) collective-permute-start(f32[24,272]{1,0:T(8,128)} %get-tuple-element.87), channel_id=1, source_target_pairs={{0,1},{1,2},{2,3},{3,4},{4,5},{5,6},{6,7},{7,8},{8,9},{9,10},{10,1... | collective-permute-start | bytes 78344 | tf_op jit(solution)/shard_map/ppermute | solution.py:858
  158.8 7.9 %collective-permute-start.17 = (f32[24,272]{1,0:T(8,128)}, f32[24,272]{1,0:T(8,128)S(1)}, u32[]{:S(2)}, u32[]{:S(2)}) collective-permute-start(f32[24,272]{1,0:T(8,128)} %get-tuple-element.88), channel_id=1, source_target_pairs={{1,0},{2,1},{3,2},{4,3},{5,4},{6,5},{7,6},{8,7},{9,8},{10,9},{11,1... | collective-permute-start | bytes 78344 | tf_op jit(solution)/shard_map/ppermute | solution.py:858
  161.2 14.9 %all-to-all-start.2 = ((f32[8,16,128]{2,1,0:T(8,128)}), f32[8,16,128]{2,1,0:T(8,128)S(1)}, u32[]{:S(2)}, u32[]{:S(2)}) async-start(f32[8,16,128]{2,1,0:T(8,128)} %slice_add_fusion.2), calls=%async_computation.2 | async-start | bytes 131072 | tf_op jit(solution)/shard_map/all_to_all | solution.py:891
  168.9 9.4 %collective-permute-start.18 = (f32[24,384]{1,0:T(8,128)}, f32[24,384]{1,0:T(8,128)}, u32[]{:S(2)}, u32[]{:S(2)}) collective-permute-start(f32[24,384]{1,0:T(8,128)} %get-tuple-element.91), channel_id=1, source_target_pairs={{0,16},{16,32},{32,48},{48,64},{64,80},{80,96},{96,112},{1,17},{17... | collective-permute-start | bytes 110600 | tf_op jit(solution)/shard_map/ppermute | solution.py:858
  174.0 9.8 %collective-permute-start.19 = (f32[24,384]{1,0:T(8,128)}, f32[24,384]{1,0:T(8,128)}, u32[]{:S(2)}, u32[]{:S(2)}) collective-permute-start(f32[24,384]{1,0:T(8,128)} %get-tuple-element.92), channel_id=1, source_target_pairs={{16,0},{32,16},{48,32},{64,48},{80,64},{96,80},{112,96},{17,1},{33... | collective-permute-start | bytes 110600 | tf_op jit(solution)/shard_map/ppermute | solution.py:858
  (22 other events, 254.8 us)

commit v7 on v6

--- a/solution.py
+++ b/solution.py
@@ -288,6 +288,7 @@
             pltpu.SemaphoreType.DMA((chips,)),
         ],
         name="merge_tiles",
+        compiler_params=pltpu.CompilerParams(vmem_limit_bytes=67043328),
     )(own, cross)
 
 
@@ -386,6 +387,7 @@
             pltpu.SemaphoreType.DMA((3, owners)),
         ],
         name="strips_and_tiles",
+        compiler_params=pltpu.CompilerParams(vmem_limit_bytes=67043328),
     )(ids, stored, *fields)
 
 
@@ -622,7 +624,7 @@
             row = label // owners
             away = row ^ here
             column = label - row * owners
-            at = ((away & 2) * 2 + (away & 1) * 2 + (away >> 2)) * chips + (column >> 1)
+            at = ((away & 2) * 2 + (away & 1) * 2 + (row >> 2)) * chips + (column >> 1)
             other = (column ^ me) & 1
 
             @pl.when(other == 0)
@@ -749,14 +751,19 @@
             pltpu.SemaphoreType.DMA((SIDE * SIDE,)),
         ],
         name="unpack_tiles",
+        compiler_params=pltpu.CompilerParams(vmem_limit_bytes=67043328),
     )(first, *seconds)
 
 
-def forward_kernel(state, coef, west, east, south, north, out, first, second, final, sem, out_sem):
-    copy = pltpu.make_async_copy(state, first, sem)
-    copy.start()
-    copy.wait()
+def forward_kernel(state, factors, west, east, south, north, out, first, second, coef, final, sem, out_sem):
+    copies = [
+        pltpu.make_async_copy(state, first, sem.at[0]), pltpu.make_async_copy(factors, coef, sem.at[1])
+    ]
+    for copy in copies:
+        copy.start()
+    copies[0].wait()
     insert_halos(first, 0, 8, west, east, south, north)
+    copies[1].wait()
 
     def load_coef(b):
         rows = pl.ds(b, 8)
@@ -813,13 +820,14 @@
     return pl.pallas_call(
         forward_kernel,
         out_shape=jax.ShapeDtypeStruct(shape, F32),
-        in_specs=[ANY] + [VMEM] * 5,
+        in_specs=[ANY] * 2 + [VMEM] * 4,
         out_specs=ANY,
         scratch_shapes=[
             pltpu.VMEM((8, 3, ROWS, 128), F32),
             pltpu.VMEM((8, 3, ROWS, 128), F32),
+            pltpu.VMEM((8, 3, ROWS, 128), F32),
             pltpu.VMEM(shape, F32),
-            pltpu.SemaphoreType.DMA,
+            pltpu.SemaphoreType.DMA((2,)),
             pltpu.SemaphoreType.DMA((3,)),
         ],
         name="forward_window",
@@ -884,12 +892,16 @@
         wet_tiles, control_map, clash, *fields, west, east, south, north, owners
     )
     keep = keep + xor_permute(give, "lon", 1)
-    for bit in (2, 1, 4):
+    for bit in (2, 1):
         half = keep.shape[0] // 2
         keep = keep[:half] + xor_permute(keep[half:], "lat", bit)
-    parity = [list(range(c, owners, 2)) for c in range(2)]
+    groups = [
+        [row * owners + column for row in (y, y + 4) for column in range(c, owners, 2)]
+        for y in range(4)
+        for c in range(2)
+    ]
     gathered = lax.all_to_all(
-        keep, "lon", split_axis=0, concat_axis=0, axis_index_groups=parity, tiled=True
+        keep, ("lat", "lon"), split_axis=0, concat_axis=0, axis_index_groups=groups, tiled=True
     )
     control, clashes = control_rows(gathered)
 

time: 201 us -> 196 us (0.975)
  the two profiles are of different devices: /device:TPU:26 before, /device:TPU:31 now
where the time goes in v7:
time: 196 us; the launch traced here: 195 us
  waiting for transfers between devices  76.9 us (39%)
  Pallas kernels  64.3 us (33%)
  starting transfers between devices  49.3 us (25%)
    ppermute x8, waiting for transfers between devices, neighbours(): return (lax.ppermute(high, axis, up), lax.ppermute(low, axis, down))  62.3 us
    pallas_call x1, Pallas kernels, adjoint_window(): pl.pallas_call(adjoint_kernel, out_shape=(jax.ShapeDtypeStruct((2, N, LEV...  26.5 us
    ppermute x11, starting transfers between devices, xor_permute(): lax.ppermute(x, axis, [(i, i ^ bits) for i in range(lax.axis_size(axis))])  18.9 us
    ppermute x8, starting transfers between devices, neighbours(): return (lax.ppermute(high, axis, up), lax.ppermute(low, axis, down))  17.8 us
    pallas_call x1, Pallas kernels, forward_window(): pl.pallas_call(forward_kernel, out_shape=jax.ShapeDtypeStruct(shape, F32)...  14.6 us
    ppermute x11, waiting for transfers between devices, xor_permute(): lax.ppermute(x, axis, [(i, i ^ bits) for i in range(lax.axis_size(axis))])  14.6 us
    pallas_call x1, Pallas kernels, strips_and_tiles(): pl.pallas_call(head_kernel, out_shape=(strip,) * 4 + tuple((jax.ShapeDtyp...  9.25 us
    pallas_call x1, Pallas kernels, unpack_tiles(): pl.pallas_call(functools.partial(unpack_kernel, extra), out_shape=(jax.Sh...  6.83 us
  transfers between devices with their start and end apart: 21, of which 11 were waited for; matrix products, arithmetic and copies ran while one was open for 1% of the time, Pallas kernels for 21%

profile of v7, /device:TPU:31, one launch (start us, length us, event | category | flops | bytes accessed | tf_op | source)
XLA Modules:
  0.0 195.3 jit_solution(13063331034872650281)
XLA Ops:
  0.6 9.3 %strips_and_tiles.1 = (f32[48,272]{1,0:T(8,128)}, f32[48,272]{1,0:T(8,128)}, f32[48,272]{1,0:T(8,128)}, f32[48,272]{1,0:T(8,128)}, f32[16,8,8192]{2,1,0:T(8,128)...) custom-call(s32[27]{0:T(128)} %ids.1, f32[27,8,8100]{2,1,0:T(8,128)} %stored.1, s32[3,3]{1,0:T(4,128)} %wet.1, ...), custom_call_target="tpu_custom_call" | custom-call | tf_op jit(solution)/shard_map/strips_and_tiles/pallas_call | solution.py:370
  9.9 6.6 %all-to-all-start.1 = ((f32[16,8,8192]{2,1,0:T(8,128)}), f32[16,8,8192]{2,1,0:T(8,128)}, u32[]{:S(2)}, u32[]{:S(2)}) async-start(f32[16,8,8192]{2,1,0:T(8,128)} %get-tuple-element.67), calls=%async_computation.1 | async-start | bytes 8388608 | tf_op jit(solution)/shard_map/all_to_all | solution.py:886
  18.2 44.8 %collective-permute-done.12.west = f32[48,272]{1,0:T(8,128)S(1)} collective-permute-done((f32[48,272]{1,0:T(8,128)S(1)}, f32[48,272]{1,0:T(8,128)S(1)}, u32[]{:S(2)}, u32[]{:S(2)}) %collective-permute-start.12) | collective-permute-done | bytes 52256 | tf_op jit(solution)/shard_map/ppermute | solution.py:866
  63.0 2.1 %collective-permute-done.13.east = f32[48,272]{1,0:T(8,128)S(1)} collective-permute-done((f32[48,272]{1,0:T(8,128)S(1)}, f32[48,272]{1,0:T(8,128)S(1)}, u32[]{:S(2)}, u32[]{:S(2)}) %collective-permute-start.13) | collective-permute-done | bytes 52256 | tf_op jit(solution)/shard_map/ppermute | solution.py:866
  67.4 5.0 %collective-permute-start.14 = (f32[48,384]{1,0:T(8,128)}, f32[48,384]{1,0:T(8,128)}, u32[]{:S(2)}, u32[]{:S(2)}) collective-permute-start(f32[48,384]{1,0:T(8,128)} %get-tuple-element.84), channel_id=1, source_target_pairs={{0,16},{16,32},{32,48},{48,64},{64,80},{80,96},{96,112},{1,17},{17... | collective-permute-start | bytes 221192 | tf_op jit(solution)/shard_map/ppermute | solution.py:866
  72.4 1.9 collective-permute-start.15
  74.4 2.2 %merge_tiles.1 = (f32[8,8192]{1,0:T(8,128)}, f32[8,8192]{1,0:T(8,128)}, f32[8,8192]{1,0:T(8,128)}, f32[8,8192]{1,0:T(8,128)}, f32[8,8192]{1,0:T(8,128)}, /*index...) custom-call(f32[8,8,8192]{2,1,0:T(8,128)} %get-tuple-element.68.own, ...), custom_call_target="tpu_custom_call" | custom-call | tf_op jit(solution)/shard_map/merge_tiles/pallas_call | solution.py:276
  76.6 4.9 %collective-permute-done.15.north = f32[48,384]{1,0:T(8,128)} collective-permute-done((f32[48,384]{1,0:T(8,128)}, f32[48,384]{1,0:T(8,128)}, u32[]{:S(2)}, u32[]{:S(2)}) %collective-permute-start.15) | collective-permute-done | bytes 73760 | tf_op jit(solution)/shard_map/ppermute | solution.py:866
  81.5 26.5 %adjoint_window.1 = (f32[2,270,4,270]{3,2,1,0:T(4,128)}, f32[8,3,304,128]{3,2,1,0:T(8,128)}, f32[64,16,128]{2,1,0:T(8,128)}, f32[64,16,128]{2,1,0:T(8,128)}) custom-call(s32[3,3]{1,0:T(4,128)} %wet.1, s32[3,3]{1,0:T(4,128)} %labels.1, s32[1]{0:T(128)} %get-tuple-element.79.clash, f32[270,270]{1,0:T(8,128)} %zd.1, f32[270,270]{1,0:T(8,128)} %zf.1, ...), custom_call_target="tpu_custom_call" | custom-call | tf_op jit(solution)/shard_map/adjoint_window/pallas_call | solution.py:640
  108.0 7.5 %collective-permute-start.20 = (f32[64,16,128]{2,1,0:T(8,128)}, f32[64,16,128]{2,1,0:T(8,128)S(1)}, u32[]{:S(2)}, u32[]{:S(2)}) collective-permute-start(f32[64,16,128]{2,1,0:T(8,128)} %get-tuple-element.94), channel_id=1, source_target_pairs={{0,1},{1,0},{2,3},{3,2},{4,5},{5,4},{6,7},{7,6},{8,9},{9,8},{10,11... | collective-permute-start | bytes 1572872 | tf_op jit(solution)/shard_map/ppermute | solution.py:870
  118.5 4.5 %collective-permute-start.10 = (f32[8,8192]{1,0:T(8,128)S(1)}, f32[8,8192]{1,0:T(8,128)}, u32[]{:S(2)}, u32[]{:S(2)}) collective-permute-start(f32[8,8192]{1,0:T(8,128)S(1)} %copy-done.13), channel_id=1, source_target_pairs={{0,12},{1,13},{2,14},{3,15},{4,8},{5,9},{6,10},{7,11},{8,4},{9,5},... | collective-permute-start | bytes 786440 | tf_op jit(solution)/shard_map/ppermute | solution.py:870
  123.1 4.5 %collective-permute-done.21 = f32[32,16,128]{2,1,0:T(8,128)S(1)} collective-permute-done((f32[32,16,128]{2,1,0:T(8,128)S(1)}, f32[32,16,128]{2,1,0:T(8,128)S(1)}, u32[]{:S(2)}, u32[]{:S(2)}) %collective-permute-start.21) | collective-permute-done | bytes 262176 | tf_op jit(solution)/shard_map/ppermute | solution.py:870
  128.9 3.5 %collective-permute-start.6 = (f32[8,8192]{1,0:T(8,128)S(1)}, f32[8,8192]{1,0:T(8,128)}, u32[]{:S(2)}, u32[]{:S(2)}) collective-permute-start(f32[8,8192]{1,0:T(8,128)S(1)} %copy-done.10), channel_id=1, source_target_pairs={{0,4},{1,5},{2,6},{3,7},{4,0},{5,1},{6,2},{7,3},{8,12},{9,13},{10,... | collective-permute-start | bytes 786440 | tf_op jit(solution)/shard_map/ppermute | solution.py:870
  132.7 2.9 %collective-permute-done.11.refs_7_ = f32[8,8192]{1,0:T(8,128)} collective-permute-done((f32[8,8192]{1,0:T(8,128)S(1)}, f32[8,8192]{1,0:T(8,128)}, u32[]{:S(2)}, u32[]{:S(2)}) %collective-permute-start.11) | collective-permute-done | bytes 262176 | tf_op jit(solution)/shard_map/ppermute | solution.py:870
  137.5 6.0 %all-to-all-start.2 = ((f32[16,16,128]{2,1,0:T(8,128)}), f32[16,16,128]{2,1,0:T(8,128)}, u32[]{:S(2)}, u32[]{:S(2)}) async-start(f32[16,16,128]{2,1,0:T(8,128)} %slice_add_fusion.1), calls=%async_computation.2 | async-start | bytes 262144 | tf_op jit(solution)/shard_map/all_to_all | solution.py:903
  143.6 2.0 %collective-permute-done.7.refs_3_ = f32[8,8192]{1,0:T(8,128)} collective-permute-done((f32[8,8192]{1,0:T(8,128)S(1)}, f32[8,8192]{1,0:T(8,128)}, u32[]{:S(2)}, u32[]{:S(2)}) %collective-permute-start.7) | collective-permute-done | bytes 262176 | tf_op jit(solution)/shard_map/ppermute | solution.py:870
  145.6 3.4 %collective-permute-done.8.refs_4_ = f32[8,8192]{1,0:T(8,128)} collective-permute-done((f32[8,8192]{1,0:T(8,128)S(1)}, f32[8,8192]{1,0:T(8,128)}, u32[]{:S(2)}, u32[]{:S(2)}) %collective-permute-start.8) | collective-permute-done | bytes 262176 | tf_op jit(solution)/shard_map/ppermute | solution.py:870
  149.0 6.8 %unpack_tiles.3 = (f32[8,3,304,128]{3,2,1,0:T(8,128)}, f32[24,272]{1,0:T(8,128)}, f32[24,272]{1,0:T(8,128)}, f32[24,272]{1,0:T(8,128)}, f32[24,272]{1,0:T(8,128)}) custom-call(f32[16,8,8192]{2,1,0:T(8,128)} %all-to-all-done.1.first, f32[8,8192]{1,0:T(8,128)} %get-tuple-element.70.refs_0_, f32[8,8192]{1,0:T(8,128)} %collective-permute-done.5.refs_1_, ...), custom_call_target="tpu_custom_call" | custom-call | tf_op jit(solution)/shard_map/unpack_tiles/pallas_call | solution.py:739
  155.8 4.0 %collective-permute-start.16 = (f32[24,272]{1,0:T(8,128)}, f32[24,272]{1,0:T(8,128)S(1)}, u32[]{:S(2)}, u32[]{:S(2)}) collective-permute-start(f32[24,272]{1,0:T(8,128)} %get-tuple-element.87), channel_id=1, source_target_pairs={{0,1},{1,2},{2,3},{3,4},{4,5},{5,6},{6,7},{7,8},{8,9},{9,10},{10,1... | collective-permute-start | bytes 78344 | tf_op jit(solution)/shard_map/ppermute | solution.py:866
  161.2 4.3 %collective-permute-done.17.east = f32[24,272]{1,0:T(8,128)S(1)} collective-permute-done((f32[24,272]{1,0:T(8,128)}, f32[24,272]{1,0:T(8,128)S(1)}, u32[]{:S(2)}, u32[]{:S(2)}) %collective-permute-start.17) | collective-permute-done | bytes 26144 | tf_op jit(solution)/shard_map/ppermute | solution.py:866
  167.7 3.5 %collective-permute-start.18 = (f32[24,384]{1,0:T(8,128)}, f32[24,384]{1,0:T(8,128)}, u32[]{:S(2)}, u32[]{:S(2)}) collective-permute-start(f32[24,384]{1,0:T(8,128)} %get-tuple-element.91), channel_id=1, source_target_pairs={{0,16},{16,32},{32,48},{48,64},{64,80},{80,96},{96,112},{1,17},{17... | collective-permute-start | bytes 110600 | tf_op jit(solution)/shard_map/ppermute | solution.py:866
  171.2 2.1 %collective-permute-start.19 = (f32[24,384]{1,0:T(8,128)}, f32[24,384]{1,0:T(8,128)}, u32[]{:S(2)}, u32[]{:S(2)}) collective-permute-start(f32[24,384]{1,0:T(8,128)} %get-tuple-element.92), channel_id=1, source_target_pairs={{16,0},{32,16},{48,32},{64,48},{80,64},{96,80},{112,96},{17,1},{33... | collective-permute-start | bytes 110600 | tf_op jit(solution)/shard_map/ppermute | solution.py:866
  175.0 4.8 %collective-permute-done.19.north = f32[24,384]{1,0:T(8,128)} collective-permute-done((f32[24,384]{1,0:T(8,128)}, f32[24,384]{1,0:T(8,128)}, u32[]{:S(2)}, u32[]{:S(2)}) %collective-permute-start.19) | collective-permute-done | bytes 36896 | tf_op jit(solution)/shard_map/ppermute | solution.py:866
  179.9 14.6 %forward_window.3 = f32[2,270,4,270]{3,2,1,0:T(4,128)} custom-call(f32[8,3,304,128]{3,2,1,0:T(8,128)} %get-tuple-element.78.state, f32[8,3,304,128]{3,2,1,0:T(8,128)} %get-tuple-element.118.factors, f32[24,272]{1,0:T(8,128)} %copy-done.4, f32[24,272]{1,0:T(8,128)} %copy-done.5, f32[24,384]{1,0:T(8,128)} %collective-permute-done.18.south, ...), custom_call_target="tpu_custom_call" | custom-call | tf_op jit(solution)/shard_map/forward_window/pallas_call | solution.py:820
  (60 shorter events, 16.4 us)
Async XLA Ops:
  9.9 127.6 %all-to-all-start.1 = ((f32[16,8,8192]{2,1,0:T(8,128)}), f32[16,8,8192]{2,1,0:T(8,128)}, u32[]{:S(2)}, u32[]{:S(2)}) async-start(f32[16,8,8192]{2,1,0:T(8,128)} %get-tuple-element.67), calls=%async_computation.1 | async-start | bytes 8388608 | tf_op jit(solution)/shard_map/all_to_all | solution.py:886
  16.5 57.8 %collective-permute-start.4 = (f32[8,8,8192]{2,1,0:T(8,128)S(1)}, f32[8,8,8192]{2,1,0:T(8,128)}, u32[]{:S(2)}, u32[]{:S(2)}) collective-permute-start(f32[8,8,8192]{2,1,0:T(8,128)S(1)} %copy-done.6), channel_id=1, source_target_pairs={{0,1},{1,0},{2,3},{3,2},{4,5},{5,4},{6,7},{7,6},{8,9},{9,8},{10,11... | collective-permute-start | bytes 6291464 | tf_op jit(solution)/shard_map/ppermute | solution.py:870
  17.0 46.0 %collective-permute-start.12 = (f32[48,272]{1,0:T(8,128)S(1)}, f32[48,272]{1,0:T(8,128)S(1)}, u32[]{:S(2)}, u32[]{:S(2)}) collective-permute-start(f32[48,272]{1,0:T(8,128)S(1)} %copy-done.15), channel_id=1, source_target_pairs={{0,1},{1,2},{2,3},{3,4},{4,5},{5,6},{6,7},{7,8},{8,9},{9,10},{10,1... | collective-permute-start | bytes 156680 | tf_op jit(solution)/shard_map/ppermute | solution.py:866
  18.2 46.9 %collective-permute-start.13 = (f32[48,272]{1,0:T(8,128)S(1)}, f32[48,272]{1,0:T(8,128)S(1)}, u32[]{:S(2)}, u32[]{:S(2)}) collective-permute-start(f32[48,272]{1,0:T(8,128)S(1)} %copy-done.14), channel_id=1, source_target_pairs={{1,0},{2,1},{3,2},{4,3},{5,4},{6,5},{7,6},{8,7},{9,8},{10,9},{11,1... | collective-permute-start | bytes 156680 | tf_op jit(solution)/shard_map/ppermute | solution.py:866
  67.4 9.1 %collective-permute-start.14 = (f32[48,384]{1,0:T(8,128)}, f32[48,384]{1,0:T(8,128)}, u32[]{:S(2)}, u32[]{:S(2)}) collective-permute-start(f32[48,384]{1,0:T(8,128)} %get-tuple-element.84), channel_id=1, source_target_pairs={{0,16},{16,32},{32,48},{48,64},{64,80},{80,96},{96,112},{1,17},{17... | collective-permute-start | bytes 221192 | tf_op jit(solution)/shard_map/ppermute | solution.py:866
  72.4 9.0 %collective-permute-start.15 = (f32[48,384]{1,0:T(8,128)}, f32[48,384]{1,0:T(8,128)}, u32[]{:S(2)}, u32[]{:S(2)}) collective-permute-start(f32[48,384]{1,0:T(8,128)} %get-tuple-element.85), channel_id=1, source_target_pairs={{16,0},{32,16},{48,32},{64,48},{80,64},{96,80},{112,96},{17,1},{33... | collective-permute-start | bytes 221192 | tf_op jit(solution)/shard_map/ppermute | solution.py:866
  81.5 50.9 %copy-start.9 = (f32[8,8192]{1,0:T(8,128)S(1)}, f32[8,8192]{1,0:T(8,128)}, u32[]{:S(2)}) copy-start(f32[8,8192]{1,0:T(8,128)} %get-tuple-element.73) | copy-start | bytes 786436
  81.5 54.1 %copy-start.8 = (f32[8,8192]{1,0:T(8,128)S(1)}, f32[8,8192]{1,0:T(8,128)}, u32[]{:S(2)}) copy-start(f32[8,8192]{1,0:T(8,128)} %get-tuple-element.74) | copy-start | bytes 786436
  81.5 55.3 %copy-start.7 = (f32[8,8192]{1,0:T(8,128)S(1)}, f32[8,8192]{1,0:T(8,128)}, u32[]{:S(2)}) copy-start(f32[8,8192]{1,0:T(8,128)} %get-tuple-element.75) | copy-start | bytes 786436
  108.0 9.3 %collective-permute-start.20 = (f32[64,16,128]{2,1,0:T(8,128)}, f32[64,16,128]{2,1,0:T(8,128)S(1)}, u32[]{:S(2)}, u32[]{:S(2)}) collective-permute-start(f32[64,16,128]{2,1,0:T(8,128)} %get-tuple-element.94), channel_id=1, source_target_pairs={{0,1},{1,0},{2,3},{3,2},{4,5},{5,4},{6,7},{7,6},{8,9},{9,8},{10,11... | collective-permute-start | bytes 1572872 | tf_op jit(solution)/shard_map/ppermute | solution.py:870
  118.4 9.2 %collective-permute-start.21 = (f32[32,16,128]{2,1,0:T(8,128)S(1)}, f32[32,16,128]{2,1,0:T(8,128)S(1)}, u32[]{:S(2)}, u32[]{:S(2)}) collective-permute-start(f32[32,16,128]{2,1,0:T(8,128)S(1)} %slice.17), channel_id=1, source_target_pairs={{0,32},{16,48},{32,0},{48,16},{64,96},{80,112},{96,64},{112,80},{1... | collective-permute-start | bytes 786440 | tf_op jit(solution)/shard_map/ppermute | solution.py:870
  118.5 13.8 %collective-permute-start.10 = (f32[8,8192]{1,0:T(8,128)S(1)}, f32[8,8192]{1,0:T(8,128)}, u32[]{:S(2)}, u32[]{:S(2)}) collective-permute-start(f32[8,8192]{1,0:T(8,128)S(1)} %copy-done.13), channel_id=1, source_target_pairs={{0,12},{1,13},{2,14},{3,15},{4,8},{5,9},{6,10},{7,11},{8,4},{9,5},... | collective-permute-start | bytes 786440 | tf_op jit(solution)/shard_map/ppermute | solution.py:870
  123.0 12.5 %collective-permute-start.11 = (f32[8,8192]{1,0:T(8,128)S(1)}, f32[8,8192]{1,0:T(8,128)}, u32[]{:S(2)}, u32[]{:S(2)}) collective-permute-start(f32[8,8192]{1,0:T(8,128)S(1)} %copy-done.12), channel_id=1, source_target_pairs={{0,14},{1,15},{2,12},{3,13},{4,10},{5,11},{6,8},{7,9},{8,6},{9,7},... | collective-permute-start | bytes 786440 | tf_op jit(solution)/shard_map/ppermute | solution.py:870
  127.7 9.2 %collective-permute-start.22 = (f32[16,16,128]{2,1,0:T(8,128)S(1)}, f32[16,16,128]{2,1,0:T(8,128)S(1)}, u32[]{:S(2)}, u32[]{:S(2)}) collective-permute-start(f32[16,16,128]{2,1,0:T(8,128)S(1)} %slice.19), channel_id=1, source_target_pairs={{0,16},{16,0},{32,48},{48,32},{64,80},{80,64},{96,112},{112,96},{1... | collective-permute-start | bytes 393224 | tf_op jit(solution)/shard_map/ppermute | solution.py:870
  127.8 15.8 %collective-permute-start.5 = (f32[8,8192]{1,0:T(8,128)S(1)}, f32[8,8192]{1,0:T(8,128)}, u32[]{:S(2)}, u32[]{:S(2)}) collective-permute-start(f32[8,8192]{1,0:T(8,128)S(1)} %copy-done.11), channel_id=1, source_target_pairs={{0,2},{1,3},{2,0},{3,1},{4,6},{5,7},{6,4},{7,5},{8,10},{9,11},{10,... | collective-permute-start | bytes 786440 | tf_op jit(solution)/shard_map/ppermute | solution.py:870
  128.9 14.6 %collective-permute-start.6 = (f32[8,8192]{1,0:T(8,128)S(1)}, f32[8,8192]{1,0:T(8,128)}, u32[]{:S(2)}, u32[]{:S(2)}) collective-permute-start(f32[8,8192]{1,0:T(8,128)S(1)} %copy-done.10), channel_id=1, source_target_pairs={{0,4},{1,5},{2,6},{3,7},{4,0},{5,1},{6,2},{7,3},{8,12},{9,13},{10,... | collective-permute-start | bytes 786440 | tf_op jit(solution)/shard_map/ppermute | solution.py:870
  132.4 13.2 %collective-permute-start.7 = (f32[8,8192]{1,0:T(8,128)S(1)}, f32[8,8192]{1,0:T(8,128)}, u32[]{:S(2)}, u32[]{:S(2)}) collective-permute-start(f32[8,8192]{1,0:T(8,128)S(1)} %copy-done.9), channel_id=1, source_target_pairs={{0,6},{1,7},{2,4},{3,5},{4,2},{5,3},{6,0},{7,1},{8,14},{9,15},{10,... | collective-permute-start | bytes 786440 | tf_op jit(solution)/shard_map/ppermute | solution.py:870
  135.5 13.4 %collective-permute-start.8 = (f32[8,8192]{1,0:T(8,128)S(1)}, f32[8,8192]{1,0:T(8,128)}, u32[]{:S(2)}, u32[]{:S(2)}) collective-permute-start(f32[8,8192]{1,0:T(8,128)S(1)} %copy-done.8), channel_id=1, source_target_pairs={{0,8},{1,9},{2,10},{3,11},{4,12},{5,13},{6,14},{7,15},{8,0},{9,1},... | collective-permute-start | bytes 786440 | tf_op jit(solution)/shard_map/ppermute | solution.py:870
  136.8 12.2 %collective-permute-start.9 = (f32[8,8192]{1,0:T(8,128)S(1)}, f32[8,8192]{1,0:T(8,128)}, u32[]{:S(2)}, u32[]{:S(2)}) collective-permute-start(f32[8,8192]{1,0:T(8,128)S(1)} %copy-done.7), channel_id=1, source_target_pairs={{0,10},{1,11},{2,8},{3,9},{4,14},{5,15},{6,12},{7,13},{8,2},{9,3},... | collective-permute-start | bytes 786440 | tf_op jit(solution)/shard_map/ppermute | solution.py:870
  137.5 35.8 %all-to-all-start.2 = ((f32[16,16,128]{2,1,0:T(8,128)}), f32[16,16,128]{2,1,0:T(8,128)}, u32[]{:S(2)}, u32[]{:S(2)}) async-start(f32[16,16,128]{2,1,0:T(8,128)} %slice_add_fusion.1), calls=%async_computation.2 | async-start | bytes 262144 | tf_op jit(solution)/shard_map/all_to_all | solution.py:903
  155.8 5.4 %collective-permute-start.16 = (f32[24,272]{1,0:T(8,128)}, f32[24,272]{1,0:T(8,128)S(1)}, u32[]{:S(2)}, u32[]{:S(2)}) collective-permute-start(f32[24,272]{1,0:T(8,128)} %get-tuple-element.87), channel_id=1, source_target_pairs={{0,1},{1,2},{2,3},{3,4},{4,5},{5,6},{6,7},{7,8},{8,9},{9,10},{10,1... | collective-permute-start | bytes 78344 | tf_op jit(solution)/shard_map/ppermute | solution.py:866
  159.9 5.7 %collective-permute-start.17 = (f32[24,272]{1,0:T(8,128)}, f32[24,272]{1,0:T(8,128)S(1)}, u32[]{:S(2)}, u32[]{:S(2)}) collective-permute-start(f32[24,272]{1,0:T(8,128)} %get-tuple-element.88), channel_id=1, source_target_pairs={{1,0},{2,1},{3,2},{4,3},{5,4},{6,5},{7,6},{8,7},{9,8},{10,9},{11,1... | collective-permute-start | bytes 78344 | tf_op jit(solution)/shard_map/ppermute | solution.py:866
  167.7 7.3 %collective-permute-start.18 = (f32[24,384]{1,0:T(8,128)}, f32[24,384]{1,0:T(8,128)}, u32[]{:S(2)}, u32[]{:S(2)}) collective-permute-start(f32[24,384]{1,0:T(8,128)} %get-tuple-element.91), channel_id=1, source_target_pairs={{0,16},{16,32},{32,48},{48,64},{64,80},{80,96},{96,112},{1,17},{17... | collective-permute-start | bytes 110600 | tf_op jit(solution)/shard_map/ppermute | solution.py:866
  171.2 8.6 %collective-permute-start.19 = (f32[24,384]{1,0:T(8,128)}, f32[24,384]{1,0:T(8,128)}, u32[]{:S(2)}, u32[]{:S(2)}) collective-permute-start(f32[24,384]{1,0:T(8,128)} %get-tuple-element.92), channel_id=1, source_target_pairs={{16,0},{32,16},{48,32},{64,48},{80,64},{96,80},{112,96},{17,1},{33... | collective-permute-start | bytes 110600 | tf_op jit(solution)/shard_map/ppermute | solution.py:866
  (11 other events, 202.1 us)

commit v8 on v7

--- a/solution.py
+++ b/solution.py
@@ -398,10 +398,22 @@
         out[:, N + HALO : N + 2 * HALO] = east[:, first : first + HALO]
 
 
-def with_corners(south, north, west, east):
+def paired_kernel(south, north, west, east, one, two):
+    even = lax.axis_index("lat") & 1 == 0
+
+    @pl.when(even)
+    def _():
+        corners_kernel(south, north, west, east, two, one)
+
+    @pl.when(jnp.logical_not(even))
+    def _():
+        corners_kernel(south, north, west, east, one, two)
+
+
+def with_corners(south, north, west, east, kernel=corners_kernel):
     shape = jax.ShapeDtypeStruct((south.shape[0], LANES), F32)
     return pl.pallas_call(
-        corners_kernel,
+        kernel,
         out_shape=(shape, shape),
         in_specs=[VMEM] * 4,
         out_specs=(VMEM,) * 2,
@@ -755,7 +767,10 @@
     )(first, *seconds)
 
 
-def forward_kernel(state, factors, west, east, south, north, out, first, second, coef, final, sem, out_sem):
+def forward_kernel(state, factors, west, east, one, two, out, first, second, coef, final, south, north, sem, out_sem):
+    even = lax.axis_index("lat") & 1 == 0
+    south[...] = jnp.where(even, two[...], one[...])
+    north[...] = jnp.where(even, one[...], two[...])
     copies = [
         pltpu.make_async_copy(state, first, sem.at[0]), pltpu.make_async_copy(factors, coef, sem.at[1])
     ]
@@ -815,7 +830,7 @@
         copy.wait()
 
 
-def forward_window(state, coef, west, east, south, north):
+def forward_window(state, coef, west, east, one, two):
     shape = (2, N, LEV, N)
     return pl.pallas_call(
         forward_kernel,
@@ -827,12 +842,14 @@
             pltpu.VMEM((8, 3, ROWS, 128), F32),
             pltpu.VMEM((8, 3, ROWS, 128), F32),
             pltpu.VMEM(shape, F32),
+            pltpu.VMEM((24, LANES), F32),
+            pltpu.VMEM((24, LANES), F32),
             pltpu.SemaphoreType.DMA((2,)),
             pltpu.SemaphoreType.DMA((3,)),
         ],
         name="forward_window",
         compiler_params=pltpu.CompilerParams(vmem_limit_bytes=67043328),
-    )(state, coef, west, east, south, north)
+    )(state, coef, west, east, one, two)
 
 
 def control_kernel(gathered, control, clash):
@@ -907,8 +924,13 @@
 
     def halos(low, high, bottom, top):
         west, east = neighbours(low, high, "lon", True)
-        to_south, to_north = with_corners(bottom, top, west, east)
-        return (west, east) + neighbours(to_south, to_north, "lat", False)
+        one, two = with_corners(bottom, top, west, east, paired_kernel)
+        bands = lax.axis_size("lat")
+        pairs = [[(i, i + 1) for i in range(first, bands - 1, 2)] for first in range(2)]
+        one, two = [
+            lax.ppermute(x, "lat", pair + [(b, a) for a, b in pair]) for x, pair in zip((one, two), pairs)
+        ]
+        return west, east, one, two
 
     state, *strips = unpack_tiles(first, *seconds)
     strips = halos(*strips)

time: 196 us -> 194 us (0.990)
    ppermute x8 -> x6, starting transfers between devices: 17.8 us -> 12.1 us  [neighbours(): return (lax.ppermute(high, axis, up), lax.ppermute(low, axis, down))]
    ppermute x8 -> x6, waiting for transfers between devices: 62.3 us -> 57.5 us  [neighbours(): return (lax.ppermute(high, axis, up), lax.ppermute(low, axis, down))]
    ppermute x0 -> x2, waiting for transfers between devices: none -> 4.44 us  [halos(): lax.ppermute(x, 'lat', pair + [(b, a) for a, b in pair])]
    ppermute x0 -> x2, starting transfers between devices: none -> 3.72 us  [halos(): lax.ppermute(x, 'lat', pair + [(b, a) for a, b in pair])]
where the time goes in v8:
time: 194 us; the launch traced here: 193 us
  waiting for transfers between devices  76.5 us (39%)
  Pallas kernels  64.3 us (33%)
  starting transfers between devices  47.4 us (24%)
    ppermute x6, waiting for transfers between devices, neighbours(): return (lax.ppermute(high, axis, up), lax.ppermute(low, axis, down))  57.5 us
    pallas_call x1, Pallas kernels, adjoint_window(): pl.pallas_call(adjoint_kernel, out_shape=(jax.ShapeDtypeStruct((2, N, LEV...  26.5 us
    ppermute x11, starting transfers between devices, xor_permute(): lax.ppermute(x, axis, [(i, i ^ bits) for i in range(lax.axis_size(axis))])  18.9 us
    pallas_call x1, Pallas kernels, forward_window(): pl.pallas_call(forward_kernel, out_shape=jax.ShapeDtypeStruct(shape, F32)...  14.6 us
    ppermute x11, waiting for transfers between devices, xor_permute(): lax.ppermute(x, axis, [(i, i ^ bits) for i in range(lax.axis_size(axis))])  14.6 us
    ppermute x6, starting transfers between devices, neighbours(): return (lax.ppermute(high, axis, up), lax.ppermute(low, axis, down))  12.1 us
    pallas_call x1, Pallas kernels, strips_and_tiles(): pl.pallas_call(head_kernel, out_shape=(strip,) * 4 + tuple((jax.ShapeDtyp...  9.25 us
    pallas_call x1, Pallas kernels, unpack_tiles(): pl.pallas_call(functools.partial(unpack_kernel, extra), out_shape=(jax.Sh...  6.83 us
  transfers between devices with their start and end apart: 21, of which 11 were waited for; matrix products, arithmetic and copies ran while one was open for 1% of the time, Pallas kernels for 21%

profile of v8, /device:TPU:31, one launch (start us, length us, event | category | flops | bytes accessed | tf_op | source)
XLA Modules:
  0.0 193.0 jit_solution(14302965136034906922)
XLA Ops:
  0.6 9.3 %strips_and_tiles.1 = (f32[48,272]{1,0:T(8,128)}, f32[48,272]{1,0:T(8,128)}, f32[48,272]{1,0:T(8,128)}, f32[48,272]{1,0:T(8,128)}, f32[16,8,8192]{2,1,0:T(8,128)...) custom-call(s32[27]{0:T(128)} %ids.1, f32[27,8,8100]{2,1,0:T(8,128)} %stored.1, s32[3,3]{1,0:T(4,128)} %wet.1, ...), custom_call_target="tpu_custom_call" | custom-call | tf_op jit(solution)/shard_map/strips_and_tiles/pallas_call | solution.py:370
  9.9 6.6 %all-to-all-start.1 = ((f32[16,8,8192]{2,1,0:T(8,128)}), f32[16,8,8192]{2,1,0:T(8,128)}, u32[]{:S(2)}, u32[]{:S(2)}) async-start(f32[16,8,8192]{2,1,0:T(8,128)} %get-tuple-element.67), calls=%async_computation.1 | async-start | bytes 8388608 | tf_op jit(solution)/shard_map/all_to_all | solution.py:903
  18.2 44.8 %collective-permute-done.12.west = f32[48,272]{1,0:T(8,128)S(1)} collective-permute-done((f32[48,272]{1,0:T(8,128)S(1)}, f32[48,272]{1,0:T(8,128)S(1)}, u32[]{:S(2)}, u32[]{:S(2)}) %collective-permute-start.12) | collective-permute-done | bytes 52256 | tf_op jit(solution)/shard_map/ppermute | solution.py:883
  63.0 2.1 %collective-permute-done.13.east = f32[48,272]{1,0:T(8,128)S(1)} collective-permute-done((f32[48,272]{1,0:T(8,128)S(1)}, f32[48,272]{1,0:T(8,128)S(1)}, u32[]{:S(2)}, u32[]{:S(2)}) %collective-permute-start.13) | collective-permute-done | bytes 52256 | tf_op jit(solution)/shard_map/ppermute | solution.py:883
  67.4 5.0 %collective-permute-start.14 = (f32[48,384]{1,0:T(8,128)}, f32[48,384]{1,0:T(8,128)}, u32[]{:S(2)}, u32[]{:S(2)}) collective-permute-start(f32[48,384]{1,0:T(8,128)} %get-tuple-element.84), channel_id=1, source_target_pairs={{0,16},{16,32},{32,48},{48,64},{64,80},{80,96},{96,112},{1,17},{17... | collective-permute-start | bytes 221192 | tf_op jit(solution)/shard_map/ppermute | solution.py:883
  72.4 1.9 collective-permute-start.15
  74.4 2.2 %merge_tiles.1 = (f32[8,8192]{1,0:T(8,128)}, f32[8,8192]{1,0:T(8,128)}, f32[8,8192]{1,0:T(8,128)}, f32[8,8192]{1,0:T(8,128)}, f32[8,8192]{1,0:T(8,128)}, /*index...) custom-call(f32[8,8,8192]{2,1,0:T(8,128)} %get-tuple-element.68.own, ...), custom_call_target="tpu_custom_call" | custom-call | tf_op jit(solution)/shard_map/merge_tiles/pallas_call | solution.py:276
  76.6 4.9 %collective-permute-done.15.north = f32[48,384]{1,0:T(8,128)} collective-permute-done((f32[48,384]{1,0:T(8,128)}, f32[48,384]{1,0:T(8,128)}, u32[]{:S(2)}, u32[]{:S(2)}) %collective-permute-start.15) | collective-permute-done | bytes 73760 | tf_op jit(solution)/shard_map/ppermute | solution.py:883
  81.5 26.5 %adjoint_window.1 = (f32[2,270,4,270]{3,2,1,0:T(4,128)}, f32[8,3,304,128]{3,2,1,0:T(8,128)}, f32[64,16,128]{2,1,0:T(8,128)}, f32[64,16,128]{2,1,0:T(8,128)}) custom-call(s32[3,3]{1,0:T(4,128)} %wet.1, s32[3,3]{1,0:T(4,128)} %labels.1, s32[1]{0:T(128)} %get-tuple-element.79.clash, f32[270,270]{1,0:T(8,128)} %zd.1, f32[270,270]{1,0:T(8,128)} %zf.1, ...), custom_call_target="tpu_custom_call" | custom-call | tf_op jit(solution)/shard_map/adjoint_window/pallas_call | solution.py:652
  108.0 7.5 %collective-permute-start.20 = (f32[64,16,128]{2,1,0:T(8,128)}, f32[64,16,128]{2,1,0:T(8,128)S(1)}, u32[]{:S(2)}, u32[]{:S(2)}) collective-permute-start(f32[64,16,128]{2,1,0:T(8,128)} %get-tuple-element.94), channel_id=1, source_target_pairs={{0,1},{1,0},{2,3},{3,2},{4,5},{5,4},{6,7},{7,6},{8,9},{9,8},{10,11... | collective-permute-start | bytes 1572872 | tf_op jit(solution)/shard_map/ppermute | solution.py:887
  115.6 1.7 collective-permute-done.20
  118.5 4.5 %collective-permute-start.10 = (f32[8,8192]{1,0:T(8,128)S(1)}, f32[8,8192]{1,0:T(8,128)}, u32[]{:S(2)}, u32[]{:S(2)}) collective-permute-start(f32[8,8192]{1,0:T(8,128)S(1)} %copy-done.13), channel_id=1, source_target_pairs={{0,12},{1,13},{2,14},{3,15},{4,8},{5,9},{6,10},{7,11},{8,4},{9,5},... | collective-permute-start | bytes 786440 | tf_op jit(solution)/shard_map/ppermute | solution.py:887
  123.1 4.5 %collective-permute-done.21 = f32[32,16,128]{2,1,0:T(8,128)S(1)} collective-permute-done((f32[32,16,128]{2,1,0:T(8,128)S(1)}, f32[32,16,128]{2,1,0:T(8,128)S(1)}, u32[]{:S(2)}, u32[]{:S(2)}) %collective-permute-start.21) | collective-permute-done | bytes 262176 | tf_op jit(solution)/shard_map/ppermute | solution.py:887
  128.9 3.5 %collective-permute-start.6 = (f32[8,8192]{1,0:T(8,128)S(1)}, f32[8,8192]{1,0:T(8,128)}, u32[]{:S(2)}, u32[]{:S(2)}) collective-permute-start(f32[8,8192]{1,0:T(8,128)S(1)} %copy-done.10), channel_id=1, source_target_pairs={{0,4},{1,5},{2,6},{3,7},{4,0},{5,1},{6,2},{7,3},{8,12},{9,13},{10,... | collective-permute-start | bytes 786440 | tf_op jit(solution)/shard_map/ppermute | solution.py:887
  132.7 2.9 %collective-permute-done.11.refs_7_ = f32[8,8192]{1,0:T(8,128)} collective-permute-done((f32[8,8192]{1,0:T(8,128)S(1)}, f32[8,8192]{1,0:T(8,128)}, u32[]{:S(2)}, u32[]{:S(2)}) %collective-permute-start.11) | collective-permute-done | bytes 262176 | tf_op jit(solution)/shard_map/ppermute | solution.py:887
  137.5 6.0 %all-to-all-start.2 = ((f32[16,16,128]{2,1,0:T(8,128)}), f32[16,16,128]{2,1,0:T(8,128)}, u32[]{:S(2)}, u32[]{:S(2)}) async-start(f32[16,16,128]{2,1,0:T(8,128)} %slice_add_fusion.1), calls=%async_computation.2 | async-start | bytes 262144 | tf_op jit(solution)/shard_map/all_to_all | solution.py:920
  143.6 2.0 %collective-permute-done.7.refs_3_ = f32[8,8192]{1,0:T(8,128)} collective-permute-done((f32[8,8192]{1,0:T(8,128)S(1)}, f32[8,8192]{1,0:T(8,128)}, u32[]{:S(2)}, u32[]{:S(2)}) %collective-permute-start.7) | collective-permute-done | bytes 262176 | tf_op jit(solution)/shard_map/ppermute | solution.py:887
  145.6 3.4 %collective-permute-done.8.refs_4_ = f32[8,8192]{1,0:T(8,128)} collective-permute-done((f32[8,8192]{1,0:T(8,128)S(1)}, f32[8,8192]{1,0:T(8,128)}, u32[]{:S(2)}, u32[]{:S(2)}) %collective-permute-start.8) | collective-permute-done | bytes 262176 | tf_op jit(solution)/shard_map/ppermute | solution.py:887
  149.0 6.8 %unpack_tiles.3 = (f32[8,3,304,128]{3,2,1,0:T(8,128)}, f32[24,272]{1,0:T(8,128)}, f32[24,272]{1,0:T(8,128)}, f32[24,272]{1,0:T(8,128)}, f32[24,272]{1,0:T(8,128)}) custom-call(f32[16,8,8192]{2,1,0:T(8,128)} %all-to-all-done.1.first, f32[8,8192]{1,0:T(8,128)} %get-tuple-element.70.refs_0_, f32[8,8192]{1,0:T(8,128)} %collective-permute-done.5.refs_1_, ...), custom_call_target="tpu_custom_call" | custom-call | tf_op jit(solution)/shard_map/unpack_tiles/pallas_call | solution.py:751
  155.8 4.0 %collective-permute-start.16 = (f32[24,272]{1,0:T(8,128)}, f32[24,272]{1,0:T(8,128)S(1)}, u32[]{:S(2)}, u32[]{:S(2)}) collective-permute-start(f32[24,272]{1,0:T(8,128)} %get-tuple-element.87), channel_id=1, source_target_pairs={{0,1},{1,2},{2,3},{3,4},{4,5},{5,6},{6,7},{7,8},{8,9},{9,10},{10,1... | collective-permute-start | bytes 78344 | tf_op jit(solution)/shard_map/ppermute | solution.py:883
  161.2 4.3 %collective-permute-done.17.east = f32[24,272]{1,0:T(8,128)S(1)} collective-permute-done((f32[24,272]{1,0:T(8,128)}, f32[24,272]{1,0:T(8,128)S(1)}, u32[]{:S(2)}, u32[]{:S(2)}) %collective-permute-start.17) | collective-permute-done | bytes 26144 | tf_op jit(solution)/shard_map/ppermute | solution.py:883
  168.9 2.5 %collective-permute-start.19 = (f32[24,384]{1,0:T(8,128)}, f32[24,384]{1,0:T(8,128)}, u32[]{:S(2)}, u32[]{:S(2)}) collective-permute-start(f32[24,384]{1,0:T(8,128)} %get-tuple-element.92), channel_id=1, source_target_pairs={{16,32},{48,64},{80,96},{32,16},{64,48},{96,80},{17,33},{49,65},{8... | collective-permute-start | bytes 110600 | tf_op jit(solution)/shard_map/ppermute | solution.py:931
  173.1 4.4 %collective-permute-done.19.two = f32[24,384]{1,0:T(8,128)} collective-permute-done((f32[24,384]{1,0:T(8,128)}, f32[24,384]{1,0:T(8,128)}, u32[]{:S(2)}, u32[]{:S(2)}) %collective-permute-start.19) | collective-permute-done | bytes 36896 | tf_op jit(solution)/shard_map/ppermute | solution.py:931
  177.6 14.6 %forward_window.3 = f32[2,270,4,270]{3,2,1,0:T(4,128)} custom-call(f32[8,3,304,128]{3,2,1,0:T(8,128)} %get-tuple-element.78.state, f32[8,3,304,128]{3,2,1,0:T(8,128)} %get-tuple-element.118.factors, f32[24,272]{1,0:T(8,128)} %copy-done.4, f32[24,272]{1,0:T(8,128)} %copy-done.5, f32[24,384]{1,0:T(8,128)} %collective-permute-done.18.one, ...), custom_call_target="tpu_custom_call" | custom-call | tf_op jit(solution)/shard_map/forward_window/pallas_call | solution.py:835
  (60 shorter events, 15.9 us)
Async XLA Ops:
  9.9 127.6 %all-to-all-start.1 = ((f32[16,8,8192]{2,1,0:T(8,128)}), f32[16,8,8192]{2,1,0:T(8,128)}, u32[]{:S(2)}, u32[]{:S(2)}) async-start(f32[16,8,8192]{2,1,0:T(8,128)} %get-tuple-element.67), calls=%async_computation.1 | async-start | bytes 8388608 | tf_op jit(solution)/shard_map/all_to_all | solution.py:903
  16.5 57.8 %collective-permute-start.4 = (f32[8,8,8192]{2,1,0:T(8,128)S(1)}, f32[8,8,8192]{2,1,0:T(8,128)}, u32[]{:S(2)}, u32[]{:S(2)}) collective-permute-start(f32[8,8,8192]{2,1,0:T(8,128)S(1)} %copy-done.6), channel_id=1, source_target_pairs={{0,1},{1,0},{2,3},{3,2},{4,5},{5,4},{6,7},{7,6},{8,9},{9,8},{10,11... | collective-permute-start | bytes 6291464 | tf_op jit(solution)/shard_map/ppermute | solution.py:887
  17.0 46.0 %collective-permute-start.12 = (f32[48,272]{1,0:T(8,128)S(1)}, f32[48,272]{1,0:T(8,128)S(1)}, u32[]{:S(2)}, u32[]{:S(2)}) collective-permute-start(f32[48,272]{1,0:T(8,128)S(1)} %copy-done.15), channel_id=1, source_target_pairs={{0,1},{1,2},{2,3},{3,4},{4,5},{5,6},{6,7},{7,8},{8,9},{9,10},{10,1... | collective-permute-start | bytes 156680 | tf_op jit(solution)/shard_map/ppermute | solution.py:883
  18.2 46.9 %collective-permute-start.13 = (f32[48,272]{1,0:T(8,128)S(1)}, f32[48,272]{1,0:T(8,128)S(1)}, u32[]{:S(2)}, u32[]{:S(2)}) collective-permute-start(f32[48,272]{1,0:T(8,128)S(1)} %copy-done.14), channel_id=1, source_target_pairs={{1,0},{2,1},{3,2},{4,3},{5,4},{6,5},{7,6},{8,7},{9,8},{10,9},{11,1... | collective-permute-start | bytes 156680 | tf_op jit(solution)/shard_map/ppermute | solution.py:883
  67.4 9.1 %collective-permute-start.14 = (f32[48,384]{1,0:T(8,128)}, f32[48,384]{1,0:T(8,128)}, u32[]{:S(2)}, u32[]{:S(2)}) collective-permute-start(f32[48,384]{1,0:T(8,128)} %get-tuple-element.84), channel_id=1, source_target_pairs={{0,16},{16,32},{32,48},{48,64},{64,80},{80,96},{96,112},{1,17},{17... | collective-permute-start | bytes 221192 | tf_op jit(solution)/shard_map/ppermute | solution.py:883
  72.4 9.0 %collective-permute-start.15 = (f32[48,384]{1,0:T(8,128)}, f32[48,384]{1,0:T(8,128)}, u32[]{:S(2)}, u32[]{:S(2)}) collective-permute-start(f32[48,384]{1,0:T(8,128)} %get-tuple-element.85), channel_id=1, source_target_pairs={{16,0},{32,16},{48,32},{64,48},{80,64},{96,80},{112,96},{17,1},{33... | collective-permute-start | bytes 221192 | tf_op jit(solution)/shard_map/ppermute | solution.py:883
  81.5 50.9 %copy-start.9 = (f32[8,8192]{1,0:T(8,128)S(1)}, f32[8,8192]{1,0:T(8,128)}, u32[]{:S(2)}) copy-start(f32[8,8192]{1,0:T(8,128)} %get-tuple-element.73) | copy-start | bytes 786436
  81.5 54.1 %copy-start.8 = (f32[8,8192]{1,0:T(8,128)S(1)}, f32[8,8192]{1,0:T(8,128)}, u32[]{:S(2)}) copy-start(f32[8,8192]{1,0:T(8,128)} %get-tuple-element.74) | copy-start | bytes 786436
  81.5 55.3 %copy-start.7 = (f32[8,8192]{1,0:T(8,128)S(1)}, f32[8,8192]{1,0:T(8,128)}, u32[]{:S(2)}) copy-start(f32[8,8192]{1,0:T(8,128)} %get-tuple-element.75) | copy-start | bytes 786436
  108.0 9.3 %collective-permute-start.20 = (f32[64,16,128]{2,1,0:T(8,128)}, f32[64,16,128]{2,1,0:T(8,128)S(1)}, u32[]{:S(2)}, u32[]{:S(2)}) collective-permute-start(f32[64,16,128]{2,1,0:T(8,128)} %get-tuple-element.94), channel_id=1, source_target_pairs={{0,1},{1,0},{2,3},{3,2},{4,5},{5,4},{6,7},{7,6},{8,9},{9,8},{10,11... | collective-permute-start | bytes 1572872 | tf_op jit(solution)/shard_map/ppermute | solution.py:887
  118.4 9.2 %collective-permute-start.21 = (f32[32,16,128]{2,1,0:T(8,128)S(1)}, f32[32,16,128]{2,1,0:T(8,128)S(1)}, u32[]{:S(2)}, u32[]{:S(2)}) collective-permute-start(f32[32,16,128]{2,1,0:T(8,128)S(1)} %slice.17), channel_id=1, source_target_pairs={{0,32},{16,48},{32,0},{48,16},{64,96},{80,112},{96,64},{112,80},{1... | collective-permute-start | bytes 786440 | tf_op jit(solution)/shard_map/ppermute | solution.py:887
  118.5 13.8 %collective-permute-start.10 = (f32[8,8192]{1,0:T(8,128)S(1)}, f32[8,8192]{1,0:T(8,128)}, u32[]{:S(2)}, u32[]{:S(2)}) collective-permute-start(f32[8,8192]{1,0:T(8,128)S(1)} %copy-done.13), channel_id=1, source_target_pairs={{0,12},{1,13},{2,14},{3,15},{4,8},{5,9},{6,10},{7,11},{8,4},{9,5},... | collective-permute-start | bytes 786440 | tf_op jit(solution)/shard_map/ppermute | solution.py:887
  123.0 12.5 %collective-permute-start.11 = (f32[8,8192]{1,0:T(8,128)S(1)}, f32[8,8192]{1,0:T(8,128)}, u32[]{:S(2)}, u32[]{:S(2)}) collective-permute-start(f32[8,8192]{1,0:T(8,128)S(1)} %copy-done.12), channel_id=1, source_target_pairs={{0,14},{1,15},{2,12},{3,13},{4,10},{5,11},{6,8},{7,9},{8,6},{9,7},... | collective-permute-start | bytes 786440 | tf_op jit(solution)/shard_map/ppermute | solution.py:887
  127.7 9.2 %collective-permute-start.22 = (f32[16,16,128]{2,1,0:T(8,128)S(1)}, f32[16,16,128]{2,1,0:T(8,128)S(1)}, u32[]{:S(2)}, u32[]{:S(2)}) collective-permute-start(f32[16,16,128]{2,1,0:T(8,128)S(1)} %slice.19), channel_id=1, source_target_pairs={{0,16},{16,0},{32,48},{48,32},{64,80},{80,64},{96,112},{112,96},{1... | collective-permute-start | bytes 393224 | tf_op jit(solution)/shard_map/ppermute | solution.py:887
  127.8 15.8 %collective-permute-start.5 = (f32[8,8192]{1,0:T(8,128)S(1)}, f32[8,8192]{1,0:T(8,128)}, u32[]{:S(2)}, u32[]{:S(2)}) collective-permute-start(f32[8,8192]{1,0:T(8,128)S(1)} %copy-done.11), channel_id=1, source_target_pairs={{0,2},{1,3},{2,0},{3,1},{4,6},{5,7},{6,4},{7,5},{8,10},{9,11},{10,... | collective-permute-start | bytes 786440 | tf_op jit(solution)/shard_map/ppermute | solution.py:887
  128.9 14.6 %collective-permute-start.6 = (f32[8,8192]{1,0:T(8,128)S(1)}, f32[8,8192]{1,0:T(8,128)}, u32[]{:S(2)}, u32[]{:S(2)}) collective-permute-start(f32[8,8192]{1,0:T(8,128)S(1)} %copy-done.10), channel_id=1, source_target_pairs={{0,4},{1,5},{2,6},{3,7},{4,0},{5,1},{6,2},{7,3},{8,12},{9,13},{10,... | collective-permute-start | bytes 786440 | tf_op jit(solution)/shard_map/ppermute | solution.py:887
  132.4 13.2 %collective-permute-start.7 = (f32[8,8192]{1,0:T(8,128)S(1)}, f32[8,8192]{1,0:T(8,128)}, u32[]{:S(2)}, u32[]{:S(2)}) collective-permute-start(f32[8,8192]{1,0:T(8,128)S(1)} %copy-done.9), channel_id=1, source_target_pairs={{0,6},{1,7},{2,4},{3,5},{4,2},{5,3},{6,0},{7,1},{8,14},{9,15},{10,... | collective-permute-start | bytes 786440 | tf_op jit(solution)/shard_map/ppermute | solution.py:887
  135.5 13.4 %collective-permute-start.8 = (f32[8,8192]{1,0:T(8,128)S(1)}, f32[8,8192]{1,0:T(8,128)}, u32[]{:S(2)}, u32[]{:S(2)}) collective-permute-start(f32[8,8192]{1,0:T(8,128)S(1)} %copy-done.8), channel_id=1, source_target_pairs={{0,8},{1,9},{2,10},{3,11},{4,12},{5,13},{6,14},{7,15},{8,0},{9,1},... | collective-permute-start | bytes 786440 | tf_op jit(solution)/shard_map/ppermute | solution.py:887
  136.8 12.2 %collective-permute-start.9 = (f32[8,8192]{1,0:T(8,128)S(1)}, f32[8,8192]{1,0:T(8,128)}, u32[]{:S(2)}, u32[]{:S(2)}) collective-permute-start(f32[8,8192]{1,0:T(8,128)S(1)} %copy-done.7), channel_id=1, source_target_pairs={{0,10},{1,11},{2,8},{3,9},{4,14},{5,15},{6,12},{7,13},{8,2},{9,3},... | collective-permute-start | bytes 786440 | tf_op jit(solution)/shard_map/ppermute | solution.py:887
  137.5 33.9 %all-to-all-start.2 = ((f32[16,16,128]{2,1,0:T(8,128)}), f32[16,16,128]{2,1,0:T(8,128)}, u32[]{:S(2)}, u32[]{:S(2)}) async-start(f32[16,16,128]{2,1,0:T(8,128)} %slice_add_fusion.1), calls=%async_computation.2 | async-start | bytes 262144 | tf_op jit(solution)/shard_map/all_to_all | solution.py:920
  155.8 5.4 %collective-permute-start.16 = (f32[24,272]{1,0:T(8,128)}, f32[24,272]{1,0:T(8,128)S(1)}, u32[]{:S(2)}, u32[]{:S(2)}) collective-permute-start(f32[24,272]{1,0:T(8,128)} %get-tuple-element.87), channel_id=1, source_target_pairs={{0,1},{1,2},{2,3},{3,4},{4,5},{5,6},{6,7},{7,8},{8,9},{9,10},{10,1... | collective-permute-start | bytes 78344 | tf_op jit(solution)/shard_map/ppermute | solution.py:883
  159.9 5.7 %collective-permute-start.17 = (f32[24,272]{1,0:T(8,128)}, f32[24,272]{1,0:T(8,128)S(1)}, u32[]{:S(2)}, u32[]{:S(2)}) collective-permute-start(f32[24,272]{1,0:T(8,128)} %get-tuple-element.88), channel_id=1, source_target_pairs={{1,0},{2,1},{3,2},{4,3},{5,4},{6,5},{7,6},{8,7},{9,8},{10,9},{11,1... | collective-permute-start | bytes 78344 | tf_op jit(solution)/shard_map/ppermute | solution.py:883
  167.7 5.4 %collective-permute-start.18 = (f32[24,384]{1,0:T(8,128)}, f32[24,384]{1,0:T(8,128)}, u32[]{:S(2)}, u32[]{:S(2)}) collective-permute-start(f32[24,384]{1,0:T(8,128)} %get-tuple-element.91), channel_id=1, source_target_pairs={{0,16},{32,48},{64,80},{96,112},{16,0},{48,32},{80,64},{112,96},{1... | collective-permute-start | bytes 110600 | tf_op jit(solution)/shard_map/ppermute | solution.py:931
  168.9 8.6 %collective-permute-start.19 = (f32[24,384]{1,0:T(8,128)}, f32[24,384]{1,0:T(8,128)}, u32[]{:S(2)}, u32[]{:S(2)}) collective-permute-start(f32[24,384]{1,0:T(8,128)} %get-tuple-element.92), channel_id=1, source_target_pairs={{16,32},{48,64},{80,96},{32,16},{64,48},{96,80},{17,33},{49,65},{8... | collective-permute-start | bytes 110600 | tf_op jit(solution)/shard_map/ppermute | solution.py:931
  (11 other events, 202.1 us)

commit v9 on v8

--- a/solution.py
+++ b/solution.py
@@ -398,7 +398,10 @@
         out[:, N + HALO : N + 2 * HALO] = east[:, first : first + HALO]
 
 
-def paired_kernel(south, north, west, east, one, two):
+def paired_kernel(south, north, near, far, one, two):
+    even = lax.axis_index("lon") & 1 == 0
+    west = jnp.where(even, far[...], near[...])
+    east = jnp.where(even, near[...], far[...])
     even = lax.axis_index("lat") & 1 == 0
 
     @pl.when(even)
@@ -735,8 +738,11 @@
         for j in range(3):
             state[:, j, pl.ds(aligned(TOP + 8 * g), 8), :] = block[:, :, 128 * j : 128 * j + 128]
 
-    west[...] = strip_columns(lambda f: state[f, 0, TOP : TOP + N + 2, :], 8, 0)
-    east[...] = strip_columns(lambda f: state[f, 2, TOP : TOP + N + 2, :], 8, N - HALO - 256)
+    even = lax.axis_index("lon") & 1 == 0
+    low = strip_columns(lambda f: state[f, 0, TOP : TOP + N + 2, :], 8, 0)
+    high = strip_columns(lambda f: state[f, 2, TOP : TOP + N + 2, :], 8, N - HALO - 256)
+    west[...] = jnp.where(even, high, low)
+    east[...] = jnp.where(even, low, high)
     for f in range(8):
         for j, width in BLOCKS:
             lanes = slice(128 * j, 128 * j + width)
@@ -767,7 +773,12 @@
     )(first, *seconds)
 
 
-def forward_kernel(state, factors, west, east, one, two, out, first, second, coef, final, south, north, sem, out_sem):
+def forward_kernel(
+    state, factors, near, far, one, two, out, first, second, coef, final, south, north, west, east, sem, out_sem
+):
+    even = lax.axis_index("lon") & 1 == 0
+    west[...] = jnp.where(even, far[...], near[...])
+    east[...] = jnp.where(even, near[...], far[...])
     even = lax.axis_index("lat") & 1 == 0
     south[...] = jnp.where(even, two[...], one[...])
     north[...] = jnp.where(even, one[...], two[...])
@@ -844,6 +855,8 @@
             pltpu.VMEM(shape, F32),
             pltpu.VMEM((24, LANES), F32),
             pltpu.VMEM((24, LANES), F32),
+            pltpu.VMEM((24, N + 2), F32),
+            pltpu.VMEM((24, N + 2), F32),
             pltpu.SemaphoreType.DMA((2,)),
             pltpu.SemaphoreType.DMA((3,)),
         ],
@@ -905,9 +918,7 @@
     south, north = neighbours(*with_corners(bottom, top, west, east), "lat", False)
     *seconds, clash = merge_tiles(own, cross)
     seconds = [seconds[0]] + [xor_permute(x, "lon", 2 * c) for c, x in enumerate(seconds) if c > 0]
-    initial, coef, keep, give = adjoint_window(
-        wet_tiles, control_map, clash, *fields, west, east, south, north, owners
-    )
+    initial, coef, keep, give = adjoint_window(wet_tiles, control_map, clash, *fields, west, east, south, north, owners)
     keep = keep + xor_permute(give, "lon", 1)
     for bit in (2, 1):
         half = keep.shape[0] // 2
@@ -917,13 +928,15 @@
         for y in range(4)
         for c in range(2)
     ]
-    gathered = lax.all_to_all(
-        keep, ("lat", "lon"), split_axis=0, concat_axis=0, axis_index_groups=groups, tiled=True
-    )
+    gathered = lax.all_to_all(keep, ("lat", "lon"), split_axis=0, concat_axis=0, axis_index_groups=groups, tiled=True)
     control, clashes = control_rows(gathered)
 
     def halos(low, high, bottom, top):
-        west, east = neighbours(low, high, "lon", True)
+        owners = lax.axis_size("lon")
+        pairs = [[(i, (i + 1) % owners) for i in range(first, owners, 2)] for first in range(2)]
+        west, east = [
+            lax.ppermute(x, "lon", pair + [(b, a) for a, b in pair]) for x, pair in zip((low, high), pairs)
+        ]
         one, two = with_corners(bottom, top, west, east, paired_kernel)
         bands = lax.axis_size("lat")
         pairs = [[(i, i + 1) for i in range(first, bands - 1, 2)] for first in range(2)]

time: 194 us -> 194 us (level)
  the two profiles are of different devices: /device:TPU:31 before, /device:TPU:24 now
where the time goes in v9:
time: 194 us; the launch traced here: 193 us
  waiting for transfers between devices  70.1 us (36%)
  Pallas kernels  64.3 us (33%)
  starting transfers between devices  53.7 us (28%)
    ppermute x4, waiting for transfers between devices, neighbours(): return (lax.ppermute(high, axis, up), lax.ppermute(low, axis, down))  52.7 us
    pallas_call x1, Pallas kernels, adjoint_window(): pl.pallas_call(adjoint_kernel, out_shape=(jax.ShapeDtypeStruct((2, N, LEV...  26.5 us
    ppermute x11, starting transfers between devices, xor_permute(): lax.ppermute(x, axis, [(i, i ^ bits) for i in range(lax.axis_size(axis))])  25.2 us
    pallas_call x1, Pallas kernels, forward_window(): pl.pallas_call(forward_kernel, out_shape=jax.ShapeDtypeStruct(shape, F32)...  14.6 us
    ppermute x4, starting transfers between devices, neighbours(): return (lax.ppermute(high, axis, up), lax.ppermute(low, axis, down))  11 us
    pallas_call x1, Pallas kernels, strips_and_tiles(): pl.pallas_call(head_kernel, out_shape=(strip,) * 4 + tuple((jax.ShapeDtyp...  9.13 us
    ppermute x11, waiting for transfers between devices, xor_permute(): lax.ppermute(x, axis, [(i, i ^ bits) for i in range(lax.axis_size(axis))])  8.83 us
    pallas_call x1, Pallas kernels, unpack_tiles(): pl.pallas_call(functools.partial(unpack_kernel, extra), out_shape=(jax.Sh...  6.92 us
  transfers between devices with their start and end apart: 21, of which 8 were waited for; matrix products, arithmetic and copies ran while one was open for 1% of the time, Pallas kernels for 21%

profile of v9, /device:TPU:24, one launch (start us, length us, event | category | flops | bytes accessed | tf_op | source)
XLA Modules:
  0.0 192.9 jit_solution(13556015797507697335)
XLA Ops:
  0.6 9.1 %strips_and_tiles.1 = (f32[48,272]{1,0:T(8,128)}, f32[48,272]{1,0:T(8,128)}, f32[48,272]{1,0:T(8,128)}, f32[48,272]{1,0:T(8,128)}, f32[16,8,8192]{2,1,0:T(8,128)...) custom-call(s32[27]{0:T(128)} %ids.1, f32[27,8,8100]{2,1,0:T(8,128)} %stored.1, s32[3,3]{1,0:T(4,128)} %wet.1, ...), custom_call_target="tpu_custom_call" | custom-call | tf_op jit(solution)/shard_map/strips_and_tiles/pallas_call | solution.py:370
  9.8 6.1 %all-to-all-start.1 = ((f32[16,8,8192]{2,1,0:T(8,128)}), f32[16,8,8192]{2,1,0:T(8,128)}, u32[]{:S(2)}, u32[]{:S(2)}) async-start(f32[16,8,8192]{2,1,0:T(8,128)} %get-tuple-element.67), calls=%async_computation.1 | async-start | bytes 8388608 | tf_op jit(solution)/shard_map/all_to_all | solution.py:916
  16.5 3.7 %collective-permute-start.13 = (f32[48,272]{1,0:T(8,128)S(1)}, f32[48,272]{1,0:T(8,128)S(1)}, u32[]{:S(2)}, u32[]{:S(2)}) collective-permute-start(f32[48,272]{1,0:T(8,128)S(1)} %copy-done.14), channel_id=1, source_target_pairs={{1,0},{2,1},{3,2},{4,3},{5,4},{6,5},{7,6},{8,7},{9,8},{10,9},{11,1... | collective-permute-start | bytes 156680 | tf_op jit(solution)/shard_map/ppermute | solution.py:896
  20.2 46.6 %collective-permute-done.12.west = f32[48,272]{1,0:T(8,128)S(1)} collective-permute-done((f32[48,272]{1,0:T(8,128)S(1)}, f32[48,272]{1,0:T(8,128)S(1)}, u32[]{:S(2)}, u32[]{:S(2)}) %collective-permute-start.12) | collective-permute-done | bytes 52256 | tf_op jit(solution)/shard_map/ppermute | solution.py:896
  69.3 5.3 %collective-permute-start.14 = (f32[48,384]{1,0:T(8,128)}, f32[48,384]{1,0:T(8,128)}, u32[]{:S(2)}, u32[]{:S(2)}) collective-permute-start(f32[48,384]{1,0:T(8,128)} %get-tuple-element.84), channel_id=1, source_target_pairs={{0,16},{16,32},{32,48},{48,64},{64,80},{80,96},{96,112},{1,17},{17... | collective-permute-start | bytes 221192 | tf_op jit(solution)/shard_map/ppermute | solution.py:896
  74.5 1.9 collective-permute-start.15
  76.5 2.2 %merge_tiles.1 = (f32[8,8192]{1,0:T(8,128)}, f32[8,8192]{1,0:T(8,128)}, f32[8,8192]{1,0:T(8,128)}, f32[8,8192]{1,0:T(8,128)}, f32[8,8192]{1,0:T(8,128)}, /*index...) custom-call(f32[8,8,8192]{2,1,0:T(8,128)} %get-tuple-element.68.own, ...), custom_call_target="tpu_custom_call" | custom-call | tf_op jit(solution)/shard_map/merge_tiles/pallas_call | solution.py:276
  78.6 6.0 %collective-permute-done.15.north = f32[48,384]{1,0:T(8,128)} collective-permute-done((f32[48,384]{1,0:T(8,128)}, f32[48,384]{1,0:T(8,128)}, u32[]{:S(2)}, u32[]{:S(2)}) %collective-permute-start.15) | collective-permute-done | bytes 73760 | tf_op jit(solution)/shard_map/ppermute | solution.py:896
  84.7 26.5 %adjoint_window.1 = (f32[2,270,4,270]{3,2,1,0:T(4,128)}, f32[8,3,304,128]{3,2,1,0:T(8,128)}, f32[64,16,128]{2,1,0:T(8,128)}, f32[64,16,128]{2,1,0:T(8,128)}) custom-call(s32[3,3]{1,0:T(4,128)} %wet.1, s32[3,3]{1,0:T(4,128)} %labels.1, s32[1]{0:T(128)} %get-tuple-element.79.clash, f32[270,270]{1,0:T(8,128)} %zd.1, f32[270,270]{1,0:T(8,128)} %zf.1, ...), custom_call_target="tpu_custom_call" | custom-call | tf_op jit(solution)/shard_map/adjoint_window/pallas_call | solution.py:655
  111.3 4.7 %collective-permute-start.20 = (f32[64,16,128]{2,1,0:T(8,128)}, f32[64,16,128]{2,1,0:T(8,128)S(1)}, u32[]{:S(2)}, u32[]{:S(2)}) collective-permute-start(f32[64,16,128]{2,1,0:T(8,128)} %get-tuple-element.94), channel_id=1, source_target_pairs={{0,1},{1,0},{2,3},{3,2},{4,5},{5,4},{6,7},{7,6},{8,9},{9,8},{10,11... | collective-permute-start | bytes 1572872 | tf_op jit(solution)/shard_map/ppermute | solution.py:900
  119.0 3.4 %collective-permute-start.10 = (f32[8,8192]{1,0:T(8,128)S(1)}, f32[8,8192]{1,0:T(8,128)}, u32[]{:S(2)}, u32[]{:S(2)}) collective-permute-start(f32[8,8192]{1,0:T(8,128)S(1)} %copy-done.13), channel_id=1, source_target_pairs={{0,12},{1,13},{2,14},{3,15},{4,8},{5,9},{6,10},{7,11},{8,4},{9,5},... | collective-permute-start | bytes 786440 | tf_op jit(solution)/shard_map/ppermute | solution.py:900
  122.4 4.4 %collective-permute-start.11 = (f32[8,8192]{1,0:T(8,128)S(1)}, f32[8,8192]{1,0:T(8,128)}, u32[]{:S(2)}, u32[]{:S(2)}) collective-permute-start(f32[8,8192]{1,0:T(8,128)S(1)} %copy-done.12), channel_id=1, source_target_pairs={{0,14},{1,15},{2,12},{3,13},{4,10},{5,11},{6,8},{7,9},{8,6},{9,7},... | collective-permute-start | bytes 786440 | tf_op jit(solution)/shard_map/ppermute | solution.py:900
  126.8 2.2 %collective-permute-done.21 = f32[32,16,128]{2,1,0:T(8,128)S(1)} collective-permute-done((f32[32,16,128]{2,1,0:T(8,128)S(1)}, f32[32,16,128]{2,1,0:T(8,128)S(1)}, u32[]{:S(2)}, u32[]{:S(2)}) %collective-permute-start.21) | collective-permute-done | bytes 262176 | tf_op jit(solution)/shard_map/ppermute | solution.py:900
  129.2 4.0 %collective-permute-start.5 = (f32[8,8192]{1,0:T(8,128)S(1)}, f32[8,8192]{1,0:T(8,128)}, u32[]{:S(2)}, u32[]{:S(2)}) collective-permute-start(f32[8,8192]{1,0:T(8,128)S(1)} %copy-done.11), channel_id=1, source_target_pairs={{0,2},{1,3},{2,0},{3,1},{4,6},{5,7},{6,4},{7,5},{8,10},{9,11},{10,... | collective-permute-start | bytes 786440 | tf_op jit(solution)/shard_map/ppermute | solution.py:900
  133.2 2.8 %collective-permute-start.7 = (f32[8,8192]{1,0:T(8,128)S(1)}, f32[8,8192]{1,0:T(8,128)}, u32[]{:S(2)}, u32[]{:S(2)}) collective-permute-start(f32[8,8192]{1,0:T(8,128)S(1)} %copy-done.9), channel_id=1, source_target_pairs={{0,6},{1,7},{2,4},{3,5},{4,2},{5,3},{6,0},{7,1},{8,14},{9,15},{10,... | collective-permute-start | bytes 786440 | tf_op jit(solution)/shard_map/ppermute | solution.py:900
  136.5 4.8 %collective-permute-start.9 = (f32[8,8192]{1,0:T(8,128)S(1)}, f32[8,8192]{1,0:T(8,128)}, u32[]{:S(2)}, u32[]{:S(2)}) collective-permute-start(f32[8,8192]{1,0:T(8,128)S(1)} %copy-done.7), channel_id=1, source_target_pairs={{0,10},{1,11},{2,8},{3,9},{4,14},{5,15},{6,12},{7,13},{8,2},{9,3},... | collective-permute-start | bytes 786440 | tf_op jit(solution)/shard_map/ppermute | solution.py:900
  142.0 4.2 %all-to-all-start.2 = ((f32[16,16,128]{2,1,0:T(8,128)}), f32[16,16,128]{2,1,0:T(8,128)}, u32[]{:S(2)}, u32[]{:S(2)}) async-start(f32[16,16,128]{2,1,0:T(8,128)} %slice_add_fusion.1), calls=%async_computation.2 | async-start | bytes 262144 | tf_op jit(solution)/shard_map/all_to_all | solution.py:931
  147.6 3.4 %collective-permute-done.9.refs_5_ = f32[8,8192]{1,0:T(8,128)} collective-permute-done((f32[8,8192]{1,0:T(8,128)S(1)}, f32[8,8192]{1,0:T(8,128)}, u32[]{:S(2)}, u32[]{:S(2)}) %collective-permute-start.9) | collective-permute-done | bytes 262176 | tf_op jit(solution)/shard_map/ppermute | solution.py:900
  151.0 6.9 %unpack_tiles.3 = (f32[8,3,304,128]{3,2,1,0:T(8,128)}, f32[24,272]{1,0:T(8,128)}, f32[24,272]{1,0:T(8,128)}, f32[24,272]{1,0:T(8,128)}, f32[24,272]{1,0:T(8,128)}) custom-call(f32[16,8,8192]{2,1,0:T(8,128)} %all-to-all-done.1.first, f32[8,8192]{1,0:T(8,128)} %get-tuple-element.70.refs_0_, f32[8,8192]{1,0:T(8,128)} %collective-permute-done.5.refs_1_, ...), custom_call_target="tpu_custom_call" | custom-call | tf_op jit(solution)/shard_map/unpack_tiles/pallas_call | solution.py:757
  158.0 3.2 %collective-permute-start.17 = (f32[24,272]{1,0:T(8,128)}, f32[24,272]{1,0:T(8,128)S(1)}, u32[]{:S(2)}, u32[]{:S(2)}) collective-permute-start(f32[24,272]{1,0:T(8,128)} %get-tuple-element.88), channel_id=1, source_target_pairs={{1,2},{3,4},{5,6},{7,8},{9,10},{11,12},{13,14},{15,0},{2,1},{4,3},... | collective-permute-start | bytes 78344 | tf_op jit(solution)/shard_map/ppermute | solution.py:938
  161.2 2.6 %collective-permute-done.17.far = f32[24,272]{1,0:T(8,128)S(1)} collective-permute-done((f32[24,272]{1,0:T(8,128)}, f32[24,272]{1,0:T(8,128)S(1)}, u32[]{:S(2)}, u32[]{:S(2)}) %collective-permute-start.17) | collective-permute-done | bytes 26144 | tf_op jit(solution)/shard_map/ppermute | solution.py:938
  167.7 2.1 %collective-permute-start.19 = (f32[24,384]{1,0:T(8,128)}, f32[24,384]{1,0:T(8,128)}, u32[]{:S(2)}, u32[]{:S(2)}) collective-permute-start(f32[24,384]{1,0:T(8,128)} %get-tuple-element.92), channel_id=1, source_target_pairs={{16,32},{48,64},{80,96},{32,16},{64,48},{96,80},{17,33},{49,65},{8... | collective-permute-start | bytes 110600 | tf_op jit(solution)/shard_map/ppermute | solution.py:944
  171.6 5.9 %collective-permute-done.19.two = f32[24,384]{1,0:T(8,128)} collective-permute-done((f32[24,384]{1,0:T(8,128)}, f32[24,384]{1,0:T(8,128)}, u32[]{:S(2)}, u32[]{:S(2)}) %collective-permute-start.19) | collective-permute-done | bytes 36896 | tf_op jit(solution)/shard_map/ppermute | solution.py:944
  177.5 14.6 %forward_window.3 = f32[2,270,4,270]{3,2,1,0:T(4,128)} custom-call(f32[8,3,304,128]{3,2,1,0:T(8,128)} %get-tuple-element.78.state, f32[8,3,304,128]{3,2,1,0:T(8,128)} %get-tuple-element.118.factors, f32[24,272]{1,0:T(8,128)} %copy-done.4, f32[24,272]{1,0:T(8,128)} %copy-done.5, f32[24,384]{1,0:T(8,128)} %collective-permute-done.18.one, ...), custom_call_target="tpu_custom_call" | custom-call | tf_op jit(solution)/shard_map/forward_window/pallas_call | solution.py:846
  (60 shorter events, 15.1 us)
Async XLA Ops:
  9.8 132.2 %all-to-all-start.1 = ((f32[16,8,8192]{2,1,0:T(8,128)}), f32[16,8,8192]{2,1,0:T(8,128)}, u32[]{:S(2)}, u32[]{:S(2)}) async-start(f32[16,8,8192]{2,1,0:T(8,128)} %get-tuple-element.67), calls=%async_computation.1 | async-start | bytes 8388608 | tf_op jit(solution)/shard_map/all_to_all | solution.py:916
  15.9 60.5 %collective-permute-start.4 = (f32[8,8,8192]{2,1,0:T(8,128)S(1)}, f32[8,8,8192]{2,1,0:T(8,128)}, u32[]{:S(2)}, u32[]{:S(2)}) collective-permute-start(f32[8,8,8192]{2,1,0:T(8,128)S(1)} %copy-done.6), channel_id=1, source_target_pairs={{0,1},{1,0},{2,3},{3,2},{4,5},{5,4},{6,7},{7,6},{8,9},{9,8},{10,11... | collective-permute-start | bytes 6291464 | tf_op jit(solution)/shard_map/ppermute | solution.py:900
  16.4 50.5 %collective-permute-start.12 = (f32[48,272]{1,0:T(8,128)S(1)}, f32[48,272]{1,0:T(8,128)S(1)}, u32[]{:S(2)}, u32[]{:S(2)}) collective-permute-start(f32[48,272]{1,0:T(8,128)S(1)} %copy-done.15), channel_id=1, source_target_pairs={{0,1},{1,2},{2,3},{3,4},{4,5},{5,6},{6,7},{7,8},{8,9},{9,10},{10,1... | collective-permute-start | bytes 156680 | tf_op jit(solution)/shard_map/ppermute | solution.py:896
  16.5 50.3 %collective-permute-start.13 = (f32[48,272]{1,0:T(8,128)S(1)}, f32[48,272]{1,0:T(8,128)S(1)}, u32[]{:S(2)}, u32[]{:S(2)}) collective-permute-start(f32[48,272]{1,0:T(8,128)S(1)} %copy-done.14), channel_id=1, source_target_pairs={{1,0},{2,1},{3,2},{4,3},{5,4},{6,5},{7,6},{8,7},{9,8},{10,9},{11,1... | collective-permute-start | bytes 156680 | tf_op jit(solution)/shard_map/ppermute | solution.py:896
  69.3 9.4 %collective-permute-start.14 = (f32[48,384]{1,0:T(8,128)}, f32[48,384]{1,0:T(8,128)}, u32[]{:S(2)}, u32[]{:S(2)}) collective-permute-start(f32[48,384]{1,0:T(8,128)} %get-tuple-element.84), channel_id=1, source_target_pairs={{0,16},{16,32},{32,48},{48,64},{64,80},{80,96},{96,112},{1,17},{17... | collective-permute-start | bytes 221192 | tf_op jit(solution)/shard_map/ppermute | solution.py:896
  74.5 10.2 %collective-permute-start.15 = (f32[48,384]{1,0:T(8,128)}, f32[48,384]{1,0:T(8,128)}, u32[]{:S(2)}, u32[]{:S(2)}) collective-permute-start(f32[48,384]{1,0:T(8,128)} %get-tuple-element.85), channel_id=1, source_target_pairs={{16,0},{32,16},{48,32},{64,48},{80,64},{96,80},{112,96},{17,1},{33... | collective-permute-start | bytes 221192 | tf_op jit(solution)/shard_map/ppermute | solution.py:896
  84.7 48.5 %copy-start.9 = (f32[8,8192]{1,0:T(8,128)S(1)}, f32[8,8192]{1,0:T(8,128)}, u32[]{:S(2)}) copy-start(f32[8,8192]{1,0:T(8,128)} %get-tuple-element.73) | copy-start | bytes 786436
  84.7 51.3 %copy-start.8 = (f32[8,8192]{1,0:T(8,128)S(1)}, f32[8,8192]{1,0:T(8,128)}, u32[]{:S(2)}) copy-start(f32[8,8192]{1,0:T(8,128)} %get-tuple-element.74) | copy-start | bytes 786436
  84.7 51.7 %copy-start.7 = (f32[8,8192]{1,0:T(8,128)S(1)}, f32[8,8192]{1,0:T(8,128)}, u32[]{:S(2)}) copy-start(f32[8,8192]{1,0:T(8,128)} %get-tuple-element.75) | copy-start | bytes 786436
  111.3 6.4 %collective-permute-start.20 = (f32[64,16,128]{2,1,0:T(8,128)}, f32[64,16,128]{2,1,0:T(8,128)S(1)}, u32[]{:S(2)}, u32[]{:S(2)}) collective-permute-start(f32[64,16,128]{2,1,0:T(8,128)} %get-tuple-element.94), channel_id=1, source_target_pairs={{0,1},{1,0},{2,3},{3,2},{4,5},{5,4},{6,7},{7,6},{8,9},{9,8},{10,11... | collective-permute-start | bytes 1572872 | tf_op jit(solution)/shard_map/ppermute | solution.py:900
  118.9 10.2 %collective-permute-start.21 = (f32[32,16,128]{2,1,0:T(8,128)S(1)}, f32[32,16,128]{2,1,0:T(8,128)S(1)}, u32[]{:S(2)}, u32[]{:S(2)}) collective-permute-start(f32[32,16,128]{2,1,0:T(8,128)S(1)} %slice.17), channel_id=1, source_target_pairs={{0,32},{16,48},{32,0},{48,16},{64,96},{80,112},{96,64},{112,80},{1... | collective-permute-start | bytes 786440 | tf_op jit(solution)/shard_map/ppermute | solution.py:900
  119.0 14.2 %collective-permute-start.10 = (f32[8,8192]{1,0:T(8,128)S(1)}, f32[8,8192]{1,0:T(8,128)}, u32[]{:S(2)}, u32[]{:S(2)}) collective-permute-start(f32[8,8192]{1,0:T(8,128)S(1)} %copy-done.13), channel_id=1, source_target_pairs={{0,12},{1,13},{2,14},{3,15},{4,8},{5,9},{6,10},{7,11},{8,4},{9,5},... | collective-permute-start | bytes 786440 | tf_op jit(solution)/shard_map/ppermute | solution.py:900
  122.4 13.6 %collective-permute-start.11 = (f32[8,8192]{1,0:T(8,128)S(1)}, f32[8,8192]{1,0:T(8,128)}, u32[]{:S(2)}, u32[]{:S(2)}) collective-permute-start(f32[8,8192]{1,0:T(8,128)S(1)} %copy-done.12), channel_id=1, source_target_pairs={{0,14},{1,15},{2,12},{3,13},{4,10},{5,11},{6,8},{7,9},{8,6},{9,7},... | collective-permute-start | bytes 786440 | tf_op jit(solution)/shard_map/ppermute | solution.py:900
  129.1 7.4 %collective-permute-start.22 = (f32[16,16,128]{2,1,0:T(8,128)S(1)}, f32[16,16,128]{2,1,0:T(8,128)S(1)}, u32[]{:S(2)}, u32[]{:S(2)}) collective-permute-start(f32[16,16,128]{2,1,0:T(8,128)S(1)} %slice.19), channel_id=1, source_target_pairs={{0,16},{16,0},{32,48},{48,32},{64,80},{80,64},{96,112},{112,96},{1... | collective-permute-start | bytes 393224 | tf_op jit(solution)/shard_map/ppermute | solution.py:900
  129.2 17.0 %collective-permute-start.5 = (f32[8,8192]{1,0:T(8,128)S(1)}, f32[8,8192]{1,0:T(8,128)}, u32[]{:S(2)}, u32[]{:S(2)}) collective-permute-start(f32[8,8192]{1,0:T(8,128)S(1)} %copy-done.11), channel_id=1, source_target_pairs={{0,2},{1,3},{2,0},{3,1},{4,6},{5,7},{6,4},{7,5},{8,10},{9,11},{10,... | collective-permute-start | bytes 786440 | tf_op jit(solution)/shard_map/ppermute | solution.py:900
  133.2 12.9 %collective-permute-start.6 = (f32[8,8192]{1,0:T(8,128)S(1)}, f32[8,8192]{1,0:T(8,128)}, u32[]{:S(2)}, u32[]{:S(2)}) collective-permute-start(f32[8,8192]{1,0:T(8,128)S(1)} %copy-done.10), channel_id=1, source_target_pairs={{0,4},{1,5},{2,6},{3,7},{4,0},{5,1},{6,2},{7,3},{8,12},{9,13},{10,... | collective-permute-start | bytes 786440 | tf_op jit(solution)/shard_map/ppermute | solution.py:900
  133.2 14.4 %collective-permute-start.7 = (f32[8,8192]{1,0:T(8,128)S(1)}, f32[8,8192]{1,0:T(8,128)}, u32[]{:S(2)}, u32[]{:S(2)}) collective-permute-start(f32[8,8192]{1,0:T(8,128)S(1)} %copy-done.9), channel_id=1, source_target_pairs={{0,6},{1,7},{2,4},{3,5},{4,2},{5,3},{6,0},{7,1},{8,14},{9,15},{10,... | collective-permute-start | bytes 786440 | tf_op jit(solution)/shard_map/ppermute | solution.py:900
  136.0 11.6 %collective-permute-start.8 = (f32[8,8192]{1,0:T(8,128)S(1)}, f32[8,8192]{1,0:T(8,128)}, u32[]{:S(2)}, u32[]{:S(2)}) collective-permute-start(f32[8,8192]{1,0:T(8,128)S(1)} %copy-done.8), channel_id=1, source_target_pairs={{0,8},{1,9},{2,10},{3,11},{4,12},{5,13},{6,14},{7,15},{8,0},{9,1},... | collective-permute-start | bytes 786440 | tf_op jit(solution)/shard_map/ppermute | solution.py:900
  136.5 14.5 %collective-permute-start.9 = (f32[8,8192]{1,0:T(8,128)S(1)}, f32[8,8192]{1,0:T(8,128)}, u32[]{:S(2)}, u32[]{:S(2)}) collective-permute-start(f32[8,8192]{1,0:T(8,128)S(1)} %copy-done.7), channel_id=1, source_target_pairs={{0,10},{1,11},{2,8},{3,9},{4,14},{5,15},{6,12},{7,13},{8,2},{9,3},... | collective-permute-start | bytes 786440 | tf_op jit(solution)/shard_map/ppermute | solution.py:900
  142.0 27.9 %all-to-all-start.2 = ((f32[16,16,128]{2,1,0:T(8,128)}), f32[16,16,128]{2,1,0:T(8,128)}, u32[]{:S(2)}, u32[]{:S(2)}) async-start(f32[16,16,128]{2,1,0:T(8,128)} %slice_add_fusion.1), calls=%async_computation.2 | async-start | bytes 262144 | tf_op jit(solution)/shard_map/all_to_all | solution.py:931
  157.9 3.3 %collective-permute-start.16 = (f32[24,272]{1,0:T(8,128)}, f32[24,272]{1,0:T(8,128)S(1)}, u32[]{:S(2)}, u32[]{:S(2)}) collective-permute-start(f32[24,272]{1,0:T(8,128)} %get-tuple-element.87), channel_id=1, source_target_pairs={{0,1},{2,3},{4,5},{6,7},{8,9},{10,11},{12,13},{14,15},{1,0},{3,2},... | collective-permute-start | bytes 78344 | tf_op jit(solution)/shard_map/ppermute | solution.py:938
  158.0 5.8 %collective-permute-start.17 = (f32[24,272]{1,0:T(8,128)}, f32[24,272]{1,0:T(8,128)S(1)}, u32[]{:S(2)}, u32[]{:S(2)}) collective-permute-start(f32[24,272]{1,0:T(8,128)} %get-tuple-element.88), channel_id=1, source_target_pairs={{1,2},{3,4},{5,6},{7,8},{9,10},{11,12},{13,14},{15,0},{2,1},{4,3},... | collective-permute-start | bytes 78344 | tf_op jit(solution)/shard_map/ppermute | solution.py:938
  165.9 5.6 %collective-permute-start.18 = (f32[24,384]{1,0:T(8,128)}, f32[24,384]{1,0:T(8,128)}, u32[]{:S(2)}, u32[]{:S(2)}) collective-permute-start(f32[24,384]{1,0:T(8,128)} %get-tuple-element.91), channel_id=1, source_target_pairs={{0,16},{32,48},{64,80},{96,112},{16,0},{48,32},{80,64},{112,96},{1... | collective-permute-start | bytes 110600 | tf_op jit(solution)/shard_map/ppermute | solution.py:944
  167.7 9.8 %collective-permute-start.19 = (f32[24,384]{1,0:T(8,128)}, f32[24,384]{1,0:T(8,128)}, u32[]{:S(2)}, u32[]{:S(2)}) collective-permute-start(f32[24,384]{1,0:T(8,128)} %get-tuple-element.92), channel_id=1, source_target_pairs={{16,32},{48,64},{80,96},{32,16},{64,48},{96,80},{17,33},{49,65},{8... | collective-permute-start | bytes 110600 | tf_op jit(solution)/shard_map/ppermute | solution.py:944
  (11 other events, 188.9 us)
